TPU v7x, 128 devices: a whole 4x4x4 slice. The times are simulated.
128 devices in a mesh: tile: 16 (over x, z_lo, core), col: 8 (over y, z_hi).
Axes of the slice: x: 4, y: 4, z: 4 (z_hi: 2, z_lo: 2; z = z_hi * 2 + z_lo), core: 2. Of those that a mesh axis runs over, the one named last changes fastest.
Arguments:
- u_velocity: float32 [8192, 4096], P('tile', 'col'), may hold values from -12 to 12
- v_velocity: float32 [8192, 4096], P('tile', 'col'), may hold values from -12 to 12
- ocean_mask: int32 [64, 32], P('tile', 'col'), may hold values from 0 to 1, as said below
- tile_owner: int32 [64, 32], P('tile', 'col'), may hold values from 0 to 15, as said below
- lower_edge_quarter_turns: int32 [16], replicated, may hold values from 0 to 3
Outputs:
- library: float32 [16, 8, 16, 16, 1024], P('tile', 'col')
- gram: float32 [16, 16], replicated
Inputs may be any that keep to these rules, and one draw needn't show every extreme that they name: `ocean_mask`: in every column of devices (4 x 4 tile blocks), at least one device has only ocean tiles. `tile_owner`: among the ocean tiles of one device at most 1 share an owner; the ocean tiles of one column of devices are spread over its 16 owners so that the owners' counts differ by at most one. Land tiles carry an owner that is not used.
All inputs are finite; a program needn't handle non-finite values.
Results may differ from a plain program's by a relative error of at most 0.00014.
Values sent between devices are 32-bit elements; how exact they have to be, the bound alone decides.
No kernel may reach another device: no remote copies, remote signals or barrier semaphores. Data moves between devices by JAX's collectives and lax.ppermute only.
A program may use at most 192 MiB of HBM per device.

v0:
```python
import jax
import jax.numpy as jnp
from jax import lax
from jax.sharding import PartitionSpec as P

PASSES = 8


KAPPA = 0.2


def with_halo(cells, sides, width):
    for axis, dim in sides:
        count = lax.axis_size(axis)
        head = lax.slice_in_dim(cells, 0, width, axis=dim)
        tail = lax.slice_in_dim(cells, cells.shape[dim] - width, cells.shape[dim], axis=dim)
        cells = jnp.concatenate(
            [
                lax.ppermute(tail, axis, [(i, (i + 1) % count) for i in range(count)]),
                cells,
                lax.ppermute(head, axis, [((i + 1) % count, i) for i in range(count)]),
            ],
            axis=dim,
        )
    return cells


def quarter(first, second, turns):
    cosine = jnp.where(turns == 0, 1.0, jnp.where(turns == 2, -1.0, 0.0)).astype(first.dtype)
    sine = jnp.where(turns == 1, 1.0, jnp.where(turns == 3, -1.0, 0.0)).astype(first.dtype)
    return (cosine * first - sine * second, sine * first + cosine * second)


def turn_rims(padded, width, k_top, k_bottom):
    top_u, top_v = quarter(padded[0, :width], padded[1, :width], k_top)
    low_u, low_v = quarter(padded[0, -width:], padded[1, -width:], k_bottom)
    upper = jnp.stack([top_u, top_v])
    lower = jnp.stack([low_u, low_v])
    return jnp.concatenate([upper, padded[:, width:-width], lower], axis=1)


def relax(padded):
    centre = padded[:, 1:-1, 1:-1]
    beside_all = (
        padded[:, :-2, 1:-1] + padded[:, 2:, 1:-1] + padded[:, 1:-1, :-2] + padded[:, 1:-1, 2:]
    )
    return centre + KAPPA * (beside_all - 4.0 * centre)


def derive(padded):
    first = padded[..., 0, :, :]
    second = padded[..., 1, :, :]
    u_part = first[..., 1:-1, 1:-1]
    v_part = second[..., 1:-1, 1:-1]
    u_dx = (first[..., 1:-1, 2:] - first[..., 1:-1, :-2]) * 0.5
    u_dy = (first[..., 2:, 1:-1] - first[..., :-2, 1:-1]) * 0.5
    v_dx = (second[..., 1:-1, 2:] - second[..., 1:-1, :-2]) * 0.5
    v_dy = (second[..., 2:, 1:-1] - second[..., :-2, 1:-1]) * 0.5
    return jnp.stack([u_part, v_part, v_dx - u_dy, u_dy + v_dx, u_dx - v_dy], axis=-3)


def make_terms(base):
    u_part = base[..., 0, :]
    v_part = base[..., 1, :]
    vort = base[..., 2, :]
    strain = base[..., 3, :]
    stretch = base[..., 4, :]
    listed = [
        u_part,
        v_part,
        vort,
        strain,
        stretch,
        vort * vort,
        vort * strain,
        vort * stretch,
        strain * strain,
        stretch * stretch,
        strain * stretch,
        u_part * vort,
        v_part * vort,
        u_part * strain,
        v_part * stretch,
        u_part * v_part,
    ]
    return jnp.stack(listed, axis=-2)


def to_tiles(field, grid_x, grid_y, side):
    leading = field.shape[:-2]
    shaped = field.reshape(leading + (grid_x, side, grid_y, side))
    shaped = jnp.swapaxes(shaped, -3, -2)
    return shaped.reshape(leading + (grid_x * grid_y, side * side))


def per_device(u_velocity, v_velocity, ocean_mask, tile_owner, lower_edge_quarter_turns):
    rows_tile = lax.axis_size("tile")
    here = lax.axis_index("tile")
    k_top = lower_edge_quarter_turns[here]
    k_bottom = (4 - lower_edge_quarter_turns[(here + 1) % rows_tile]) % 4
    field = jnp.stack([u_velocity, v_velocity])
    for step in range(PASSES):
        padded = with_halo(field, (("tile", 1), ("col", 2)), 1)
        field = relax(turn_rims(padded, 1, k_top, k_bottom))
    fine_rows, fine_cols = u_velocity.shape
    coarse = field.reshape(2, fine_rows // 4, 4, fine_cols // 4, 4).mean(axis=(2, 4))
    coarse_pad = with_halo(coarse, (("tile", 1), ("col", 2)), 1)
    coarse_pad = turn_rims(coarse_pad, 1, k_top, k_bottom)
    grid_x, grid_y = ocean_mask.shape
    side = coarse.shape[1] // grid_x
    starting_tile_set = jnp.swapaxes(to_tiles(derive(coarse_pad), grid_x, grid_y, side), 0, 1)
    live = ocean_mask.reshape(-1) == 1
    owners = tile_owner.reshape(-1)
    tiles = live.shape[0]
    slots = tiles // rows_tile
    local = jnp.arange(tiles, dtype=jnp.int32)
    same = (owners[:, None] == owners[None, :]) & live[None, :] & (local[None, :] < local[:, None])
    slot = jnp.sum(same.astype(jnp.int32), axis=1)
    target = jnp.arange(rows_tile * slots, dtype=jnp.int32)
    chosen_terms = (
        live[None, :]
        & (owners[None, :] == target[:, None] // slots)
        & (slot[None, :] == target[:, None] % slots)
    ).astype(jnp.float32)
    library = make_terms(
        lax.all_to_all(
            jnp.einsum(
                "vh,hsd->vsd", chosen_terms, starting_tile_set, precision=lax.Precision.HIGHEST
            ),
            "tile",
            split_axis=0,
            concat_axis=0,
            tiled=True,
        )
    )
    part = jnp.einsum("pnc,pmc->nm", library, library, precision=lax.Precision.HIGHEST)
    gram = lax.psum(part, ("tile", "col")) / (fine_rows // 4 * (fine_cols // 4))
    return (library[None, None], gram)


def solution(mesh):
    in_specs = (P("tile", "col"), P("tile", "col"), P("tile", "col"), P("tile", "col"), P())
    out_specs = (P("tile", "col", None, None, None), P())
    return jax.shard_map(
        per_device, mesh=mesh, in_specs=in_specs, out_specs=out_specs, check_vma=False
    )
```

profile of v0, /device:TPU:0, one launch (start us, length us, event | category | flops | bytes accessed | tf_op | source)
XLA Modules:
  0.0 373.5 jit_solution(4603771623657914441)
XLA Ops:
  1.7 3.8 %collective-permute-start.1 = (f32[2,1,512]{2,1,0:T(1,128)S(1)}, f32[2,1,512]{2,1,0:T(1,128)S(1)}, u32[]{:S(2)}, u32[]{:S(2)}) collective-permute-start(f32[2,1,512]{2,1,0:T(1,128)S(1)} %get-tuple-element.91), channel_id=1, source_target_pairs={{8,0},{16,8},{24,16},{32,24},{40,32},{48,40},{56,48},{64,56},{72,6... | collective-permute-start | bytes 12296 | tf_op jit(solution)/shard_map/ppermute | solution.py:21
  7.3 4.0 %collective-permute-start.2 = (f32[2,514,1]{1,0,2:T(2,128)S(1)}, f32[2,514,1]{1,0,2:T(2,128)S(1)}, u32[]{:S(2)}, u32[]{:S(2)}) collective-permute-start(f32[2,514,1]{1,0,2:T(2,128)S(1)} %copy.202), channel_id=1, source_target_pairs={{0,1},{1,2},{2,3},{3,4},{4,5},{5,6},{6,7},{7,0},{8,9},{9,10},{10,1... | collective-permute-start | bytes 12344 | tf_op jit(solution)/shard_map/ppermute | solution.py:19
  11.5 2.5 collective-permute-start.3
  20.9 6.4 %fusion.45 = f32[2,512,512]{2,1,0:T(8,128)S(1)} fusion(f32[2,514,1]{2,1,0:T(8,128)} %copy-done.15, f32[2,1,512]{2,1,0:T(1,128)S(1)} %collective-permute-done.1, f32[2,1,512]{2,1,0:T(1,128)S(1)} %collective-permute-done, f32[1,512,512]{2,1,0:T(8,128)S(1)} %bitcast.34, f32[1,512,512]{2,1,0:T(8,128)S(1)} %bitcast.28, f32[2,514,1]{2,1,0:T(8,128)} %copy-done.13, ...), kind=kLoop, calls=%fused_computation.129 | loop fusion | flops 10485760 | bytes 6324288 | tf_op jit(solution)/shard_map/add | solution.py:47
  27.4 3.8 %collective-permute-start.5 = (f32[2,1,512]{2,1,0:T(1,128)S(1)}, f32[2,1,512]{2,1,0:T(1,128)S(1)}, u32[]{:S(2)}, u32[]{:S(2)}) collective-permute-start(f32[2,1,512]{2,1,0:T(1,128)S(1)} %get-tuple-element.89), channel_id=1, source_target_pairs={{8,0},{16,8},{24,16},{32,24},{40,32},{48,40},{56,48},{64,56},{72,6... | collective-permute-start | bytes 12296 | tf_op jit(solution)/shard_map/ppermute | solution.py:21
  36.2 5.1 %collective-permute-start.7 = (f32[2,514,1]{1,0,2:T(2,128)S(1)}, f32[2,514,1]{1,0,2:T(2,128)S(1)}, u32[]{:S(2)}, u32[]{:S(2)}) collective-permute-start(f32[2,514,1]{1,0,2:T(2,128)S(1)} %copy.209), channel_id=1, source_target_pairs={{1,0},{2,1},{3,2},{4,3},{5,4},{6,5},{7,6},{0,7},{9,8},{10,9},{11,1... | collective-permute-start | bytes 12344 | tf_op jit(solution)/shard_map/ppermute | solution.py:21
  43.6 2.0 pad_maximum_fusion.2
  46.9 8.1 %fusion.39 = f32[2,512,512]{2,1,0:T(8,128)S(1)} fusion(f32[2,512,512]{2,1,0:T(8,128)} %copy-done.9, f32[2,514,1]{2,1,0:T(8,128)S(1)} %copy-done.16, f32[2,1,512]{2,1,0:T(1,128)S(1)} %collective-permute-done.5, f32[2,1,512]{2,1,0:T(1,128)S(1)} %collective-permute-done.4, f32[2,514,1]{2,1,0:T(8,128)} %copy-done.14, f32[2,512,514]{2,1,0:T(8,128)S(1)} %slice.600, ...), kind=kLoop, calls=%fused_computation.113 | loop fusion | flops 8912896 | bytes 6324288 | tf_op jit(solution)/shard_map/add | solution.py:47
  55.1 3.8 %collective-permute-start.9 = (f32[2,1,512]{2,1,0:T(1,128)S(1)}, f32[2,1,512]{2,1,0:T(1,128)S(1)}, u32[]{:S(2)}, u32[]{:S(2)}) collective-permute-start(f32[2,1,512]{2,1,0:T(1,128)S(1)} %get-tuple-element.87), channel_id=1, source_target_pairs={{8,0},{16,8},{24,16},{32,24},{40,32},{48,40},{56,48},{64,56},{72,6... | collective-permute-start | bytes 12296 | tf_op jit(solution)/shard_map/ppermute | solution.py:21
  58.9 1.3 collective-permute-done.8
  60.7 2.1 collective-permute-start.10
  63.1 3.8 %collective-permute-start.11 = (f32[2,514,1]{1,0,2:T(2,128)S(1)}, f32[2,514,1]{1,0,2:T(2,128)S(1)}, u32[]{:S(2)}, u32[]{:S(2)}) collective-permute-start(f32[2,514,1]{1,0,2:T(2,128)S(1)} %copy.215), channel_id=1, source_target_pairs={{1,0},{2,1},{3,2},{4,3},{5,4},{6,5},{7,6},{0,7},{9,8},{10,9},{11,1... | collective-permute-start | bytes 12344 | tf_op jit(solution)/shard_map/ppermute | solution.py:21
  66.9 1.4 collective-permute-done.10
  70.1 5.0 %fusion.33 = f32[2,512,512]{2,1,0:T(8,128)S(1)} fusion(f32[2,512,512]{2,1,0:T(8,128)S(1)} %fusion.39, f32[2,514,1]{2,1,0:T(8,128)S(1)} %copy.217, f32[2,1,512]{2,1,0:T(1,128)S(1)} %collective-permute-done.9, f32[2,1,512]{2,1,0:T(1,128)S(1)} %collective-permute-done.8, f32[2,514,1]{2,1,0:T(8,128)S(1)} %copy.216, f32[2,512,514]{2,1,0:T(8,128)S(1)} %slice.603, ...), kind=kLoop, calls=%fused_computation.97 | loop fusion | flops 8912896 | bytes 6324288 | tf_op jit(solution)/shard_map/add | solution.py:47
  75.2 3.8 %collective-permute-start.13 = (f32[2,1,512]{2,1,0:T(1,128)S(1)}, f32[2,1,512]{2,1,0:T(1,128)S(1)}, u32[]{:S(2)}, u32[]{:S(2)}) collective-permute-start(f32[2,1,512]{2,1,0:T(1,128)S(1)} %get-tuple-element.85), channel_id=1, source_target_pairs={{8,0},{16,8},{24,16},{32,24},{40,32},{48,40},{56,48},{64,56},{72,6... | collective-permute-start | bytes 12296 | tf_op jit(solution)/shard_map/ppermute | solution.py:21
  79.1 1.3 collective-permute-done.12
  80.9 2.3 collective-permute-start.14
  83.4 3.6 collective-permute-start.15
  90.3 5.0 %fusion.27 = f32[2,512,512]{2,1,0:T(8,128)S(1)} fusion(f32[2,512,512]{2,1,0:T(8,128)S(1)} %copy-done.1, f32[2,514,1]{2,1,0:T(8,128)S(1)} %copy.223, f32[2,1,512]{2,1,0:T(1,128)S(1)} %collective-permute-done.13, f32[2,1,512]{2,1,0:T(1,128)S(1)} %collective-permute-done.12, f32[2,514,1]{2,1,0:T(8,128)S(1)} %copy.222, f32[2,512,514]{2,1,0:T(8,128)S(1)} %slice.606, ...), kind=kLoop, calls=%fused_computation.81 | loop fusion | flops 8912896 | bytes 6324288 | tf_op jit(solution)/shard_map/add | solution.py:47
  95.4 3.8 %collective-permute-start.17 = (f32[2,1,512]{2,1,0:T(1,128)S(1)}, f32[2,1,512]{2,1,0:T(1,128)S(1)}, u32[]{:S(2)}, u32[]{:S(2)}) collective-permute-start(f32[2,1,512]{2,1,0:T(1,128)S(1)} %get-tuple-element.83), channel_id=1, source_target_pairs={{8,0},{16,8},{24,16},{32,24},{40,32},{48,40},{56,48},{64,56},{72,6... | collective-permute-start | bytes 12296 | tf_op jit(solution)/shard_map/ppermute | solution.py:21
  101.0 2.9 collective-permute-start.18
  104.2 2.8 collective-permute-start.19
  107.0 1.3 collective-permute-done.18
  111.0 5.0 %fusion.21 = f32[2,512,512]{2,1,0:T(8,128)S(1)} fusion(f32[2,512,512]{2,1,0:T(8,128)S(1)} %copy-done.3, f32[2,514,1]{2,1,0:T(8,128)S(1)} %copy.229, f32[2,1,512]{2,1,0:T(1,128)S(1)} %collective-permute-done.17, f32[2,1,512]{2,1,0:T(1,128)S(1)} %collective-permute-done.16, f32[2,514,1]{2,1,0:T(8,128)S(1)} %copy.228, f32[2,512,514]{2,1,0:T(8,128)S(1)} %slice.609, ...), kind=kLoop, calls=%fused_computation.65 | loop fusion | flops 8912896 | bytes 6324288 | tf_op jit(solution)/shard_map/add | solution.py:47
  116.0 3.8 %collective-permute-start.21 = (f32[2,1,512]{2,1,0:T(1,128)S(1)}, f32[2,1,512]{2,1,0:T(1,128)S(1)}, u32[]{:S(2)}, u32[]{:S(2)}) collective-permute-start(f32[2,1,512]{2,1,0:T(1,128)S(1)} %get-tuple-element.81), channel_id=1, source_target_pairs={{8,0},{16,8},{24,16},{32,24},{40,32},{48,40},{56,48},{64,56},{72,6... | collective-permute-start | bytes 12296 | tf_op jit(solution)/shard_map/ppermute | solution.py:21
  121.7 2.6 collective-permute-start.22
  124.5 3.5 collective-permute-start.23
  131.7 5.0 %fusion.15 = f32[2,512,512]{2,1,0:T(8,128)S(1)} fusion(f32[2,512,512]{2,1,0:T(8,128)S(1)} %copy-done.5, f32[2,514,1]{2,1,0:T(8,128)S(1)} %copy.235, f32[2,1,512]{2,1,0:T(1,128)S(1)} %collective-permute-done.21, f32[2,1,512]{2,1,0:T(1,128)S(1)} %collective-permute-done.20, f32[2,514,1]{2,1,0:T(8,128)S(1)} %copy.234, f32[2,512,514]{2,1,0:T(8,128)S(1)} %slice.612, ...), kind=kLoop, calls=%fused_computation.49 | loop fusion | flops 8912896 | bytes 6324288 | tf_op jit(solution)/shard_map/add | solution.py:47
  136.8 3.8 %collective-permute-start.25 = (f32[2,1,512]{2,1,0:T(1,128)S(1)}, f32[2,1,512]{2,1,0:T(1,128)S(1)}, u32[]{:S(2)}, u32[]{:S(2)}) collective-permute-start(f32[2,1,512]{2,1,0:T(1,128)S(1)} %get-tuple-element.79), channel_id=1, source_target_pairs={{8,0},{16,8},{24,16},{32,24},{40,32},{48,40},{56,48},{64,56},{72,6... | collective-permute-start | bytes 12296 | tf_op jit(solution)/shard_map/ppermute | solution.py:21
  142.4 2.6 collective-permute-start.26
  145.2 3.1 collective-permute-start.27
  148.3 1.3 collective-permute-done.26
  152.0 1.5 copy-done.8
  153.5 4.9 %fusion.9 = f32[2,512,512]{2,1,0:T(8,128)S(1)} fusion(f32[2,512,512]{2,1,0:T(8,128)S(1)} %copy-done.8, f32[2,514,1]{2,1,0:T(8,128)S(1)} %copy.241, f32[2,1,512]{2,1,0:T(1,128)S(1)} %collective-permute-done.25, f32[2,1,512]{2,1,0:T(1,128)S(1)} %collective-permute-done.24, f32[2,514,1]{2,1,0:T(8,128)S(1)} %copy.240, f32[2,512,514]{2,1,0:T(8,128)S(1)} %slice.615, ...), kind=kLoop, calls=%fused_computation.33 | loop fusion | flops 8912896 | bytes 6324288 | tf_op jit(solution)/shard_map/add | solution.py:47
  158.6 3.8 %collective-permute-start.29 = (f32[2,1,512]{2,1,0:T(1,128)S(1)}, f32[2,1,512]{2,1,0:T(1,128)S(1)}, u32[]{:S(2)}, u32[]{:S(2)}) collective-permute-start(f32[2,1,512]{2,1,0:T(1,128)S(1)} %get-tuple-element.77), channel_id=1, source_target_pairs={{8,0},{16,8},{24,16},{32,24},{40,32},{48,40},{56,48},{64,56},{72,6... | collective-permute-start | bytes 12296 | tf_op jit(solution)/shard_map/ppermute | solution.py:21
  164.2 2.6 collective-permute-start.30
  167.0 3.3 collective-permute-start.31
  173.9 5.9 %fusion.3 = f32[2,512,512]{2,1,0:T(8,128)} fusion(f32[2,512,512]{2,1,0:T(8,128)S(1)} %fusion.9, f32[2,514,1]{2,1,0:T(8,128)S(1)} %copy.247, f32[2,1,512]{2,1,0:T(1,128)S(1)} %collective-permute-done.29, f32[2,1,512]{2,1,0:T(1,128)S(1)} %collective-permute-done.28, f32[2,514,1]{2,1,0:T(8,128)S(1)} %copy.246, f32[2,512,514]{2,1,0:T(8,128)S(1)} %slice.618, ...), kind=kLoop, calls=%fused_computation.17 | loop fusion | flops 8912896 | bytes 6324288 | tf_op jit(solution)/shard_map/add | solution.py:47
  179.9 71.4 %reshape.326 = f32[2,128,4,128,4]{4,3,2,1,0:T(8,128)} reshape(f32[2,512,512]{2,1,0:T(8,128)} %fusion.3) | data formatting | bytes 4194304 | tf_op jit(solution)/shard_map/reshape | solution.py:106
  251.3 20.8 %reduce_sum.19 = f32[2,128,128]{2,1,0:T(8,128)S(1)} reduce(f32[2,128,4,128,4]{4,3,2,1,0:T(8,128)} %reshape.326, f32[]{:T(128)} %constant.89.clone.1), dimensions={2,4}, to_apply=%region_1.2 | reduce | flops 491520 | bytes 2228228 | tf_op jit(solution)/shard_map/reduce_sum | solution.py:106
  272.2 3.8 %collective-permute-start.33 = (f32[2,1,128]{2,1,0:T(1,128)S(1)}, f32[2,1,128]{2,1,0:T(1,128)S(1)}, u32[]{:S(2)}, u32[]{:S(2)}) collective-permute-start(f32[2,1,128]{2,1,0:T(1,128)S(1)} %get-tuple-element.113), channel_id=1, source_target_pairs={{8,0},{16,8},{24,16},{32,24},{40,32},{48,40},{56,48},{64,56},{72,6... | collective-permute-start | bytes 3080 | tf_op jit(solution)/shard_map/ppermute | solution.py:21
  277.5 4.3 %collective-permute-start.34 = (f32[2,130,1]{2,1,0:T(8,128)S(1)}, f32[2,130,1]{2,1,0:T(8,128)S(1)}, u32[]{:S(2)}, u32[]{:S(2)}) collective-permute-start(f32[2,130,1]{2,1,0:T(8,128)S(1)} %get-tuple-element.110), channel_id=1, source_target_pairs={{0,1},{1,2},{2,3},{3,4},{4,5},{5,6},{6,7},{7,0},{8,9},{9,10},{10,1... | collective-permute-start | bytes 3128 | tf_op jit(solution)/shard_map/ppermute | solution.py:19
  281.8 1.4 collective-permute-start.35
  283.2 3.0 collective-permute-done.34
  286.2 2.1 collective-permute-done.35
  291.3 14.1 %all_to_all.5 = f32[16,5,1024]{2,1,0:T(8,128)S(1)} all-to-all(f32[16,5,1024]{2,1,0:T(8,128)S(1)} %copy.251), channel_id=1, replica_groups=mesh['tile'=16,'col'=8] {'tile'}, dimensions={0} | all-to-all | bytes 655360 | tf_op jit(solution)/shard_map/all_to_all | solution.py:126
  307.2 1.5 convolution_bitcast_fusion
  308.7 64.0 %psum.7 = f32[16,16]{1,0:T(8,128)S(1)} all-reduce(f32[16,16]{1,0:T(8,128)S(1)} %convolution_bitcast_fusion), channel_id=1, replica_groups=mesh['tile'=16,'col'=8] {'tile','col'}, use_global_device_ids=true, to_apply=%region_2.3 | all-reduce | flops 256 | bytes 2048 | tf_op jit(solution)/shard_map/psum | solution.py:137
  (210 shorter events, 49.0 us)
Async XLA Ops:
  0.6 6.2 %copy-start.10 = (f32[512,512]{1,0:T(8,128)S(1)}, f32[512,512]{1,0:T(8,128)}, u32[]{:S(2)}) copy-start(f32[512,512]{1,0:T(8,128)} %param.5) | copy-start | bytes 3145732
  0.6 6.2 %copy-start.11 = (f32[512,512]{1,0:T(8,128)S(1)}, f32[512,512]{1,0:T(8,128)}, u32[]{:S(2)}) copy-start(f32[512,512]{1,0:T(8,128)} %param.6) | copy-start | bytes 3145732
  1.6 5.2 %collective-permute-start = (f32[2,1,512]{2,1,0:T(1,128)S(1)}, f32[2,1,512]{2,1,0:T(1,128)S(1)}, u32[]{:S(2)}, u32[]{:S(2)}) collective-permute-start(f32[2,1,512]{2,1,0:T(1,128)S(1)} %get-tuple-element.90), channel_id=1, source_target_pairs={{0,8},{8,16},{16,24},{24,32},{32,40},{40,48},{48,56},{56,64},{64,7... | collective-permute-start | bytes 12296 | tf_op jit(solution)/shard_map/ppermute | solution.py:19
  1.6 12.3 %copy-start.18 = (s32[16]{0:T(128)S(1)}, s32[16]{0:T(128)}, u32[]{:S(2)}) copy-start(s32[16]{0:T(128)} %param.9) | copy-start | bytes 196
  1.7 5.2 %collective-permute-start.1 = (f32[2,1,512]{2,1,0:T(1,128)S(1)}, f32[2,1,512]{2,1,0:T(1,128)S(1)}, u32[]{:S(2)}, u32[]{:S(2)}) collective-permute-start(f32[2,1,512]{2,1,0:T(1,128)S(1)} %get-tuple-element.91), channel_id=1, source_target_pairs={{8,0},{16,8},{24,16},{32,24},{40,32},{48,40},{56,48},{64,56},{72,6... | collective-permute-start | bytes 12296 | tf_op jit(solution)/shard_map/ppermute | solution.py:21
  7.3 10.6 %collective-permute-start.2 = (f32[2,514,1]{1,0,2:T(2,128)S(1)}, f32[2,514,1]{1,0,2:T(2,128)S(1)}, u32[]{:S(2)}, u32[]{:S(2)}) collective-permute-start(f32[2,514,1]{1,0,2:T(2,128)S(1)} %copy.202), channel_id=1, source_target_pairs={{0,1},{1,2},{2,3},{3,4},{4,5},{5,6},{6,7},{7,0},{8,9},{9,10},{10,1... | collective-permute-start | bytes 12344 | tf_op jit(solution)/shard_map/ppermute | solution.py:19
  11.5 6.6 %collective-permute-start.3 = (f32[2,514,1]{1,0,2:T(2,128)S(1)}, f32[2,514,1]{1,0,2:T(2,128)S(1)}, u32[]{:S(2)}, u32[]{:S(2)}) collective-permute-start(f32[2,514,1]{1,0,2:T(2,128)S(1)} %copy.203), channel_id=1, source_target_pairs={{1,0},{2,1},{3,2},{4,3},{5,4},{6,5},{7,6},{0,7},{9,8},{10,9},{11,1... | collective-permute-start | bytes 12344 | tf_op jit(solution)/shard_map/ppermute | solution.py:21
  27.3 19.5 %copy-start.9 = (f32[2,512,512]{2,1,0:T(8,128)}, f32[2,512,512]{2,1,0:T(8,128)S(1)}, u32[]{:S(2)}) copy-start(f32[2,512,512]{2,1,0:T(8,128)S(1)} %fusion.45) | copy-start | bytes 6291460
  27.3 5.2 %collective-permute-start.4 = (f32[2,1,512]{2,1,0:T(1,128)S(1)}, f32[2,1,512]{2,1,0:T(1,128)S(1)}, u32[]{:S(2)}, u32[]{:S(2)}) collective-permute-start(f32[2,1,512]{2,1,0:T(1,128)S(1)} %get-tuple-element.88), channel_id=1, source_target_pairs={{0,8},{8,16},{16,24},{24,32},{32,40},{40,48},{48,56},{56,64},{64,7... | collective-permute-start | bytes 12296 | tf_op jit(solution)/shard_map/ppermute | solution.py:19
  27.4 5.2 %collective-permute-start.5 = (f32[2,1,512]{2,1,0:T(1,128)S(1)}, f32[2,1,512]{2,1,0:T(1,128)S(1)}, u32[]{:S(2)}, u32[]{:S(2)}) collective-permute-start(f32[2,1,512]{2,1,0:T(1,128)S(1)} %get-tuple-element.89), channel_id=1, source_target_pairs={{8,0},{16,8},{24,16},{32,24},{40,32},{48,40},{56,48},{64,56},{72,6... | collective-permute-start | bytes 12296 | tf_op jit(solution)/shard_map/ppermute | solution.py:21
  34.8 7.3 %collective-permute-start.6 = (f32[2,514,1]{1,0,2:T(2,128)S(1)}, f32[2,514,1]{1,0,2:T(2,128)S(1)}, u32[]{:S(2)}, u32[]{:S(2)}) collective-permute-start(f32[2,514,1]{1,0,2:T(2,128)S(1)} %copy.208), channel_id=1, source_target_pairs={{0,1},{1,2},{2,3},{3,4},{4,5},{5,6},{6,7},{7,0},{8,9},{9,10},{10,1... | collective-permute-start | bytes 12344 | tf_op jit(solution)/shard_map/ppermute | solution.py:19
  36.2 6.4 %collective-permute-start.7 = (f32[2,514,1]{1,0,2:T(2,128)S(1)}, f32[2,514,1]{1,0,2:T(2,128)S(1)}, u32[]{:S(2)}, u32[]{:S(2)}) collective-permute-start(f32[2,514,1]{1,0,2:T(2,128)S(1)} %copy.209), channel_id=1, source_target_pairs={{1,0},{2,1},{3,2},{4,3},{5,4},{6,5},{7,6},{0,7},{9,8},{10,9},{11,1... | collective-permute-start | bytes 12344 | tf_op jit(solution)/shard_map/ppermute | solution.py:21
  55.0 5.2 %collective-permute-start.8 = (f32[2,1,512]{2,1,0:T(1,128)S(1)}, f32[2,1,512]{2,1,0:T(1,128)S(1)}, u32[]{:S(2)}, u32[]{:S(2)}) collective-permute-start(f32[2,1,512]{2,1,0:T(1,128)S(1)} %get-tuple-element.86), channel_id=1, source_target_pairs={{0,8},{8,16},{16,24},{24,32},{32,40},{40,48},{48,56},{56,64},{64,7... | collective-permute-start | bytes 12296 | tf_op jit(solution)/shard_map/ppermute | solution.py:19
  55.1 5.2 %collective-permute-start.9 = (f32[2,1,512]{2,1,0:T(1,128)S(1)}, f32[2,1,512]{2,1,0:T(1,128)S(1)}, u32[]{:S(2)}, u32[]{:S(2)}) collective-permute-start(f32[2,1,512]{2,1,0:T(1,128)S(1)} %get-tuple-element.87), channel_id=1, source_target_pairs={{8,0},{16,8},{24,16},{32,24},{40,32},{48,40},{56,48},{64,56},{72,6... | collective-permute-start | bytes 12296 | tf_op jit(solution)/shard_map/ppermute | solution.py:21
  60.7 7.6 %collective-permute-start.10 = (f32[2,514,1]{1,0,2:T(2,128)S(1)}, f32[2,514,1]{1,0,2:T(2,128)S(1)}, u32[]{:S(2)}, u32[]{:S(2)}) collective-permute-start(f32[2,514,1]{1,0,2:T(2,128)S(1)} %copy.214), channel_id=1, source_target_pairs={{0,1},{1,2},{2,3},{3,4},{4,5},{5,6},{6,7},{7,0},{8,9},{9,10},{10,1... | collective-permute-start | bytes 12344 | tf_op jit(solution)/shard_map/ppermute | solution.py:19
  63.1 5.5 %collective-permute-start.11 = (f32[2,514,1]{1,0,2:T(2,128)S(1)}, f32[2,514,1]{1,0,2:T(2,128)S(1)}, u32[]{:S(2)}, u32[]{:S(2)}) collective-permute-start(f32[2,514,1]{1,0,2:T(2,128)S(1)} %copy.215), channel_id=1, source_target_pairs={{1,0},{2,1},{3,2},{4,3},{5,4},{6,5},{7,6},{0,7},{9,8},{10,9},{11,1... | collective-permute-start | bytes 12344 | tf_op jit(solution)/shard_map/ppermute | solution.py:21
  75.1 5.2 %collective-permute-start.12 = (f32[2,1,512]{2,1,0:T(1,128)S(1)}, f32[2,1,512]{2,1,0:T(1,128)S(1)}, u32[]{:S(2)}, u32[]{:S(2)}) collective-permute-start(f32[2,1,512]{2,1,0:T(1,128)S(1)} %get-tuple-element.84), channel_id=1, source_target_pairs={{0,8},{8,16},{16,24},{24,32},{32,40},{40,48},{48,56},{56,64},{64,7... | collective-permute-start | bytes 12296 | tf_op jit(solution)/shard_map/ppermute | solution.py:19
  75.2 5.2 %collective-permute-start.13 = (f32[2,1,512]{2,1,0:T(1,128)S(1)}, f32[2,1,512]{2,1,0:T(1,128)S(1)}, u32[]{:S(2)}, u32[]{:S(2)}) collective-permute-start(f32[2,1,512]{2,1,0:T(1,128)S(1)} %get-tuple-element.85), channel_id=1, source_target_pairs={{8,0},{16,8},{24,16},{32,24},{40,32},{48,40},{56,48},{64,56},{72,6... | collective-permute-start | bytes 12296 | tf_op jit(solution)/shard_map/ppermute | solution.py:21
  80.6 8.3 %copy-start.1 = (f32[2,512,512]{2,1,0:T(8,128)S(1)}, f32[2,512,512]{2,1,0:T(8,128)}, u32[]{:S(2)}) copy-start(f32[2,512,512]{2,1,0:T(8,128)} %copy-done) | copy-start | bytes 6291460
  80.9 7.3 %collective-permute-start.14 = (f32[2,514,1]{1,0,2:T(2,128)S(1)}, f32[2,514,1]{1,0,2:T(2,128)S(1)}, u32[]{:S(2)}, u32[]{:S(2)}) collective-permute-start(f32[2,514,1]{1,0,2:T(2,128)S(1)} %copy.220), channel_id=1, source_target_pairs={{0,1},{1,2},{2,3},{3,4},{4,5},{5,6},{6,7},{7,0},{8,9},{9,10},{10,1... | collective-permute-start | bytes 12344 | tf_op jit(solution)/shard_map/ppermute | solution.py:19
  83.4 5.3 %collective-permute-start.15 = (f32[2,514,1]{1,0,2:T(2,128)S(1)}, f32[2,514,1]{1,0,2:T(2,128)S(1)}, u32[]{:S(2)}, u32[]{:S(2)}) collective-permute-start(f32[2,514,1]{1,0,2:T(2,128)S(1)} %copy.221), channel_id=1, source_target_pairs={{1,0},{2,1},{3,2},{4,3},{5,4},{6,5},{7,6},{0,7},{9,8},{10,9},{11,1... | collective-permute-start | bytes 12344 | tf_op jit(solution)/shard_map/ppermute | solution.py:21
  95.3 5.2 %collective-permute-start.16 = (f32[2,1,512]{2,1,0:T(1,128)S(1)}, f32[2,1,512]{2,1,0:T(1,128)S(1)}, u32[]{:S(2)}, u32[]{:S(2)}) collective-permute-start(f32[2,1,512]{2,1,0:T(1,128)S(1)} %get-tuple-element.82), channel_id=1, source_target_pairs={{0,8},{8,16},{16,24},{24,32},{32,40},{40,48},{48,56},{56,64},{64,7... | collective-permute-start | bytes 12296 | tf_op jit(solution)/shard_map/ppermute | solution.py:19
  95.4 5.2 %collective-permute-start.17 = (f32[2,1,512]{2,1,0:T(1,128)S(1)}, f32[2,1,512]{2,1,0:T(1,128)S(1)}, u32[]{:S(2)}, u32[]{:S(2)}) collective-permute-start(f32[2,1,512]{2,1,0:T(1,128)S(1)} %get-tuple-element.83), channel_id=1, source_target_pairs={{8,0},{16,8},{24,16},{32,24},{40,32},{48,40},{56,48},{64,56},{72,6... | collective-permute-start | bytes 12296 | tf_op jit(solution)/shard_map/ppermute | solution.py:21
  100.8 8.8 %copy-start.3 = (f32[2,512,512]{2,1,0:T(8,128)S(1)}, f32[2,512,512]{2,1,0:T(8,128)}, u32[]{:S(2)}) copy-start(f32[2,512,512]{2,1,0:T(8,128)} %copy-done.2) | copy-start | bytes 6291460
  101.0 7.3 %collective-permute-start.18 = (f32[2,514,1]{1,0,2:T(2,128)S(1)}, f32[2,514,1]{1,0,2:T(2,128)S(1)}, u32[]{:S(2)}, u32[]{:S(2)}) collective-permute-start(f32[2,514,1]{1,0,2:T(2,128)S(1)} %copy.226), channel_id=1, source_target_pairs={{0,1},{1,2},{2,3},{3,4},{4,5},{5,6},{6,7},{7,0},{8,9},{9,10},{10,1... | collective-permute-start | bytes 12344 | tf_op jit(solution)/shard_map/ppermute | solution.py:19
  104.2 5.2 %collective-permute-start.19 = (f32[2,514,1]{1,0,2:T(2,128)S(1)}, f32[2,514,1]{1,0,2:T(2,128)S(1)}, u32[]{:S(2)}, u32[]{:S(2)}) collective-permute-start(f32[2,514,1]{1,0,2:T(2,128)S(1)} %copy.227), channel_id=1, source_target_pairs={{1,0},{2,1},{3,2},{4,3},{5,4},{6,5},{7,6},{0,7},{9,8},{10,9},{11,1... | collective-permute-start | bytes 12344 | tf_op jit(solution)/shard_map/ppermute | solution.py:21
  115.9 5.3 %copy-start.4 = (f32[2,512,512]{2,1,0:T(8,128)}, f32[2,512,512]{2,1,0:T(8,128)S(1)}, u32[]{:S(2)}) copy-start(f32[2,512,512]{2,1,0:T(8,128)S(1)} %fusion.21) | copy-start | bytes 6291460
  116.0 5.2 %collective-permute-start.20 = (f32[2,1,512]{2,1,0:T(1,128)S(1)}, f32[2,1,512]{2,1,0:T(1,128)S(1)}, u32[]{:S(2)}, u32[]{:S(2)}) collective-permute-start(f32[2,1,512]{2,1,0:T(1,128)S(1)} %get-tuple-element.80), channel_id=1, source_target_pairs={{0,8},{8,16},{16,24},{24,32},{32,40},{40,48},{48,56},{56,64},{64,7... | collective-permute-start | bytes 12296 | tf_op jit(solution)/shard_map/ppermute | solution.py:19
  116.0 5.2 %collective-permute-start.21 = (f32[2,1,512]{2,1,0:T(1,128)S(1)}, f32[2,1,512]{2,1,0:T(1,128)S(1)}, u32[]{:S(2)}, u32[]{:S(2)}) collective-permute-start(f32[2,1,512]{2,1,0:T(1,128)S(1)} %get-tuple-element.81), channel_id=1, source_target_pairs={{8,0},{16,8},{24,16},{32,24},{40,32},{48,40},{56,48},{64,56},{72,6... | collective-permute-start | bytes 12296 | tf_op jit(solution)/shard_map/ppermute | solution.py:21
  121.5 8.8 %copy-start.5 = (f32[2,512,512]{2,1,0:T(8,128)S(1)}, f32[2,512,512]{2,1,0:T(8,128)}, u32[]{:S(2)}) copy-start(f32[2,512,512]{2,1,0:T(8,128)} %copy-done.4) | copy-start | bytes 6291460
  121.7 7.3 %collective-permute-start.22 = (f32[2,514,1]{1,0,2:T(2,128)S(1)}, f32[2,514,1]{1,0,2:T(2,128)S(1)}, u32[]{:S(2)}, u32[]{:S(2)}) collective-permute-start(f32[2,514,1]{1,0,2:T(2,128)S(1)} %copy.232), channel_id=1, source_target_pairs={{0,1},{1,2},{2,3},{3,4},{4,5},{5,6},{6,7},{7,0},{8,9},{9,10},{10,1... | collective-permute-start | bytes 12344 | tf_op jit(solution)/shard_map/ppermute | solution.py:19
  124.5 5.6 %collective-permute-start.23 = (f32[2,514,1]{1,0,2:T(2,128)S(1)}, f32[2,514,1]{1,0,2:T(2,128)S(1)}, u32[]{:S(2)}, u32[]{:S(2)}) collective-permute-start(f32[2,514,1]{1,0,2:T(2,128)S(1)} %copy.233), channel_id=1, source_target_pairs={{1,0},{2,1},{3,2},{4,3},{5,4},{6,5},{7,6},{0,7},{9,8},{10,9},{11,1... | collective-permute-start | bytes 12344 | tf_op jit(solution)/shard_map/ppermute | solution.py:21
  136.7 5.2 %collective-permute-start.24 = (f32[2,1,512]{2,1,0:T(1,128)S(1)}, f32[2,1,512]{2,1,0:T(1,128)S(1)}, u32[]{:S(2)}, u32[]{:S(2)}) collective-permute-start(f32[2,1,512]{2,1,0:T(1,128)S(1)} %get-tuple-element.78), channel_id=1, source_target_pairs={{0,8},{8,16},{16,24},{24,32},{32,40},{40,48},{48,56},{56,64},{64,7... | collective-permute-start | bytes 12296 | tf_op jit(solution)/shard_map/ppermute | solution.py:19
  136.8 5.2 %collective-permute-start.25 = (f32[2,1,512]{2,1,0:T(1,128)S(1)}, f32[2,1,512]{2,1,0:T(1,128)S(1)}, u32[]{:S(2)}, u32[]{:S(2)}) collective-permute-start(f32[2,1,512]{2,1,0:T(1,128)S(1)} %get-tuple-element.79), channel_id=1, source_target_pairs={{8,0},{16,8},{24,16},{32,24},{40,32},{48,40},{56,48},{64,56},{72,6... | collective-permute-start | bytes 12296 | tf_op jit(solution)/shard_map/ppermute | solution.py:21
  142.2 8.5 %copy-start.7 = (f32[2,512,512]{2,1,0:T(8,128)S(1)}, f32[2,512,512]{2,1,0:T(8,128)}, u32[]{:S(2)}) copy-start(f32[2,512,512]{2,1,0:T(8,128)} %copy-done.6) | copy-start | bytes 6291460
  142.4 7.3 %collective-permute-start.26 = (f32[2,514,1]{1,0,2:T(2,128)S(1)}, f32[2,514,1]{1,0,2:T(2,128)S(1)}, u32[]{:S(2)}, u32[]{:S(2)}) collective-permute-start(f32[2,514,1]{1,0,2:T(2,128)S(1)} %copy.238), channel_id=1, source_target_pairs={{0,1},{1,2},{2,3},{3,4},{4,5},{5,6},{6,7},{7,0},{8,9},{9,10},{10,1... | collective-permute-start | bytes 12344 | tf_op jit(solution)/shard_map/ppermute | solution.py:19
  145.2 5.2 %collective-permute-start.27 = (f32[2,514,1]{1,0,2:T(2,128)S(1)}, f32[2,514,1]{1,0,2:T(2,128)S(1)}, u32[]{:S(2)}, u32[]{:S(2)}) collective-permute-start(f32[2,514,1]{1,0,2:T(2,128)S(1)} %copy.239), channel_id=1, source_target_pairs={{1,0},{2,1},{3,2},{4,3},{5,4},{6,5},{7,6},{0,7},{9,8},{10,9},{11,1... | collective-permute-start | bytes 12344 | tf_op jit(solution)/shard_map/ppermute | solution.py:21
  158.5 5.2 %collective-permute-start.28 = (f32[2,1,512]{2,1,0:T(1,128)S(1)}, f32[2,1,512]{2,1,0:T(1,128)S(1)}, u32[]{:S(2)}, u32[]{:S(2)}) collective-permute-start(f32[2,1,512]{2,1,0:T(1,128)S(1)} %get-tuple-element.76), channel_id=1, source_target_pairs={{0,8},{8,16},{16,24},{24,32},{32,40},{40,48},{48,56},{56,64},{64,7... | collective-permute-start | bytes 12296 | tf_op jit(solution)/shard_map/ppermute | solution.py:19
  158.5 11.7 %copy-start.19 = (s32[4,4]{1,0:T(4,128)S(1)}, s32[4,4]{1,0:T(4,128)}, u32[]{:S(2)}) copy-start(s32[4,4]{1,0:T(4,128)} %param.7) | copy-start | bytes 196
  158.6 11.8 %copy-start.20 = (s32[4,4]{1,0:T(4,128)S(1)}, s32[4,4]{1,0:T(4,128)}, u32[]{:S(2)}) copy-start(s32[4,4]{1,0:T(4,128)} %param.8) | copy-start | bytes 196
  158.6 5.2 %collective-permute-start.29 = (f32[2,1,512]{2,1,0:T(1,128)S(1)}, f32[2,1,512]{2,1,0:T(1,128)S(1)}, u32[]{:S(2)}, u32[]{:S(2)}) collective-permute-start(f32[2,1,512]{2,1,0:T(1,128)S(1)} %get-tuple-element.77), channel_id=1, source_target_pairs={{8,0},{16,8},{24,16},{32,24},{40,32},{48,40},{56,48},{64,56},{72,6... | collective-permute-start | bytes 12296 | tf_op jit(solution)/shard_map/ppermute | solution.py:21
  164.2 7.3 %collective-permute-start.30 = (f32[2,514,1]{1,0,2:T(2,128)S(1)}, f32[2,514,1]{1,0,2:T(2,128)S(1)}, u32[]{:S(2)}, u32[]{:S(2)}) collective-permute-start(f32[2,514,1]{1,0,2:T(2,128)S(1)} %copy.244), channel_id=1, source_target_pairs={{0,1},{1,2},{2,3},{3,4},{4,5},{5,6},{6,7},{7,0},{8,9},{9,10},{10,1... | collective-permute-start | bytes 12344 | tf_op jit(solution)/shard_map/ppermute | solution.py:19
  167.0 5.3 %collective-permute-start.31 = (f32[2,514,1]{1,0,2:T(2,128)S(1)}, f32[2,514,1]{1,0,2:T(2,128)S(1)}, u32[]{:S(2)}, u32[]{:S(2)}) collective-permute-start(f32[2,514,1]{1,0,2:T(2,128)S(1)} %copy.245), channel_id=1, source_target_pairs={{1,0},{2,1},{3,2},{4,3},{5,4},{6,5},{7,6},{0,7},{9,8},{10,9},{11,1... | collective-permute-start | bytes 12344 | tf_op jit(solution)/shard_map/ppermute | solution.py:21
  272.1 5.3 %collective-permute-start.32 = (f32[2,1,128]{2,1,0:T(1,128)S(1)}, f32[2,1,128]{2,1,0:T(1,128)S(1)}, u32[]{:S(2)}, u32[]{:S(2)}) collective-permute-start(f32[2,1,128]{2,1,0:T(1,128)S(1)} %get-tuple-element.112), channel_id=1, source_target_pairs={{0,8},{8,16},{16,24},{24,32},{32,40},{40,48},{48,56},{56,64},{64,7... | collective-permute-start | bytes 3080 | tf_op jit(solution)/shard_map/ppermute | solution.py:19
  272.2 5.2 %collective-permute-start.33 = (f32[2,1,128]{2,1,0:T(1,128)S(1)}, f32[2,1,128]{2,1,0:T(1,128)S(1)}, u32[]{:S(2)}, u32[]{:S(2)}) collective-permute-start(f32[2,1,128]{2,1,0:T(1,128)S(1)} %get-tuple-element.113), channel_id=1, source_target_pairs={{8,0},{16,8},{24,16},{32,24},{40,32},{48,40},{56,48},{64,56},{72,6... | collective-permute-start | bytes 3080 | tf_op jit(solution)/shard_map/ppermute | solution.py:21
  277.5 8.7 %collective-permute-start.34 = (f32[2,130,1]{2,1,0:T(8,128)S(1)}, f32[2,130,1]{2,1,0:T(8,128)S(1)}, u32[]{:S(2)}, u32[]{:S(2)}) collective-permute-start(f32[2,130,1]{2,1,0:T(8,128)S(1)} %get-tuple-element.110), channel_id=1, source_target_pairs={{0,1},{1,2},{2,3},{3,4},{4,5},{5,6},{6,7},{7,0},{8,9},{9,10},{10,1... | collective-permute-start | bytes 3128 | tf_op jit(solution)/shard_map/ppermute | solution.py:19
  281.8 6.6 %collective-permute-start.35 = (f32[2,130,1]{2,1,0:T(8,128)S(1)}, f32[2,130,1]{2,1,0:T(8,128)S(1)}, u32[]{:S(2)}, u32[]{:S(2)}) collective-permute-start(f32[2,130,1]{2,1,0:T(8,128)S(1)} %get-tuple-element.111), channel_id=1, source_target_pairs={{1,0},{2,1},{3,2},{4,3},{5,4},{6,5},{7,6},{0,7},{9,8},{10,9},{11,1... | collective-permute-start | bytes 3128 | tf_op jit(solution)/shard_map/ppermute | solution.py:21
  307.2 66.1 %copy-start.17 = (f32[16,16,1024]{2,1,0:T(8,128)}, f32[16,16,1024]{2,1,0:T(8,128)S(1)}, u32[]{:S(2)}) copy-start(f32[16,16,1024]{2,1,0:T(8,128)S(1)} %stack.159) | copy-start | bytes 3145732
  (9 other events, 27.0 us)
where the time goes:
time: 381 us; the launch traced here: 373 us
  local copies, waits for them, and re-layouts  89.5 us (23%)
  starting transfers between devices  88.9 us (23%)
  other arithmetic  81.8 us (21%)
  blocking collectives  78 us (20%)
  waiting for transfers between devices  28.3 us (7%)
  between operations  5.21 us (1%)
    reshape x1, local copies, waits for them, and re-layouts, per_device(): field.reshape(2, fine_rows // 4, 4, fine_cols // 4, 4).mean(axis=(2, 4))  71.4 us
    psum x1, blocking collectives, per_device(): gram = lax.psum(part, ('tile', 'col')) / (fine_rows // 4 * (fine_cols // 4))  64 us
    ppermute x18, starting transfers between devices, with_halo(): lax.ppermute(head, axis, [((i + 1) % count, i) for i in range(count)])  63.7 us
    add x8, other arithmetic, relax(): return centre + KAPPA * (beside_all - 4.0 * centre)  45.1 us
    ppermute x18, starting transfers between devices, with_halo(): lax.ppermute(tail, axis, [(i, (i + 1) % count) for i in range(count)])  25.2 us
    ppermute x18, waiting for transfers between devices, with_halo(): lax.ppermute(tail, axis, [(i, (i + 1) % count) for i in range(count)])  22.4 us
    reduce_sum x1, other arithmetic, per_device(): field.reshape(2, fine_rows // 4, 4, fine_cols // 4, 4).mean(axis=(2, 4))  20.8 us
    all_to_all x1, blocking collectives, per_device(): lax.all_to_all(jnp.einsum('vh,hsd->vsd', chosen_terms, starting_tile_set,...  14.1 us
  transfers between devices with their start and end apart: 36, of which 24 were waited for; matrix products, arithmetic and copies ran while one was open for 1% of the time, Pallas kernels for 0%

commit v1 on v0

v1 whole, which is shorter than its diff:
```python
import math

import jax
import jax.numpy as jnp
import ml_dtypes
import numpy as np
from jax import lax
from jax.experimental import pallas as pl
from jax.experimental.pallas import tpu as pltpu
from jax.sharding import PartitionSpec as P

PASSES = 8
KAPPA = 0.2
POOL = 4
CELLS = 128
HALO = 12
SIDE = 32
TERMS = 16
PAD = 8
FULL = CELLS + 2 * PAD
LANES = 128
BASES = 5
BLOCK_ROWS = 48
F32 = jnp.float32
BF16 = jnp.bfloat16

EDGE_COLS = (-1, -2, CELLS + 1, CELLS)
SCALE = KAPPA**PASSES / (POOL * POOL)


def across(power, fine, coarse):
    total = 0
    for inner in range(POOL):
        offset = fine - (POOL * coarse + inner)
        if abs(offset) <= power and (power + offset) % 2 == 0:
            total += math.comb(power, (power + offset) // 2)
    return total


def column_weights():
    fine = CELLS * POOL
    weights = np.zeros((fine, 10 * LANES), np.float32)
    for j in range(PASSES + 1):
        block = PASSES - j
        for coarse in range(CELLS):
            for f in range(max(0, POOL * coarse - 8), min(fine, POOL * coarse + 12)):
                weights[f, block * LANES + coarse] = math.comb(PASSES, j) * across(PASSES - j, f, coarse)
        for place, coarse in enumerate(EDGE_COLS):
            for f in range(max(0, POOL * coarse - 8), min(fine, POOL * coarse + 12)):
                weights[f, 9 * LANES + 4 * j + place] = math.comb(PASSES, j) * across(PASSES - j, f, coarse)
    out = weights.astype(ml_dtypes.bfloat16)
    assert (out.astype(np.float32) == weights).all()
    return out


def send_selectors():
    sel = np.zeros((2, 16, 6 * LANES), np.float32)
    spots = ((0, 1, 1), (1, 1, 0), (2, 0, 0), (8, 0, CELLS - 1), (9, 1, 3), (10, 1, 2))
    for f in range(2):
        for row, source, lane in spots:
            for piece in range(3):
                sel[f, row + 3 * f, (source * 3 + piece) * LANES + lane] = 1.0
    return sel.astype(ml_dtypes.bfloat16)


def place_matrix():
    place = np.zeros((3, 16, 4 * LANES), np.float32)
    for f in range(2):
        add, rim = 2 * f * LANES, (2 * f + 1) * LANES
        place[:, 3 * f + 0, rim + 0] = 1.0
        place[:, 3 * f + 1, add + 0] = 1.0
        place[:, 3 * f + 2, add + 1] = 1.0
        place[:, 8 + 3 * f + 0, add + CELLS - 2] = 1.0
        place[:, 8 + 3 * f + 1, add + CELLS - 1] = 1.0
        place[:, 8 + 3 * f + 2, rim + CELLS - 1] = 1.0
    return place.reshape(48, 4 * LANES).astype(ml_dtypes.bfloat16)


def head(x):
    scaled = x * 65537.0
    return scaled - (scaled - x)


def two_parts(x):
    high = head(x)
    return high.astype(BF16), (x - high).astype(BF16)


def three_parts(x):
    high = head(x)
    rest = x - high
    mid = head(rest)
    return high.astype(BF16), mid.astype(BF16), (rest - mid).astype(BF16)


def dot(a, b, dims=(((1,), (0,)), ((), ()))):
    return lax.dot_general(a, b, dims, preferred_element_type=F32)


def three_rows(t):
    rows = t[0].shape[0]
    up = pltpu.roll(t[3], 1, 0)
    down = pltpu.roll(t[0], rows - 1, 0)
    left, middle, right = t[0] + t[1], t[1] + t[2], t[2] + t[3]
    return [left + up, t[0] + middle, middle + t[3], right + down]


def own_kernel(*refs):
    w_ref, main_ref, edge_ref, high_ref, low_ref, sum_ref, first_ref, last_ref = refs[8:]
    for f in range(2):
        for c in range(4):
            for p in range(POOL):
                high, low = two_parts(refs[4 * f + c][pl.ds(p, CELLS, stride=POOL), :])
                spot = pl.ds((f * POOL + p) * CELLS, CELLS)
                high_ref[spot, c * LANES : (c + 1) * LANES] = high
                low_ref[spot, c * LANES : (c + 1) * LANES] = low
    for t in range(5):
        w = w_ref[:, 2 * t * LANES : 2 * (t + 1) * LANES]
        z = dot(high_ref[...], w) + dot(low_ref[...], w)
        for half in range(2):
            part = z[:, half * LANES : (half + 1) * LANES]
            stage = 2 * t + half
            for f in range(2):
                for_phase = [part[(f * POOL + p) * CELLS : (f * POOL + p + 1) * CELLS] for p in range(POOL)]
                if stage in (0, 9):
                    into = (sum_ref if stage == 0 else first_ref).at[f]
                    for p in range(POOL):
                        into[p, :PAD] = jnp.zeros((PAD, LANES), F32)
                        into[p, PAD:] = for_phase[p]
                else:
                    new = three_rows([sum_ref[f, p] for p in range(POOL)])
                    for p in range(POOL):
                        sum_ref[f, p, :PAD] = new[p][:PAD]
                        sum_ref[f, p, PAD:] = new[p][PAD:] + for_phase[p]
    for f in range(2):
        for p in range(POOL):
            last_ref[f, p] = first_ref[f, p]

    @pl.loop(0, PASSES)
    def _(step):
        for f in range(2):
            new = three_rows([pltpu.roll(last_ref[f, p], LANES - 4, 1) for p in range(POOL)])
            for p in range(POOL):
                last_ref[f, p] = new[p] + first_ref[f, p]

    for f in range(2):
        for from_ref, to_ref in ((sum_ref, main_ref), (last_ref, edge_ref)):
            pooled = ((from_ref[f, 0] + from_ref[f, 1]) + (from_ref[f, 2] + from_ref[f, 3])) * SCALE
            to_ref[f, : PAD + CELLS] = pooled
            to_ref[f, PAD + CELLS :] = pooled[:PAD]


def turn(first, second, k):
    cosine = jnp.where(k == 0, 1.0, jnp.where(k == 2, -1.0, 0.0)).astype(F32)
    sine = jnp.where(k == 1, 1.0, jnp.where(k == 3, -1.0, 0.0)).astype(F32)
    return cosine * first - sine * second, sine * first + cosine * second


def strip_kernel(turns_ref, above_ref, below_ref, w_ref, sel_ref, main_in, edge_in, main_ref, edge_ref, left_ref,
                 right_ref, rows_ref, strip_ref):
    tiles = turns_ref.shape[0] - 1
    here = turns_ref[tiles]
    k_top = turns_ref[here]
    k_bottom = lax.rem(4 - turns_ref[lax.rem(here + 1, tiles)], 4)
    strip_ref[...] = jnp.zeros_like(strip_ref)
    for s, (x_ref, k, start) in enumerate(((above_ref, k_top, 1), (below_ref, k_bottom, 4))):
        turned = turn(x_ref[:HALO], x_ref[HALO:], k)
        for f in range(2):
            for c in range(4):
                cut = slice(c * LANES, (c + 1) * LANES)
                rows_ref[s, f, c, :HALO] = turned[f][:, cut]
                for p in range(POOL):
                    spot = ((f * 2 + s) * POOL + p) * 8 + start
                    strip_ref[spot : spot + 3, cut] = rows_ref[s, f, c, pl.ds(p, 3, stride=POOL), :]
    high, low = two_parts(strip_ref[...])
    main_ref[...] = main_in[...]
    edge_ref[...] = edge_in[...]
    sums = [None] * 4
    for t in range(5):
        w = w_ref[:, 2 * t * LANES : 2 * (t + 1) * LANES]
        z = dot(high, w) + dot(low, w)
        for half in range(2):
            part = z[:, half * LANES : (half + 1) * LANES]
            stage = 2 * t + half
            for g in range(4):
                own = [part[(g * POOL + p) * 8 : (g * POOL + p + 1) * 8] for p in range(POOL)]
                if stage == 0:
                    sums[g] = own
                elif stage < 9:
                    sums[g] = [a + b for a, b in zip(three_rows(sums[g]), own)]
                else:
                    last = own
                    for _ in range(PASSES):
                        last = [a + b for a, b in zip(three_rows([pltpu.roll(x, LANES - 4, 1) for x in last]), own)]
                    f, s = g // 2, g % 2
                    spot, cut = ((7, 3), (PAD + CELLS - 2, 2))[s]
                    for to_ref, x in ((main_ref, sums[g]), (edge_ref, last)):
                        pooled = ((x[0] + x[1]) + (x[2] + x[3])) * SCALE
                        to_ref[f, spot : spot + 3] = to_ref[f, spot : spot + 3] + pooled[cut : cut + 3]
    out = jnp.zeros((16, FULL), F32)
    for f in range(2):
        parts = jnp.concatenate(three_parts(main_ref[f]) + three_parts(edge_ref[f]), axis=1)
        out = out + dot(sel_ref[f], parts, (((1,), (1,)), ((), ())))
    left_ref[...] = out[:8]
    right_ref[...] = out[8:]


def base_kernel(mask_ref, owner_ref, main_ref, edge_ref, from_left_ref, from_right_ref, place_ref, out_ref, field_ref,
                base_ref, term_ref, gram_ref):
    lane = lax.broadcasted_iota(jnp.int32, (1, LANES), 1)
    received = jnp.concatenate([from_left_ref[...], from_right_ref[...]], axis=0)
    placed = dot(jnp.concatenate(three_parts(received), axis=0), place_ref[...], (((0,), (0,)), ((), ())))
    inner = slice(PAD, PAD + CELLS)
    slopes = []
    for f in range(2):
        full = main_ref[f] + placed[:, 2 * f * LANES : (2 * f + 1) * LANES]
        field_ref[f] = full
        edge = edge_ref[f, inner]
        rim = placed[inner, (2 * f + 1) * LANES : (2 * f + 2) * LANES]
        rim = rim + jnp.where(lane == 0, edge, pltpu.roll(edge, LANES - 4, 1))
        centre = full[inner]
        left = jnp.where(lane == 0, rim, pltpu.roll(centre, 1, 1))
        right = jnp.where(lane == LANES - 1, rim, pltpu.roll(centre, LANES - 1, 1))
        dx = (right - left) * 0.5
        dy = (field_ref[f, PAD + 1 : PAD + 1 + CELLS] - field_ref[f, PAD - 1 : PAD - 1 + CELLS]) * 0.5
        slopes.append((centre, dx, dy))
    (u, u_dx, u_dy), (v, v_dx, v_dy) = slopes
    grid = CELLS // SIDE
    rows = []
    for a in range(grid):
        row = jnp.zeros((1, LANES), F32)
        for e in range(grid):
            row = jnp.where(lane // SIDE == e, (mask_ref[a, e] == 1).astype(F32), row)
        rows.append(jnp.broadcast_to(row, (SIDE, LANES)))
    live = jnp.concatenate(rows, axis=0) > 0.5
    for n, x in enumerate((u, v, v_dx - u_dy, u_dy + v_dx, u_dx - v_dy)):
        base_ref[n] = jnp.where(live, x, 0.0)
    for n, x in enumerate(terms_of([base_ref[n] for n in range(BASES)])):
        term_ref[n] = x
    for n in range(TERMS):
        first = term_ref[n]
        for m in range(n, TERMS):
            product = (first * term_ref[m]).reshape(CELLS // 8, 8, LANES)
            total = jnp.sum(jnp.sum(product, axis=0), axis=0, keepdims=True)
            gram_ref[n * TERMS + m : n * TERMS + m + 1] = total
            if m > n:
                gram_ref[m * TERMS + n : m * TERMS + n + 1] = total
    sums = jnp.concatenate(three_parts(gram_ref[...]), axis=1)
    gram = dot(jnp.ones((8, 3 * LANES), BF16), sums, (((1,), (1,)), ((), ())))
    owners = out_ref.shape[0]
    out_ref[...] = jnp.zeros_like(out_ref)
    for o in range(owners):
        for half in range(2):
            out_ref[o, 40 + half : 41 + half] = gram[:1, half * LANES : (half + 1) * LANES]
    for a in range(grid):
        for e in range(grid):

            @pl.when(mask_ref[a, e] == 1)
            def _():
                owner = owner_ref[a, e]
                for n in range(BASES):
                    block = None
                    for q in range(LANES // SIDE):
                        x = base_ref[n, pl.ds(a * SIDE + q, 8, stride=4), :]
                        x = pltpu.roll(x, (q - e) % 4 * SIDE, 1) if q != e else x
                        block = x if block is None else jnp.where(lane // SIDE == q, x, block)
                    out_ref[owner, 8 * n : 8 * n + 8] = block


def terms_of(base):
    u, v, vort, strain, stretch = base
    return [u, v, vort, strain, stretch, vort * vort, vort * strain, vort * stretch, strain * strain, stretch * stretch,
            strain * stretch, u * vort, v * vort, u * strain, v * stretch, u * v]


def library_kernel(x_ref, out_ref, gram_ref):
    slots = x_ref.shape[0] // BLOCK_ROWS
    k = pl.program_id(0)
    base = [x_ref[pl.ds(8 * n + k, slots, stride=BLOCK_ROWS), :] for n in range(BASES)]
    for n, x in enumerate(terms_of(base)):
        out_ref[pl.ds(n, slots, stride=TERMS), :] = x

    @pl.when(k == 0)
    def _():
        for half in range(2):
            rows = x_ref[pl.ds(40 + half, slots, stride=BLOCK_ROWS), :]
            total = jnp.sum(rows, axis=0, keepdims=True)
            for c in range(gram_ref.shape[0]):
                gram_ref[c, half : half + 1] = total


VMEM = pl.BlockSpec(memory_space=pltpu.VMEM)
SMEM = pl.BlockSpec(memory_space=pltpu.SMEM)
PARAMS = pltpu.CompilerParams(vmem_limit_bytes=48 << 20)


def struct(*shape):
    return jax.ShapeDtypeStruct(shape, F32)


def per_device(u_velocity, v_velocity, ocean_mask, tile_owner, lower_edge_quarter_turns):
    tiles, columns = lax.axis_size("tile"), lax.axis_size("col")
    onward = lambda count: [(i, (i + 1) % count) for i in range(count)]
    back = lambda count: [((i + 1) % count, i) for i in range(count)]
    weights = jnp.asarray(column_weights())
    here = lax.axis_index("tile").astype(jnp.int32)
    turns = jnp.concatenate([lower_edge_quarter_turns, here[None]])

    above = lax.ppermute(jnp.concatenate([u_velocity[-HALO:], v_velocity[-HALO:]]), "tile", onward(tiles))
    below = lax.ppermute(jnp.concatenate([u_velocity[:HALO], v_velocity[:HALO]]), "tile", back(tiles))
    main, edge = pl.pallas_call(
        own_kernel,
        out_shape=[struct(2, FULL, LANES)] * 2,
        grid=(1,),
        in_specs=[pl.BlockSpec((POOL * CELLS, LANES), lambda i, c=c: (0, c)) for c in range(4)] * 2 + [VMEM],
        out_specs=[VMEM] * 2,
        scratch_shapes=[pltpu.VMEM((2 * POOL * CELLS, POOL * CELLS), BF16)] * 2
        + [pltpu.VMEM((2, POOL, PAD + CELLS, LANES), F32)] * 3,
        compiler_params=PARAMS,
        name="own_rows",
    )(*[u_velocity] * 4, *[v_velocity] * 4, weights)
    main, edge, to_left, to_right = pl.pallas_call(
        strip_kernel,
        out_shape=[struct(2, FULL, LANES)] * 2 + [struct(8, FULL)] * 2,
        in_specs=[SMEM] + [VMEM] * 6,
        out_specs=[VMEM] * 4,
        scratch_shapes=[pltpu.VMEM((2, 2, 4, 16, LANES), F32), pltpu.VMEM((128, POOL * CELLS), F32)],
        compiler_params=PARAMS,
        name="row_strips",
    )(turns, above, below, weights, jnp.asarray(send_selectors()), main, edge)
    from_right = lax.ppermute(to_left, "col", back(columns))
    from_left = lax.ppermute(to_right, "col", onward(columns))
    blocks = pl.pallas_call(
        base_kernel,
        out_shape=struct(tiles, BLOCK_ROWS, LANES),
        in_specs=[SMEM] * 2 + [VMEM] * 5,
        out_specs=VMEM,
        scratch_shapes=[pltpu.VMEM((2, FULL, LANES), F32), pltpu.VMEM((BASES, CELLS, LANES), F32),
                        pltpu.VMEM((TERMS, CELLS, LANES), F32), pltpu.VMEM((TERMS * TERMS, LANES), F32)],
        compiler_params=PARAMS,
        name="base_fields",
    )(ocean_mask, tile_owner, main, edge, from_left, from_right, jnp.asarray(place_matrix()))
    blocks = lax.all_to_all(blocks, "tile", split_axis=0, concat_axis=0, tiled=True)
    library, gram = pl.pallas_call(
        library_kernel,
        out_shape=[struct(tiles * TERMS, SIDE * SIDE), struct(columns, 2, LANES)],
        grid=(8,),
        in_specs=[pl.BlockSpec((tiles * BLOCK_ROWS, LANES), lambda k: (0, 0))],
        out_specs=[pl.BlockSpec((tiles * TERMS, LANES), lambda k: (0, k)),
                   pl.BlockSpec((columns, 2, LANES), lambda k: (0, 0, 0))],
        compiler_params=PARAMS,
        name="library_terms",
    )(blocks.reshape(tiles * BLOCK_ROWS, LANES))
    gram = lax.all_to_all(gram, "col", split_axis=0, concat_axis=0, tiled=True)
    gram = jnp.sum(gram, axis=0).reshape(TERMS, TERMS) / (CELLS * CELLS)
    return library.reshape(1, 1, tiles, TERMS, SIDE * SIDE), gram


def solution(mesh):
    in_specs = (P("tile", "col"), P("tile", "col"), P("tile", "col"), P("tile", "col"), P())
    out_specs = (P("tile", "col", None, None, None), P())
    return jax.shard_map(
        per_device, mesh=mesh, in_specs=in_specs, out_specs=out_specs, check_vma=False
    )
```

time: 381 us -> 59.1 us (0.16); the launches traced: 373 us -> 58.9 us
  local copies, waits for them, and re-layouts: 89.5 us -> 5.29 us
  other arithmetic: 81.8 us -> 0.77 us
  starting transfers between devices: 88.9 us -> 10.5 us
  blocking collectives: 78 us -> 26.2 us
  waiting for transfers between devices: 28.3 us -> 2.67 us
  Pallas kernels: 0 us -> 12.7 us
  between operations: 5.21 us -> 0.73 us
    ppermute x36 -> x4, starting transfers between devices: 88.9 us -> 10.5 us  [the longest x1 4.01 us: per_device(): from_left = lax.ppermute(to_right, 'col', onward(columns))]
    reshape x2 -> x0, local copies, waits for them, and re-layouts: 72.1 us -> none  [the longest x1 71.4 us: per_device(): field.reshape(2, fine_rows // 4, 4, fine_cols // 4, 4).mean(axis=(2, 4))]
    psum x1 -> x0, blocking collectives: 64 us -> none  [per_device(): gram = lax.psum(part, ('tile', 'col')) / (fine_rows // 4 * (fine_cols // 4))]
    add x25 -> x0, other arithmetic: 45.3 us -> none  [the longest x8 45.1 us: relax(): return centre + KAPPA * (beside_all - 4.0 * centre)]
    ppermute x36 -> x4, waiting for transfers between devices: 28.3 us -> 2.67 us  [the longest x1 1.6 us: per_device(): from_left = lax.ppermute(to_right, 'col', onward(columns))]
    reduce_sum x2 -> x1, other arithmetic: 21 us -> 0.02 us  [per_device(): gram = jnp.sum(gram, axis=0).reshape(TERMS, TERMS) / (CELLS * CELLS)]
    pallas_call x0 -> x4, Pallas kernels: none -> 12.7 us  [the longest x1 4.88 us: per_device(): pl.pallas_call(own_kernel, out_shape=[struct(2, FULL, LANES)] * 2, grid=(...]
    all_to_all x1 -> x2, blocking collectives: 14.1 us -> 26.2 us  [the longest x1 13.7 us: per_device(): gram = lax.all_to_all(gram, 'col', split_axis=0, concat_axis=0, tiled=True)]
  transfers between devices with their start and end apart: 36 -> 4, of which waited for: 24 -> 2; matrix products, arithmetic and copies ran while one was open for 1% -> 1% of each run, Pallas kernels for 0% -> 8%
where the time goes in v1:
time: 59.1 us; the launch traced here: 58.9 us
  blocking collectives  26.2 us (44%)
  Pallas kernels  12.7 us (21%)
  starting transfers between devices  10.5 us (18%)
  local copies, waits for them, and re-layouts  5.29 us (9%)
  waiting for transfers between devices  2.67 us (5%)
  other arithmetic  0.77 us (1%)
  between operations  0.73 us (1%)
    all_to_all x1, blocking collectives, per_device(): gram = lax.all_to_all(gram, 'col', split_axis=0, concat_axis=0, tiled=True)  13.7 us
    all_to_all x1, blocking collectives, per_device(): lax.all_to_all(blocks, 'tile', split_axis=0, concat_axis=0, tiled=True)  12.5 us
    pallas_call x1, Pallas kernels, per_device(): pl.pallas_call(own_kernel, out_shape=[struct(2, FULL, LANES)] * 2, grid=(...  4.88 us
    ppermute x1, starting transfers between devices, per_device(): from_left = lax.ppermute(to_right, 'col', onward(columns))  4.01 us
    ppermute x1, starting transfers between devices, per_device(): lax.ppermute(jnp.concatenate([u_velocity[:HALO], v_velocity[:HALO]]), 'ti...  3.9 us
    unnamed x14, local copies, waits for them, and re-layouts  3.79 us
    pallas_call x1, Pallas kernels, per_device(): pl.pallas_call(library_kernel, out_shape=[struct(tiles * TERMS, SIDE * SI...  2.88 us
    pallas_call x1, Pallas kernels, per_device(): pl.pallas_call(base_kernel, out_shape=struct(tiles, BLOCK_ROWS, LANES), i...  2.77 us
  transfers between devices with their start and end apart: 4, of which 2 were waited for; matrix products, arithmetic and copies ran while one was open for 1% of the time, Pallas kernels for 8%

profile of v1, /device:TPU:0, one launch (start us, length us, event | category | flops | bytes accessed | tf_op | source)
XLA Modules:
  0.0 58.9 jit_solution(274525580809202653)
XLA Ops:
  0.6 0.8 %fusion = (f32[12,512]{1,0:T(8,128)S(1)}, f32[12,512]{1,0:T(8,128)S(1)}, f32[12,512]{1,0:T(8,128)S(1)}, f32[12,512]{1,0:T(8,128)S(1)}) fusion(f32[512,512]{1,0:T(8,128)} %refs_3_.1, f32[512,512]{1,0:T(8,128)} %refs_7_.1), kind=kLoop, calls=%fused_computation.4 | loop fusion | bytes 196608 | tf_op jit(solution)/shard_map/slice | solution.py:310
  1.5 0.1 collective-permute-start
  1.6 3.9 %collective-permute-start.1 = (f32[24,512]{1,0:T(8,128)S(1)}, f32[24,512]{1,0:T(8,128)S(1)}, u32[]{:S(2)}, u32[]{:S(2)}) collective-permute-start(f32[24,512]{1,0:T(8,128)S(1)} %pad_maximum_fusion.1), channel_id=1, source_target_pairs={{8,0},{16,8},{24,16},{32,24},{40,32},{48,40},{56,48},{64,56},{72,6... | collective-permute-start | bytes 147464 | tf_op jit(solution)/shard_map/ppermute | solution.py:310
  5.5 0.7 %pad_add_fusion.turns_ref = s32[17]{0:T(128)S(1)} fusion(s32[1]{0:T(128)} %bitcast, s32[16]{0:T(128)} %param.12), kind=kLoop, calls=%fused_computation.2 | loop fusion | flops 17 | bytes 136 | tf_op jit(solution)/shard_map/concatenate | solution.py:307
  6.2 0.0 copy-start
  6.2 1.2 %copy-done = f32[512,512]{1,0:T(8,128)S(1)} copy-done((f32[512,512]{1,0:T(8,128)S(1)}, f32[512,512]{1,0:T(8,128)}, u32[]{:S(2)}) %copy-start) | copy-done | bytes 1048600
  7.4 0.0 copy-start.1
  7.4 1.2 %copy-done.1 = f32[512,512]{1,0:T(8,128)S(1)} copy-done((f32[512,512]{1,0:T(8,128)S(1)}, f32[512,512]{1,0:T(8,128)}, u32[]{:S(2)}) %copy-start.1) | copy-done | bytes 1048600
  8.7 0.0 copy-start.2
  8.7 1.3 %copy-done.2 = bf16[512,1280]{1,0:T(8,128)(2,1)S(1)} copy-done((bf16[512,1280]{1,0:T(8,128)(2,1)S(1)}, bf16[512,1280]{1,0:T(8,128)(2,1)}, u32[]{:S(2)}) %copy-start.2) | copy-done | bytes 1310744
  10.0 0.0 copy-start.3
  10.0 4.9 %own_rows.1 = (f32[2,144,128]{2,1,0:T(8,128)S(1)}, f32[2,144,128]{2,1,0:T(8,128)S(1)}) custom-call(f32[512,512]{1,0:T(8,128)S(1)} %copy-done, f32[512,512]{1,0:T(8,128)S(1)} %copy-done, f32[512,512]{1,0:T(8,128)S(1)} %copy-done, f32[512,512]{1,0:T(8,128)S(1)} %copy-done, f32[512,512]{1,0:T(8,128)S(1)} %copy-done.1, f32[512,512]{1,0:T(8,128)S(1)} %copy-done.1, ...), custom_call_target="tpu_custom_call" | custom-call | tf_op jit(solution)/shard_map/own_rows/pallas_call | solution.py:311
  14.9 0.0 copy-start.4
  14.9 0.0 copy-start.5
  14.9 0.0 copy-start.6
  14.9 0.0 collective-permute-done.above_ref
  14.9 0.0 collective-permute-done.1.below_ref
  14.9 0.0 copy-done.3
  14.9 2.2 %row_strips.1 = (f32[2,144,128]{2,1,0:T(8,128)S(1)}, f32[2,144,128]{2,1,0:T(8,128)S(1)}, f32[8,144]{1,0:T(8,128)S(1)}, f32[8,144]{1,0:T(8,128)S(1)}) custom-call(s32[17]{0:T(128)S(1)} %pad_add_fusion.turns_ref, f32[24,512]{1,0:T(8,128)S(1)} %collective-permute-done.above_ref, f32[24,512]{1,0:T(8,128)S(1)} %collective-permute-done.1.below_ref, ...), custom_call_target="tpu_custom_call" | custom-call | tf_op jit(solution)/shard_map/row_strips/pallas_call | solution.py:322
  17.1 4.0 %collective-permute-start.2 = (f32[8,144]{1,0:T(8,128)S(1)}, f32[8,144]{1,0:T(8,128)S(1)}, u32[]{:S(2)}, u32[]{:S(2)}) collective-permute-start(f32[8,144]{1,0:T(8,128)S(1)} %get-tuple-element.14), channel_id=1, source_target_pairs={{0,1},{1,2},{2,3},{3,4},{4,5},{5,6},{6,7},{7,0},{8,9},{9,10},{10,1... | collective-permute-start | bytes 13832 | tf_op jit(solution)/shard_map/ppermute | solution.py:332
  21.1 2.5 %collective-permute-start.3 = (f32[8,144]{1,0:T(8,128)S(1)}, f32[8,144]{1,0:T(8,128)S(1)}, u32[]{:S(2)}, u32[]{:S(2)}) collective-permute-start(f32[8,144]{1,0:T(8,128)S(1)} %get-tuple-element.15), channel_id=1, source_target_pairs={{1,0},{2,1},{3,2},{4,3},{5,4},{6,5},{7,6},{0,7},{9,8},{10,9},{11,1... | collective-permute-start | bytes 13832 | tf_op jit(solution)/shard_map/ppermute | solution.py:331
  23.6 1.6 %collective-permute-done.2.from_left_ref = f32[8,144]{1,0:T(8,128)S(1)} collective-permute-done((f32[8,144]{1,0:T(8,128)S(1)}, f32[8,144]{1,0:T(8,128)S(1)}, u32[]{:S(2)}, u32[]{:S(2)}) %collective-permute-start.2) | collective-permute-done | bytes 4640 | tf_op jit(solution)/shard_map/ppermute | solution.py:332
  25.2 1.1 %collective-permute-done.3.from_right_ref = f32[8,144]{1,0:T(8,128)S(1)} collective-permute-done((f32[8,144]{1,0:T(8,128)S(1)}, f32[8,144]{1,0:T(8,128)S(1)}, u32[]{:S(2)}, u32[]{:S(2)}) %collective-permute-start.3) | collective-permute-done | bytes 4640 | tf_op jit(solution)/shard_map/ppermute | solution.py:331
  26.3 0.0 copy-done.4
  26.3 0.0 copy-done.5
  26.3 0.0 copy-done.6
  26.3 2.8 %base_fields.1 = f32[16,48,128]{2,1,0:T(8,128)S(1)} custom-call(s32[4,4]{1,0:T(4,128)S(1)} %copy-done.5, s32[4,4]{1,0:T(4,128)S(1)} %copy-done.6, f32[2,144,128]{2,1,0:T(8,128)S(1)} %get-tuple-element.12.main_ref, f32[2,144,128]{2,1,0:T(8,128)S(1)} %get-tuple-element.13.edge_ref, f32[8,144]{1,0:T(8,128)S(1)} %collective-permute-done.2.from_left_ref, ...), custom_call_target="tpu_custom_call" | custom-call | tf_op jit(solution)/shard_map/base_fields/pallas_call | solution.py:333
  29.1 12.5 %all_to_all.10 = f32[16,48,128]{2,1,0:T(8,128)S(1)} all-to-all(f32[16,48,128]{2,1,0:T(8,128)S(1)} %base_fields.1), channel_id=1, replica_groups=mesh['tile'=16,'col'=8] {'tile'}, dimensions={0} | all-to-all | bytes 786432 | tf_op jit(solution)/shard_map/all_to_all | solution.py:343
  41.6 2.9 %library_terms.1 = (f32[256,1024]{1,0:T(8,128)}, f32[8,2,128]{2,1,0:T(2,128)S(1)}) custom-call(f32[768,128]{1,0:T(8,128)S(1)} %bitcast.3), custom_call_target="tpu_custom_call" | custom-call | tf_op jit(solution)/shard_map/library_terms/pallas_call | solution.py:344
  44.5 13.7 %all_to_all.11 = f32[8,2,128]{2,1,0:T(2,128)S(1)} all-to-all(f32[8,2,128]{2,1,0:T(2,128)S(1)} %get-tuple-element.17), channel_id=1, replica_groups=mesh['tile'=16,'col'=8] {'col'}, dimensions={0} | all-to-all | bytes 16384 | tf_op jit(solution)/shard_map/all_to_all | solution.py:354
  58.2 0.7 %div.10 = f32[16,16]{1,0:T(8,128)} reshape(f32[2,128]{1,0:T(2,128)S(1)} %broadcast_multiply_fusion) | data formatting | bytes 2048 | tf_op jit(solution)/shard_map/div | solution.py:355
  (4 shorter events, 0.0 us)
Async XLA Ops:
  1.5 13.4 %collective-permute-start = (f32[24,512]{1,0:T(8,128)S(1)}, f32[24,512]{1,0:T(8,128)S(1)}, u32[]{:S(2)}, u32[]{:S(2)}) collective-permute-start(f32[24,512]{1,0:T(8,128)S(1)} %pad_maximum_fusion), channel_id=1, source_target_pairs={{0,8},{8,16},{16,24},{24,32},{32,40},{40,48},{48,56},{56,64},{64,7... | collective-permute-start | bytes 147464 | tf_op jit(solution)/shard_map/ppermute | solution.py:309
  1.6 13.3 %collective-permute-start.1 = (f32[24,512]{1,0:T(8,128)S(1)}, f32[24,512]{1,0:T(8,128)S(1)}, u32[]{:S(2)}, u32[]{:S(2)}) collective-permute-start(f32[24,512]{1,0:T(8,128)S(1)} %pad_maximum_fusion.1), channel_id=1, source_target_pairs={{8,0},{16,8},{24,16},{32,24},{40,32},{48,40},{56,48},{64,56},{72,6... | collective-permute-start | bytes 147464 | tf_op jit(solution)/shard_map/ppermute | solution.py:310
  6.2 1.2 %copy-start = (f32[512,512]{1,0:T(8,128)S(1)}, f32[512,512]{1,0:T(8,128)}, u32[]{:S(2)}) copy-start(f32[512,512]{1,0:T(8,128)} %refs_3_.1) | copy-start | bytes 3145732
  7.4 1.2 %copy-start.1 = (f32[512,512]{1,0:T(8,128)S(1)}, f32[512,512]{1,0:T(8,128)}, u32[]{:S(2)}) copy-start(f32[512,512]{1,0:T(8,128)} %refs_7_.1) | copy-start | bytes 3145732
  8.7 1.3 %copy-start.2 = (bf16[512,1280]{1,0:T(8,128)(2,1)S(1)}, bf16[512,1280]{1,0:T(8,128)(2,1)}, u32[]{:S(2)}) copy-start(bf16[512,1280]{1,0:T(8,128)(2,1)} %constant.17.clone.refs_8_.w_ref) | copy-start | bytes 3932164
  10.0 5.0 %copy-start.3 = (bf16[2,16,768]{2,1,0:T(8,128)(2,1)S(1)}, bf16[2,16,768]{2,1,0:T(8,128)(2,1)}, u32[]{:S(2)}) copy-start(bf16[2,16,768]{2,1,0:T(8,128)(2,1)} %constant.18.clone.sel_ref) | copy-start | bytes 147460
  14.9 11.4 %copy-start.4 = (bf16[48,512]{1,0:T(8,128)(2,1)S(1)}, bf16[48,512]{1,0:T(8,128)(2,1)}, u32[]{:S(2)}) copy-start(bf16[48,512]{1,0:T(8,128)(2,1)} %constant.19.clone.place_ref) | copy-start | bytes 147460
  14.9 11.4 %copy-start.5 = (s32[4,4]{1,0:T(4,128)S(1)}, s32[4,4]{1,0:T(4,128)}, u32[]{:S(2)}) copy-start(s32[4,4]{1,0:T(4,128)} %mask_ref.1) | copy-start | bytes 196
  14.9 11.4 %copy-start.6 = (s32[4,4]{1,0:T(4,128)S(1)}, s32[4,4]{1,0:T(4,128)}, u32[]{:S(2)}) copy-start(s32[4,4]{1,0:T(4,128)} %owner_ref.1) | copy-start | bytes 196
  17.1 8.1 %collective-permute-start.2 = (f32[8,144]{1,0:T(8,128)S(1)}, f32[8,144]{1,0:T(8,128)S(1)}, u32[]{:S(2)}, u32[]{:S(2)}) collective-permute-start(f32[8,144]{1,0:T(8,128)S(1)} %get-tuple-element.14), channel_id=1, source_target_pairs={{0,1},{1,2},{2,3},{3,4},{4,5},{5,6},{6,7},{7,0},{8,9},{9,10},{10,1... | collective-permute-start | bytes 13832 | tf_op jit(solution)/shard_map/ppermute | solution.py:332
  21.1 5.2 %collective-permute-start.3 = (f32[8,144]{1,0:T(8,128)S(1)}, f32[8,144]{1,0:T(8,128)S(1)}, u32[]{:S(2)}, u32[]{:S(2)}) collective-permute-start(f32[8,144]{1,0:T(8,128)S(1)} %get-tuple-element.15), channel_id=1, source_target_pairs={{1,0},{2,1},{3,2},{4,3},{5,4},{6,5},{7,6},{0,7},{9,8},{10,9},{11,1... | collective-permute-start | bytes 13832 | tf_op jit(solution)/shard_map/ppermute | solution.py:331

commit v2 on v1

--- a/solution.py
+++ b/solution.py
@@ -24,7 +24,9 @@
 F32 = jnp.float32
 BF16 = jnp.bfloat16
 
-EDGE_COLS = (-1, -2, CELLS + 1, CELLS)
+HALF = CELLS // 2
+EDGE_COLS = (HALF, HALF + 1, -2, -1)
+EDGE_LANE = {CELLS: 0, CELLS + 1: 1, -2: HALF + 2, -1: HALF + 3}
 SCALE = KAPPA**PASSES / (POOL * POOL)
 
 
@@ -38,16 +40,18 @@
 
 
 def column_weights():
-    fine = CELLS * POOL
-    weights = np.zeros((fine, 10 * LANES), np.float32)
+    fine = HALF * POOL
+    weights = np.zeros((fine, 5 * LANES), np.float32)
+
+    def fill(column, j, coarse):
+        for f in range(max(0, POOL * coarse - PASSES), min(fine, POOL * coarse + POOL + PASSES)):
+            weights[f, column] = math.comb(PASSES, j) * across(PASSES - j, f, coarse)
+
     for j in range(PASSES + 1):
-        block = PASSES - j
-        for coarse in range(CELLS):
-            for f in range(max(0, POOL * coarse - 8), min(fine, POOL * coarse + 12)):
-                weights[f, block * LANES + coarse] = math.comb(PASSES, j) * across(PASSES - j, f, coarse)
+        for coarse in range(HALF):
+            fill((PASSES - j) * HALF + coarse, j, coarse)
         for place, coarse in enumerate(EDGE_COLS):
-            for f in range(max(0, POOL * coarse - 8), min(fine, POOL * coarse + 12)):
-                weights[f, 9 * LANES + 4 * j + place] = math.comb(PASSES, j) * across(PASSES - j, f, coarse)
+            fill(9 * HALF + 4 * j + place, j, coarse)
     out = weights.astype(ml_dtypes.bfloat16)
     assert (out.astype(np.float32) == weights).all()
     return out
@@ -55,7 +59,8 @@
 
 def send_selectors():
     sel = np.zeros((2, 16, 6 * LANES), np.float32)
-    spots = ((0, 1, 1), (1, 1, 0), (2, 0, 0), (8, 0, CELLS - 1), (9, 1, 3), (10, 1, 2))
+    spots = ((0, 1, EDGE_LANE[-2]), (1, 1, EDGE_LANE[-1]), (2, 0, 0),
+             (8, 0, CELLS - 1), (9, 1, EDGE_LANE[CELLS]), (10, 1, EDGE_LANE[CELLS + 1]))
     for f in range(2):
         for row, source, lane in spots:
             for piece in range(3):
@@ -105,47 +110,96 @@
     return [left + up, t[0] + middle, middle + t[3], right + down]
 
 
-def own_kernel(*refs):
-    w_ref, main_ref, edge_ref, high_ref, low_ref, sum_ref, first_ref, last_ref = refs[8:]
+def halves(z, rows, tile):
+    cut = slice(tile * LANES, (tile + 1) * LANES)
+    low_lanes = lax.broadcasted_iota(jnp.int32, (1, LANES), 1) < HALF
+    first, second = z[:rows, cut], z[rows:, cut]
+    turned = pltpu.roll(second, HALF, 1)
+    return jnp.where(low_lanes, first, turned), (first, second, turned, low_lanes)
+
+
+def other_half(parts):
+    first, second, _, low_lanes = parts
+    return jnp.where(low_lanes, pltpu.roll(first, HALF, 1), second)
+
+
+def edge_half(parts):
+    first, _, turned, low_lanes = parts
+    return jnp.where(low_lanes, turned, first)
+
+
+def join(main, edge):
+    lane = lax.broadcasted_iota(jnp.int32, (1, LANES), 1)
+    main = main + jnp.where((lane == HALF) | (lane == HALF + 1), edge, 0.0)
+    return main + jnp.where((lane == HALF - 1) | (lane == HALF - 2), pltpu.roll(edge, HALF - 4, 1), 0.0)
+
+
+def own_kernel(u_hbm, v_hbm, w_hbm, main_ref, edge_ref, x_ref, w_ref, parts_ref, sum_ref, first_ref, last_ref, x_sem,
+               w_sem):
+    fine = HALF * POOL
+    x_copies = [[pltpu.make_async_copy(hbm.at[:, pl.ds(c * LANES, LANES)], x_ref.at[f, c], x_sem.at[f, c])
+                 for c in range(4)] for f, hbm in enumerate((u_hbm, v_hbm))]
+    w_copies = [pltpu.make_async_copy(w_hbm, w_ref.at[pl.ds(part * fine, fine)], w_sem.at[part]) for part in range(2)]
+    for copy in (*x_copies[0], *x_copies[1], *w_copies):
+        copy.start()
+    rows = 2 * POOL * CELLS
     for f in range(2):
         for c in range(4):
+            x_copies[f][c].wait()
             for p in range(POOL):
-                high, low = two_parts(refs[4 * f + c][pl.ds(p, CELLS, stride=POOL), :])
-                spot = pl.ds((f * POOL + p) * CELLS, CELLS)
-                high_ref[spot, c * LANES : (c + 1) * LANES] = high
-                low_ref[spot, c * LANES : (c + 1) * LANES] = low
-    for t in range(5):
-        w = w_ref[:, 2 * t * LANES : 2 * (t + 1) * LANES]
-        z = dot(high_ref[...], w) + dot(low_ref[...], w)
-        for half in range(2):
-            part = z[:, half * LANES : (half + 1) * LANES]
-            stage = 2 * t + half
-            for f in range(2):
-                for_phase = [part[(f * POOL + p) * CELLS : (f * POOL + p + 1) * CELLS] for p in range(POOL)]
-                if stage in (0, 9):
-                    into = (sum_ref if stage == 0 else first_ref).at[f]
-                    for p in range(POOL):
-                        into[p, :PAD] = jnp.zeros((PAD, LANES), F32)
-                        into[p, PAD:] = for_phase[p]
-                else:
-                    new = three_rows([sum_ref[f, p] for p in range(POOL)])
-                    for p in range(POOL):
-                        sum_ref[f, p, :PAD] = new[p][:PAD]
-                        sum_ref[f, p, PAD:] = new[p][PAD:] + for_phase[p]
+                high, low = two_parts(x_ref[f, c, pl.ds(p, CELLS, stride=POOL), :])
+                spot = pl.ds(c // 2 * rows + (f * POOL + p) * CELLS, CELLS)
+                lane = c % 2 * LANES
+                parts_ref[spot, lane : lane + LANES] = high
+                parts_ref[spot, fine + lane : fine + lane + LANES] = low
+    for copy in w_copies:
+        copy.wait()
+    for f in range(2):
+        for p in range(POOL):
+            sum_ref[f, p, :PAD] = jnp.zeros((PAD, LANES), F32)
+            first_ref[f, p, :PAD] = jnp.zeros((PAD, LANES), F32)
+
+    def step(part):
+        for f in range(2):
+            new = three_rows([sum_ref[f, p] for p in range(POOL)])
+            for p in range(POOL):
+                block = (f * POOL + p) * CELLS
+                sum_ref[f, p, :PAD] = new[p][:PAD]
+                sum_ref[f, p, PAD:] = new[p][PAD:] + part[block : block + CELLS]
+
+    def store(to_ref, part):
+        for f in range(2):
+            for p in range(POOL):
+                block = (f * POOL + p) * CELLS
+                to_ref[f, p, PAD:] = part[block : block + CELLS]
+
+    for start in (0, 2, 4):
+        wide = min(2, 5 - start)
+        z = dot(parts_ref[...], w_ref[:, start * LANES : (start + wide) * LANES])
+        for tile in range(wide):
+            part, both = halves(z, rows, tile)
+            if start + tile == 0:
+                store(sum_ref, part)
+            else:
+                step(part)
+            if start + tile < 4:
+                step(other_half(both))
+            else:
+                store(first_ref, edge_half(both))
     for f in range(2):
         for p in range(POOL):
             last_ref[f, p] = first_ref[f, p]
 
     @pl.loop(0, PASSES)
-    def _(step):
+    def _(count):
         for f in range(2):
             new = three_rows([pltpu.roll(last_ref[f, p], LANES - 4, 1) for p in range(POOL)])
             for p in range(POOL):
                 last_ref[f, p] = new[p] + first_ref[f, p]
 
     for f in range(2):
-        for from_ref, to_ref in ((sum_ref, main_ref), (last_ref, edge_ref)):
-            pooled = ((from_ref[f, 0] + from_ref[f, 1]) + (from_ref[f, 2] + from_ref[f, 3])) * SCALE
+        main, edge = [((x[f, 0] + x[f, 1]) + (x[f, 2] + x[f, 3])) * SCALE for x in (sum_ref, last_ref)]
+        for to_ref, pooled in ((main_ref, join(main, edge)), (edge_ref, edge)):
             to_ref[f, : PAD + CELLS] = pooled
             to_ref[f, PAD + CELLS :] = pooled[:PAD]
 
@@ -156,10 +210,10 @@
     return cosine * first - sine * second, sine * first + cosine * second
 
 
-def strip_kernel(turns_ref, above_ref, below_ref, w_ref, sel_ref, main_in, edge_in, main_ref, edge_ref, left_ref,
+def strip_kernel(here_ref, turns_ref, above_ref, below_ref, w_ref, sel_ref, main_in, edge_in, main_ref, edge_ref, left_ref,
                  right_ref, rows_ref, strip_ref):
-    tiles = turns_ref.shape[0] - 1
-    here = turns_ref[tiles]
+    tiles = turns_ref.shape[0]
+    here = here_ref[0]
     k_top = turns_ref[here]
     k_bottom = lax.rem(4 - turns_ref[lax.rem(here + 1, tiles)], 4)
     strip_ref[...] = jnp.zeros_like(strip_ref)
@@ -167,36 +221,31 @@
         turned = turn(x_ref[:HALO], x_ref[HALO:], k)
         for f in range(2):
             for c in range(4):
-                cut = slice(c * LANES, (c + 1) * LANES)
-                rows_ref[s, f, c, :HALO] = turned[f][:, cut]
+                rows_ref[s, f, c, :HALO] = turned[f][:, c * LANES : (c + 1) * LANES]
+                cut = slice(c % 2 * LANES, (c % 2 + 1) * LANES)
                 for p in range(POOL):
-                    spot = ((f * 2 + s) * POOL + p) * 8 + start
+                    spot = c // 2 * 128 + ((f * 2 + s) * POOL + p) * 8 + start
                     strip_ref[spot : spot + 3, cut] = rows_ref[s, f, c, pl.ds(p, 3, stride=POOL), :]
-    high, low = two_parts(strip_ref[...])
+    parts = jnp.concatenate(two_parts(strip_ref[...]), axis=1)
     main_ref[...] = main_in[...]
     edge_ref[...] = edge_in[...]
-    sums = [None] * 4
-    for t in range(5):
-        w = w_ref[:, 2 * t * LANES : 2 * (t + 1) * LANES]
-        z = dot(high, w) + dot(low, w)
-        for half in range(2):
-            part = z[:, half * LANES : (half + 1) * LANES]
-            stage = 2 * t + half
-            for g in range(4):
-                own = [part[(g * POOL + p) * 8 : (g * POOL + p + 1) * 8] for p in range(POOL)]
-                if stage == 0:
-                    sums[g] = own
-                elif stage < 9:
-                    sums[g] = [a + b for a, b in zip(three_rows(sums[g]), own)]
-                else:
-                    last = own
-                    for _ in range(PASSES):
-                        last = [a + b for a, b in zip(three_rows([pltpu.roll(x, LANES - 4, 1) for x in last]), own)]
-                    f, s = g // 2, g % 2
-                    spot, cut = ((7, 3), (PAD + CELLS - 2, 2))[s]
-                    for to_ref, x in ((main_ref, sums[g]), (edge_ref, last)):
-                        pooled = ((x[0] + x[1]) + (x[2] + x[3])) * SCALE
-                        to_ref[f, spot : spot + 3] = to_ref[f, spot : spot + 3] + pooled[cut : cut + 3]
+    w = jnp.concatenate([w_ref[...]] * 2, axis=0)
+    z = dot(parts, w)
+    own = []
+    for tile in range(5):
+        part, both = halves(z, 128, tile)
+        own += [part, other_half(both) if tile < 4 else edge_half(both)]
+    for g in range(4):
+        f, s = g // 2, g % 2
+        cut = [[x[(g * POOL + p) * 8 : (g * POOL + p + 1) * 8] for p in range(POOL)] for x in own]
+        total, last = cut[0], cut[9]
+        for stage in range(1, 9):
+            total = [a + b for a, b in zip(three_rows(total), cut[stage])]
+            last = [a + b for a, b in zip(three_rows([pltpu.roll(x, LANES - 4, 1) for x in last]), cut[9])]
+        main, edge = [((x[0] + x[1]) + (x[2] + x[3])) * SCALE for x in (total, last)]
+        spot, start = ((7, 3), (PAD + CELLS - 2, 2))[s]
+        for to_ref, x in ((main_ref, join(main, edge)), (edge_ref, edge)):
+            to_ref[f, spot : spot + 3] = to_ref[f, spot : spot + 3] + x[start : start + 3]
     out = jnp.zeros((16, FULL), F32)
     for f in range(2):
         parts = jnp.concatenate(three_parts(main_ref[f]) + three_parts(edge_ref[f]), axis=1)
@@ -217,7 +266,8 @@
         field_ref[f] = full
         edge = edge_ref[f, inner]
         rim = placed[inner, (2 * f + 1) * LANES : (2 * f + 2) * LANES]
-        rim = rim + jnp.where(lane == 0, edge, pltpu.roll(edge, LANES - 4, 1))
+        to_first, to_last = LANES - EDGE_LANE[-1], LANES - 1 - EDGE_LANE[CELLS]
+        rim = rim + jnp.where(lane == 0, pltpu.roll(edge, to_first, 1), pltpu.roll(edge, to_last, 1))
         centre = full[inner]
         left = jnp.where(lane == 0, rim, pltpu.roll(centre, 1, 1))
         right = jnp.where(lane == LANES - 1, rim, pltpu.roll(centre, LANES - 1, 1))
@@ -273,23 +323,27 @@
             strain * stretch, u * vort, v * vort, u * strain, v * stretch, u * v]
 
 
-def library_kernel(x_ref, out_ref, gram_ref):
+def library_kernel(x_ref, out_hbm, gram_ref, out_ref, sem):
     slots = x_ref.shape[0] // BLOCK_ROWS
-    k = pl.program_id(0)
-    base = [x_ref[pl.ds(8 * n + k, slots, stride=BLOCK_ROWS), :] for n in range(BASES)]
-    for n, x in enumerate(terms_of(base)):
-        out_ref[pl.ds(n, slots, stride=TERMS), :] = x
-
-    @pl.when(k == 0)
-    def _():
-        for half in range(2):
-            rows = x_ref[pl.ds(40 + half, slots, stride=BLOCK_ROWS), :]
-            total = jnp.sum(rows, axis=0, keepdims=True)
-            for c in range(gram_ref.shape[0]):
-                gram_ref[c, half : half + 1] = total
+    copies = []
+    for k in range(8):
+        base = [x_ref[pl.ds(8 * n + k, slots, stride=BLOCK_ROWS), :] for n in range(BASES)]
+        for n, x in enumerate(terms_of(base)):
+            out_ref[k, pl.ds(n, slots, stride=TERMS), :] = x
+        copies.append(pltpu.make_async_copy(out_ref.at[k], out_hbm.at[:, pl.ds(k * LANES, LANES)], sem.at[k]))
+        copies[k].start()
+    totals = [jnp.sum(x_ref[pl.ds(40 + half, slots, stride=BLOCK_ROWS), :], axis=0, keepdims=True) for half in range(2)]
+    for n in range(TERMS):
+        row = totals[n // 8]
+        row = pltpu.roll(row, LANES - n % 8 * TERMS, 1) if n % 8 else row
+        for c in range(gram_ref.shape[0]):
+            gram_ref[c, n : n + 1] = row
+    for copy in copies:
+        copy.wait()
 
 
 VMEM = pl.BlockSpec(memory_space=pltpu.VMEM)
+HBM = pl.BlockSpec(memory_space=pltpu.HBM)
 SMEM = pl.BlockSpec(memory_space=pltpu.SMEM)
 PARAMS = pltpu.CompilerParams(vmem_limit_bytes=48 << 20)
 
@@ -303,31 +357,31 @@
     onward = lambda count: [(i, (i + 1) % count) for i in range(count)]
     back = lambda count: [((i + 1) % count, i) for i in range(count)]
     weights = jnp.asarray(column_weights())
-    here = lax.axis_index("tile").astype(jnp.int32)
-    turns = jnp.concatenate([lower_edge_quarter_turns, here[None]])
+    here = lax.axis_index("tile").astype(jnp.int32)[None]
 
     above = lax.ppermute(jnp.concatenate([u_velocity[-HALO:], v_velocity[-HALO:]]), "tile", onward(tiles))
     below = lax.ppermute(jnp.concatenate([u_velocity[:HALO], v_velocity[:HALO]]), "tile", back(tiles))
     main, edge = pl.pallas_call(
         own_kernel,
         out_shape=[struct(2, FULL, LANES)] * 2,
-        grid=(1,),
-        in_specs=[pl.BlockSpec((POOL * CELLS, LANES), lambda i, c=c: (0, c)) for c in range(4)] * 2 + [VMEM],
+        in_specs=[HBM] * 3,
         out_specs=[VMEM] * 2,
-        scratch_shapes=[pltpu.VMEM((2 * POOL * CELLS, POOL * CELLS), BF16)] * 2
-        + [pltpu.VMEM((2, POOL, PAD + CELLS, LANES), F32)] * 3,
+        scratch_shapes=[pltpu.VMEM((2, 4, POOL * CELLS, LANES), F32), pltpu.VMEM((POOL * CELLS, 5 * LANES), BF16),
+                        pltpu.VMEM((4 * POOL * CELLS, POOL * CELLS), BF16)]
+        + [pltpu.VMEM((2, POOL, PAD + CELLS, LANES), F32)] * 3
+        + [pltpu.SemaphoreType.DMA((2, 4)), pltpu.SemaphoreType.DMA((2,))],
         compiler_params=PARAMS,
         name="own_rows",
-    )(*[u_velocity] * 4, *[v_velocity] * 4, weights)
+    )(*[pltpu.with_memory_space_constraint(x, pltpu.HBM) for x in (u_velocity, v_velocity, weights)])
     main, edge, to_left, to_right = pl.pallas_call(
         strip_kernel,
         out_shape=[struct(2, FULL, LANES)] * 2 + [struct(8, FULL)] * 2,
-        in_specs=[SMEM] + [VMEM] * 6,
+        in_specs=[SMEM] * 2 + [VMEM] * 6,
         out_specs=[VMEM] * 4,
-        scratch_shapes=[pltpu.VMEM((2, 2, 4, 16, LANES), F32), pltpu.VMEM((128, POOL * CELLS), F32)],
+        scratch_shapes=[pltpu.VMEM((2, 2, 4, 16, LANES), F32), pltpu.VMEM((256, 2 * LANES), F32)],
         compiler_params=PARAMS,
         name="row_strips",
-    )(turns, above, below, weights, jnp.asarray(send_selectors()), main, edge)
+    )(here, lower_edge_quarter_turns, above, below, weights, jnp.asarray(send_selectors()), main, edge)
     from_right = lax.ppermute(to_left, "col", back(columns))
     from_left = lax.ppermute(to_right, "col", onward(columns))
     blocks = pl.pallas_call(
@@ -343,16 +397,15 @@
     blocks = lax.all_to_all(blocks, "tile", split_axis=0, concat_axis=0, tiled=True)
     library, gram = pl.pallas_call(
         library_kernel,
-        out_shape=[struct(tiles * TERMS, SIDE * SIDE), struct(columns, 2, LANES)],
-        grid=(8,),
-        in_specs=[pl.BlockSpec((tiles * BLOCK_ROWS, LANES), lambda k: (0, 0))],
-        out_specs=[pl.BlockSpec((tiles * TERMS, LANES), lambda k: (0, k)),
-                   pl.BlockSpec((columns, 2, LANES), lambda k: (0, 0, 0))],
+        out_shape=[struct(tiles * TERMS, SIDE * SIDE), struct(columns, TERMS, LANES)],
+        in_specs=[VMEM],
+        out_specs=[HBM, VMEM],
+        scratch_shapes=[pltpu.VMEM((8, tiles * TERMS, LANES), F32), pltpu.SemaphoreType.DMA((8,))],
         compiler_params=PARAMS,
         name="library_terms",
     )(blocks.reshape(tiles * BLOCK_ROWS, LANES))
     gram = lax.all_to_all(gram, "col", split_axis=0, concat_axis=0, tiled=True)
-    gram = jnp.sum(gram, axis=0).reshape(TERMS, TERMS) / (CELLS * CELLS)
+    gram = jnp.sum(gram, axis=0)[:, :TERMS] / (CELLS * CELLS)
     return library.reshape(1, 1, tiles, TERMS, SIDE * SIDE), gram
 
 

time: 59.1 us -> 54.7 us (0.926)
  local copies, waits for them, and re-layouts: 5.29 us -> 1.47 us
    unnamed x14 -> x12, local copies, waits for them, and re-layouts: 3.79 us -> 0.65 us
    pallas_call x1, Pallas kernels: 2.88 us -> 1.13 us  [per_device(): pl.pallas_call(library_kernel, out_shape=[struct(tiles * TERMS, SIDE * SI...]
    pallas_call x1, Pallas kernels: 4.88 us -> 6.09 us  [per_device(): pl.pallas_call(own_kernel, out_shape=[struct(2, FULL, LANES)] * 2, in_spe...]
    concatenate x1 -> x0, other arithmetic: 0.73 us -> none  [per_device(): turns = jnp.concatenate([lower_edge_quarter_turns, here[None]])]
    div x1 -> x0, local copies, waits for them, and re-layouts: 0.68 us -> none  [per_device(): gram = jnp.sum(gram, axis=0).reshape(TERMS, TERMS) / (CELLS * CELLS)]
    div x1, other arithmetic: 0.01 us -> 0.6 us  [per_device(): gram = jnp.sum(gram, axis=0)[:, :TERMS] / (CELLS * CELLS)]
  transfers between devices with their start and end apart: 4 -> 4, of which waited for: 2 -> 2; matrix products, arithmetic and copies ran while one was open for 1% -> 0% of each run, Pallas kernels for 8% -> 11%
where the time goes in v2:
time: 54.7 us; the launch traced here: 54.4 us
  blocking collectives  26.2 us (48%)
  Pallas kernels  12.2 us (22%)
  starting transfers between devices  10.5 us (19%)
  waiting for transfers between devices  2.63 us (5%)
  local copies, waits for them, and re-layouts  1.47 us (3%)
  between operations  0.73 us (1%)
  other arithmetic  0.63 us (1%)
    all_to_all x1, blocking collectives, per_device(): gram = lax.all_to_all(gram, 'col', split_axis=0, concat_axis=0, tiled=True)  13.8 us
    all_to_all x1, blocking collectives, per_device(): lax.all_to_all(blocks, 'tile', split_axis=0, concat_axis=0, tiled=True)  12.4 us
    pallas_call x1, Pallas kernels, per_device(): pl.pallas_call(own_kernel, out_shape=[struct(2, FULL, LANES)] * 2, in_spe...  6.09 us
    ppermute x1, starting transfers between devices, per_device(): from_left = lax.ppermute(to_right, 'col', onward(columns))  4.02 us
    ppermute x1, starting transfers between devices, per_device(): lax.ppermute(jnp.concatenate([u_velocity[:HALO], v_velocity[:HALO]]), 'ti...  3.9 us
    pallas_call x1, Pallas kernels, per_device(): pl.pallas_call(base_kernel, out_shape=struct(tiles, BLOCK_ROWS, LANES), i...  2.85 us
    ppermute x1, starting transfers between devices, per_device(): from_right = lax.ppermute(to_left, 'col', back(columns))  2.53 us
    pallas_call x1, Pallas kernels, per_device(): pl.pallas_call(strip_kernel, out_shape=[struct(2, FULL, LANES)] * 2 + [st...  2.14 us
  transfers between devices with their start and end apart: 4, of which 2 were waited for; matrix products, arithmetic and copies ran while one was open for 0% of the time, Pallas kernels for 11%

profile of v2, /device:TPU:0, one launch (start us, length us, event | category | flops | bytes accessed | tf_op | source)
XLA Modules:
  0.0 54.4 jit_solution(17385679630601437316)
XLA Ops:
  0.6 0.8 %fusion = (f32[12,512]{1,0:T(8,128)S(1)}, f32[12,512]{1,0:T(8,128)S(1)}, f32[12,512]{1,0:T(8,128)S(1)}, f32[12,512]{1,0:T(8,128)S(1)}) fusion(f32[512,512]{1,0:T(8,128)} %u_hbm.1, f32[512,512]{1,0:T(8,128)} %v_hbm.1), kind=kLoop, calls=%fused_computation.3 | loop fusion | bytes 196608 | tf_op jit(solution)/shard_map/slice | solution.py:363
  1.5 0.1 collective-permute-start
  1.6 3.9 %collective-permute-start.1 = (f32[24,512]{1,0:T(8,128)S(1)}, f32[24,512]{1,0:T(8,128)S(1)}, u32[]{:S(2)}, u32[]{:S(2)}) collective-permute-start(f32[24,512]{1,0:T(8,128)S(1)} %pad_maximum_fusion.1), channel_id=1, source_target_pairs={{8,0},{16,8},{24,16},{32,24},{40,32},{48,40},{56,48},{64,56},{72,6... | collective-permute-start | bytes 147464 | tf_op jit(solution)/shard_map/ppermute | solution.py:363
  5.5 0.0 copy-start
  5.5 0.0 copy-start.2
  5.5 6.1 %own_rows.1 = (f32[2,144,128]{2,1,0:T(8,128)S(1)}, f32[2,144,128]{2,1,0:T(8,128)S(1)}) custom-call(f32[512,512]{1,0:T(8,128)} %u_hbm.1, f32[512,512]{1,0:T(8,128)} %v_hbm.1, bf16[256,640]{1,0:T(8,128)(2,1)} %constant.17.clone.w_hbm.w_ref), custom_call_target="tpu_custom_call" | custom-call | tf_op jit(solution)/shard_map/own_rows/pallas_call | solution.py:364
  11.6 0.0 collective-permute-done.above_ref
  11.6 0.0 collective-permute-done.1.below_ref
  11.6 0.0 copy-start.5
  11.6 0.0 copy-done
  11.6 0.0 copy-done.2
  11.6 0.6 %copy-done.5 = s32[16]{0:T(128)S(1)} copy-done((s32[16]{0:T(128)S(1)}, s32[16]{0:T(128)}, u32[]{:S(2)}) %copy-start.5) | copy-done | bytes 88
  12.3 0.0 copy-start.1
  12.3 2.1 %row_strips.1 = (f32[2,144,128]{2,1,0:T(8,128)S(1)}, f32[2,144,128]{2,1,0:T(8,128)S(1)}, f32[8,144]{1,0:T(8,128)S(1)}, f32[8,144]{1,0:T(8,128)S(1)}) custom-call(s32[1]{0:T(128)} %bitcast.here_ref, s32[16]{0:T(128)S(1)} %copy-done.5, f32[24,512]{1,0:T(8,128)S(1)} %collective-permute-done.above_ref, f32[24,512]{1,0:T(8,128)S(1)} %collective-permute-done.1.below_ref, ...), custom_call_target="tpu_custom_call" | custom-call | tf_op jit(solution)/shard_map/row_strips/pallas_call | solution.py:376
  14.4 4.0 %collective-permute-start.2 = (f32[8,144]{1,0:T(8,128)S(1)}, f32[8,144]{1,0:T(8,128)S(1)}, u32[]{:S(2)}, u32[]{:S(2)}) collective-permute-start(f32[8,144]{1,0:T(8,128)S(1)} %get-tuple-element.14), channel_id=1, source_target_pairs={{0,1},{1,2},{2,3},{3,4},{4,5},{5,6},{6,7},{7,0},{8,9},{9,10},{10,1... | collective-permute-start | bytes 13832 | tf_op jit(solution)/shard_map/ppermute | solution.py:386
  18.4 0.0 copy-start.4
  18.4 0.0 copy-start.3
  18.4 2.5 %collective-permute-start.3 = (f32[8,144]{1,0:T(8,128)S(1)}, f32[8,144]{1,0:T(8,128)S(1)}, u32[]{:S(2)}, u32[]{:S(2)}) collective-permute-start(f32[8,144]{1,0:T(8,128)S(1)} %get-tuple-element.15), channel_id=1, source_target_pairs={{1,0},{2,1},{3,2},{4,3},{5,4},{6,5},{7,6},{0,7},{9,8},{10,9},{11,1... | collective-permute-start | bytes 13832 | tf_op jit(solution)/shard_map/ppermute | solution.py:385
  21.0 1.5 %collective-permute-done.2.from_left_ref = f32[8,144]{1,0:T(8,128)S(1)} collective-permute-done((f32[8,144]{1,0:T(8,128)S(1)}, f32[8,144]{1,0:T(8,128)S(1)}, u32[]{:S(2)}, u32[]{:S(2)}) %collective-permute-start.2) | collective-permute-done | bytes 4640 | tf_op jit(solution)/shard_map/ppermute | solution.py:386
  22.5 1.1 %collective-permute-done.3.from_right_ref = f32[8,144]{1,0:T(8,128)S(1)} collective-permute-done((f32[8,144]{1,0:T(8,128)S(1)}, f32[8,144]{1,0:T(8,128)S(1)}, u32[]{:S(2)}, u32[]{:S(2)}) %collective-permute-start.3) | collective-permute-done | bytes 4640 | tf_op jit(solution)/shard_map/ppermute | solution.py:385
  23.6 0.0 copy-done.1
  23.6 0.0 copy-done.4
  23.6 0.0 copy-done.3
  23.6 2.9 %base_fields.1 = f32[16,48,128]{2,1,0:T(8,128)S(1)} custom-call(s32[4,4]{1,0:T(4,128)S(1)} %copy-done.3, s32[4,4]{1,0:T(4,128)S(1)} %copy-done.4, f32[2,144,128]{2,1,0:T(8,128)S(1)} %get-tuple-element.12.main_ref, f32[2,144,128]{2,1,0:T(8,128)S(1)} %get-tuple-element.13.edge_ref, f32[8,144]{1,0:T(8,128)S(1)} %collective-permute-done.2.from_left_ref, ...), custom_call_target="tpu_custom_call" | custom-call | tf_op jit(solution)/shard_map/base_fields/pallas_call | solution.py:387
  26.5 12.4 %all_to_all.10 = f32[16,48,128]{2,1,0:T(8,128)S(1)} all-to-all(f32[16,48,128]{2,1,0:T(8,128)S(1)} %base_fields.1), channel_id=1, replica_groups=mesh['tile'=16,'col'=8] {'tile'}, dimensions={0} | all-to-all | bytes 786432 | tf_op jit(solution)/shard_map/all_to_all | solution.py:397
  38.9 1.1 %library_terms.1 = (f32[256,1024]{1,0:T(8,128)}, f32[8,16,128]{2,1,0:T(8,128)S(1)}) custom-call(f32[768,128]{1,0:T(8,128)S(1)} %bitcast.3), custom_call_target="tpu_custom_call" | custom-call | tf_op jit(solution)/shard_map/library_terms/pallas_call | solution.py:398
  40.0 13.8 %all_to_all.11 = f32[8,16,128]{2,1,0:T(8,128)S(1)} all-to-all(f32[8,16,128]{2,1,0:T(8,128)S(1)} %get-tuple-element.17), channel_id=1, replica_groups=mesh['tile'=16,'col'=8] {'col'}, dimensions={0} | all-to-all | bytes 131072 | tf_op jit(solution)/shard_map/all_to_all | solution.py:407
  53.8 0.6 %slice_multiply_fusion = f32[16,16]{1,0:T(8,128)} fusion(f32[16,128]{1,0:T(8,128)S(1)} %reduce_sum.9), kind=kLoop, calls=%fused_computation.2 | loop fusion | flops 256 | bytes 2048 | tf_op jit(solution)/shard_map/div | solution.py:408
  (3 shorter events, 0.0 us)
Async XLA Ops:
  1.5 10.1 %collective-permute-start = (f32[24,512]{1,0:T(8,128)S(1)}, f32[24,512]{1,0:T(8,128)S(1)}, u32[]{:S(2)}, u32[]{:S(2)}) collective-permute-start(f32[24,512]{1,0:T(8,128)S(1)} %pad_maximum_fusion), channel_id=1, source_target_pairs={{0,8},{8,16},{16,24},{24,32},{32,40},{40,48},{48,56},{56,64},{64,7... | collective-permute-start | bytes 147464 | tf_op jit(solution)/shard_map/ppermute | solution.py:362
  1.6 10.0 %collective-permute-start.1 = (f32[24,512]{1,0:T(8,128)S(1)}, f32[24,512]{1,0:T(8,128)S(1)}, u32[]{:S(2)}, u32[]{:S(2)}) collective-permute-start(f32[24,512]{1,0:T(8,128)S(1)} %pad_maximum_fusion.1), channel_id=1, source_target_pairs={{8,0},{16,8},{24,16},{32,24},{40,32},{48,40},{56,48},{64,56},{72,6... | collective-permute-start | bytes 147464 | tf_op jit(solution)/shard_map/ppermute | solution.py:363
  5.5 6.1 %copy-start = (bf16[256,640]{1,0:T(8,128)(2,1)S(1)}, bf16[256,640]{1,0:T(8,128)(2,1)}, u32[]{:S(2)}) copy-start(bf16[256,640]{1,0:T(8,128)(2,1)} %constant.17.clone.w_hbm.w_ref) | copy-start | bytes 983044
  5.5 6.1 %copy-start.2 = (bf16[2,16,768]{2,1,0:T(8,128)(2,1)S(1)}, bf16[2,16,768]{2,1,0:T(8,128)(2,1)}, u32[]{:S(2)}) copy-start(bf16[2,16,768]{2,1,0:T(8,128)(2,1)} %constant.18.clone.sel_ref) | copy-start | bytes 147460
  11.6 0.7 %copy-start.5 = (s32[16]{0:T(128)S(1)}, s32[16]{0:T(128)}, u32[]{:S(2)}) copy-start(s32[16]{0:T(128)} %turns_ref.1) | copy-start | bytes 196
  12.3 11.3 %copy-start.1 = (bf16[48,512]{1,0:T(8,128)(2,1)S(1)}, bf16[48,512]{1,0:T(8,128)(2,1)}, u32[]{:S(2)}) copy-start(bf16[48,512]{1,0:T(8,128)(2,1)} %constant.19.clone.place_ref) | copy-start | bytes 147460
  14.4 8.1 %collective-permute-start.2 = (f32[8,144]{1,0:T(8,128)S(1)}, f32[8,144]{1,0:T(8,128)S(1)}, u32[]{:S(2)}, u32[]{:S(2)}) collective-permute-start(f32[8,144]{1,0:T(8,128)S(1)} %get-tuple-element.14), channel_id=1, source_target_pairs={{0,1},{1,2},{2,3},{3,4},{4,5},{5,6},{6,7},{7,0},{8,9},{9,10},{10,1... | collective-permute-start | bytes 13832 | tf_op jit(solution)/shard_map/ppermute | solution.py:386
  18.4 5.2 %copy-start.4 = (s32[4,4]{1,0:T(4,128)S(1)}, s32[4,4]{1,0:T(4,128)}, u32[]{:S(2)}) copy-start(s32[4,4]{1,0:T(4,128)} %owner_ref.1) | copy-start | bytes 196
  18.4 5.2 %copy-start.3 = (s32[4,4]{1,0:T(4,128)S(1)}, s32[4,4]{1,0:T(4,128)}, u32[]{:S(2)}) copy-start(s32[4,4]{1,0:T(4,128)} %mask_ref.1) | copy-start | bytes 196
  18.4 5.2 %collective-permute-start.3 = (f32[8,144]{1,0:T(8,128)S(1)}, f32[8,144]{1,0:T(8,128)S(1)}, u32[]{:S(2)}, u32[]{:S(2)}) collective-permute-start(f32[8,144]{1,0:T(8,128)S(1)} %get-tuple-element.15), channel_id=1, source_target_pairs={{1,0},{2,1},{3,2},{4,3},{5,4},{6,5},{7,6},{0,7},{9,8},{10,9},{11,1... | collective-permute-start | bytes 13832 | tf_op jit(solution)/shard_map/ppermute | solution.py:385

commit v3 on v2

v3 whole, which is shorter than its diff:
```python
import math

import jax
import jax.numpy as jnp
import ml_dtypes
import numpy as np
from jax import lax
from jax.experimental import pallas as pl
from jax.experimental.pallas import tpu as pltpu
from jax.sharding import PartitionSpec as P

PASSES = 8
KAPPA = 0.2
POOL = 4
CELLS = 128
HALO = 12
SIDE = 32
TERMS = 16
PAD = 8
FULL = CELLS + 2 * PAD
LANES = 128
BASES = 5
BLOCK_ROWS = 48
F32 = jnp.float32
BF16 = jnp.bfloat16

SCALE = KAPPA**PASSES / (POOL * POOL)
RIM_COLS = (-2, -1, 0, CELLS - 1, CELLS, CELLS + 1)


def across(power, fine, coarse):
    total = 0
    for inner in range(POOL):
        offset = fine - (POOL * coarse + inner)
        if abs(offset) <= power and (power + offset) % 2 == 0:
            total += math.comb(power, (power + offset) // 2)
    return total


def column_weights():
    fine = CELLS * POOL
    main = np.zeros((fine, 9 * LANES), np.float32)
    rim = np.zeros((fine, LANES), np.float32)
    for j in range(PASSES + 1):
        for coarse in range(-2, CELLS + 2):
            for f in range(max(0, POOL * coarse - PASSES), min(fine, POOL * coarse + POOL + PASSES)):
                value = math.comb(PASSES, j) * across(PASSES - j, f, coarse)
                if 0 <= coarse < CELLS:
                    main[f, (PASSES - j) * LANES + coarse] = value
                if coarse in RIM_COLS:
                    rim[f, 6 * j + RIM_COLS.index(coarse)] = value
    assert not rim[64 : fine - 64].any()
    rim[LANES - 64 : LANES] = rim[fine - 64 :]
    rim[LANES : 2 * LANES] = rim[:LANES]
    weights = np.concatenate([main, rim], axis=1)
    out = weights.astype(ml_dtypes.bfloat16)
    assert (out.astype(np.float32) == weights).all()
    return out


def rim_selector():
    row = lax.broadcasted_iota(jnp.int32, (32, 1), 0)
    source = jnp.full((32, 1), -1, jnp.int32)
    for f in range(2):
        for c in range(3):
            source = jnp.where(row == 3 * f + c, 64 * f + c, source)
            source = jnp.where(row == 8 + 3 * f + c, 64 * f + 3 + c, source)
        source = jnp.where(row == 16 + 2 * f, 64 * f + 1, source)
        source = jnp.where(row == 17 + 2 * f, 64 * f + 4, source)
    lane = lax.broadcasted_iota(jnp.int32, (32, 3 * LANES), 1) % LANES
    return jnp.where(lane == source, 1.0, 0.0).astype(BF16)


def place_matrix():
    place = np.zeros((3, 32, 4 * LANES), np.float32)
    for f in range(2):
        add, rim = 2 * f * LANES, (2 * f + 1) * LANES
        place[:, 3 * f + 0, rim + 0] = 1.0
        place[:, 3 * f + 1, add + 0] = 1.0
        place[:, 3 * f + 2, add + 1] = 1.0
        place[:, 8 + 3 * f + 0, add + CELLS - 2] = 1.0
        place[:, 8 + 3 * f + 1, add + CELLS - 1] = 1.0
        place[:, 8 + 3 * f + 2, rim + CELLS - 1] = 1.0
        place[:, 16 + 2 * f, rim + 0] = 1.0
        place[:, 17 + 2 * f, rim + CELLS - 1] = 1.0
    return place.reshape(96, 4 * LANES).astype(ml_dtypes.bfloat16)


def head(x):
    scaled = x * 65537.0
    return scaled - (scaled - x)


def two_parts(x):
    high = head(x)
    return high.astype(BF16), (x - high).astype(BF16)


def three_parts(x):
    high = head(x)
    rest = x - high
    mid = head(rest)
    return high.astype(BF16), mid.astype(BF16), (rest - mid).astype(BF16)


def dot(a, b, dims=(((1,), (0,)), ((), ()))):
    return lax.dot_general(a, b, dims, preferred_element_type=F32)


def three_rows(t):
    rows = t[0].shape[0]
    up = pltpu.roll(t[3], 1, 0)
    down = pltpu.roll(t[0], rows - 1, 0)
    left, middle, right = t[0] + t[1], t[1] + t[2], t[2] + t[3]
    return [left + up, t[0] + middle, middle + t[3], right + down]


def turn(first, second, k):
    cosine = jnp.where(k == 0, 1.0, jnp.where(k == 2, -1.0, 0.0)).astype(F32)
    sine = jnp.where(k == 1, 1.0, jnp.where(k == 3, -1.0, 0.0)).astype(F32)
    return cosine * first - sine * second, sine * first + cosine * second


def send_kernel(here_ref, turns_hbm, u_hbm, v_hbm, up_ref, down_ref, x_ref, turns_ref, sem, turns_sem):
    rows = u_hbm.shape[0]
    copies = [pltpu.make_async_copy(hbm.at[pl.ds(start, 16)], x_ref.at[side, f], sem.at[side, f])
              for side, start in enumerate((0, rows - 16)) for f, hbm in enumerate((u_hbm, v_hbm))]
    table = pltpu.make_async_copy(turns_hbm, turns_ref, turns_sem)
    table.start()
    for copy in copies:
        copy.start()
    table.wait()
    tiles = turns_ref.shape[0]
    here = here_ref[0]
    k_up = lax.rem(4 - turns_ref[here], 4)
    k_down = turns_ref[lax.rem(here + 1, tiles)]
    for copy in copies:
        copy.wait()
    for side, (to_ref, k, start) in enumerate(((up_ref, k_up, 0), (down_ref, k_down, 16 - HALO))):
        for f, x in enumerate(turn(x_ref[side, 0], x_ref[side, 1], k)):
            to_ref[f * HALO : (f + 1) * HALO] = x[start : start + HALO]


def phase_rows(p, own, above_ref, below_ref, f, cut, strip_ref):
    strip_ref[...] = jnp.zeros_like(strip_ref)
    for m in range(3):
        strip_ref[5 + m : 6 + m] = above_ref[f * HALO + 4 * m + p : f * HALO + 4 * m + p + 1, cut]
        strip_ref[8 + m : 9 + m] = below_ref[f * HALO + 4 * m + p : f * HALO + 4 * m + p + 1, cut]
    return jnp.concatenate([strip_ref[:8], own, strip_ref[8:]], axis=0)


def rim_kernel(u_first, u_last, v_first, v_last, above_ref, below_ref, w_ref, left_ref, right_ref, own_ref,
               parts_ref, first_ref, last_ref, strip_ref):
    lane = lax.broadcasted_iota(jnp.int32, (1, LANES), 1)
    for f, (head_ref, tail_ref) in enumerate(((u_first, u_last), (v_first, v_last))):
        for p in range(POOL):
            spot = pl.ds(p, CELLS, stride=POOL)
            ends = [phase_rows(p, ref[spot, :], above_ref, below_ref, f, slice(c * LANES, (c + 1) * LANES), strip_ref)
                    for c, ref in ((0, head_ref), (3, tail_ref))]
            parts = jnp.concatenate(two_parts(jnp.where(lane < 64, *ends)), axis=1)
            parts_ref[(f * POOL + p) * FULL : (f * POOL + p + 1) * FULL] = parts
    z = dot(parts_ref[...], w_ref[...])
    for p in range(POOL):
        u, v = [z[(f * POOL + p) * FULL : (f * POOL + p + 1) * FULL] for f in range(2)]
        both = jnp.where(lane < 64, u, pltpu.roll(v, 64, 1))
        first_ref[p] = both
        last_ref[p] = both
    for _ in range(PASSES):
        new = three_rows([pltpu.roll(last_ref[p], LANES - 6, 1) for p in range(POOL)])
        for p in range(POOL):
            last_ref[p] = new[p] + first_ref[p]
    pooled = ((last_ref[0] + last_ref[1]) + (last_ref[2] + last_ref[3])) * SCALE
    out = dot(rim_selector(), jnp.concatenate(three_parts(pooled), axis=1), (((1,), (1,)), ((), ())))
    left_ref[...] = out[:8]
    right_ref[...] = out[8:16]
    own_ref[...] = out[16:]


def main_kernel(*refs):
    above_ref, below_ref, w_ref, _, main_ref, parts_ref, sum_ref, strip_ref = refs[8:]
    fine = POOL * CELLS
    for f in range(2):
        for c in range(4):
            cut = slice(c * LANES, (c + 1) * LANES)
            for p in range(POOL):
                own = refs[4 * f + c][pl.ds(p, CELLS, stride=POOL), :]
                high, low = two_parts(phase_rows(p, own, above_ref, below_ref, f, cut, strip_ref))
                spot = slice((f * POOL + p) * FULL, (f * POOL + p + 1) * FULL)
                parts_ref[spot, cut] = high
                parts_ref[spot, fine + c * LANES : fine + (c + 1) * LANES] = low
    for start in range(0, 9, 2):
        wide = min(2, 9 - start)
        w = w_ref[:, start * LANES : (start + wide) * LANES]
        z = dot(parts_ref[:, :fine], w) + dot(parts_ref[:, fine:], w)
        for stage in range(start, start + wide):
            part = z[:, (stage - start) * LANES : (stage - start + 1) * LANES]
            for f in range(2):
                own = [part[(f * POOL + p) * FULL : (f * POOL + p + 1) * FULL] for p in range(POOL)]
                if stage:
                    own = [a + b for a, b in zip(three_rows([sum_ref[f, p] for p in range(POOL)]), own)]
                for p in range(POOL):
                    sum_ref[f, p] = own[p]
    for f in range(2):
        main_ref[f] = ((sum_ref[f, 0] + sum_ref[f, 1]) + (sum_ref[f, 2] + sum_ref[f, 3])) * SCALE


def base_kernel(mask_ref, owner_ref, main_ref, own_ref, from_left_ref, from_right_ref, place_ref, out_ref, field_ref,
                base_ref, term_ref, gram_ref):
    lane = lax.broadcasted_iota(jnp.int32, (1, LANES), 1)
    received = jnp.concatenate([from_left_ref[...], from_right_ref[...], own_ref[...]], axis=0)
    placed = dot(jnp.concatenate(three_parts(received), axis=0), place_ref[...], (((0,), (0,)), ((), ())))
    inner = slice(PAD, PAD + CELLS)
    slopes = []
    for f in range(2):
        full = main_ref[f] + placed[:, 2 * f * LANES : (2 * f + 1) * LANES]
        field_ref[f] = full
        rim = placed[inner, (2 * f + 1) * LANES : (2 * f + 2) * LANES]
        centre = full[inner]
        left = jnp.where(lane == 0, rim, pltpu.roll(centre, 1, 1))
        right = jnp.where(lane == LANES - 1, rim, pltpu.roll(centre, LANES - 1, 1))
        dx = (right - left) * 0.5
        dy = (field_ref[f, PAD + 1 : PAD + 1 + CELLS] - field_ref[f, PAD - 1 : PAD - 1 + CELLS]) * 0.5
        slopes.append((centre, dx, dy))
    (u, u_dx, u_dy), (v, v_dx, v_dy) = slopes
    grid = CELLS // SIDE
    rows = []
    for a in range(grid):
        row = jnp.zeros((1, LANES), F32)
        for e in range(grid):
            row = jnp.where(lane // SIDE == e, (mask_ref[a, e] == 1).astype(F32), row)
        rows.append(jnp.broadcast_to(row, (SIDE, LANES)))
    live = jnp.concatenate(rows, axis=0) > 0.5
    for n, x in enumerate((u, v, v_dx - u_dy, u_dy + v_dx, u_dx - v_dy)):
        base_ref[n] = jnp.where(live, x, 0.0)
    for n, x in enumerate(terms_of([base_ref[n] for n in range(BASES)])):
        term_ref[n] = x
    for n in range(TERMS):
        first = term_ref[n]
        for m in range(n, TERMS):
            product = (first * term_ref[m]).reshape(CELLS // 8, 8, LANES)
            total = jnp.sum(jnp.sum(product, axis=0), axis=0, keepdims=True)
            gram_ref[n * TERMS + m : n * TERMS + m + 1] = total
            if m > n:
                gram_ref[m * TERMS + n : m * TERMS + n + 1] = total
    sums = jnp.concatenate(three_parts(gram_ref[...]), axis=1)
    gram = dot(jnp.ones((8, 3 * LANES), BF16), sums, (((1,), (1,)), ((), ())))
    owners = out_ref.shape[0]
    out_ref[...] = jnp.zeros_like(out_ref)
    for o in range(owners):
        for half in range(2):
            out_ref[o, 40 + half : 41 + half] = gram[:1, half * LANES : (half + 1) * LANES]
    for a in range(grid):
        for e in range(grid):

            @pl.when(mask_ref[a, e] == 1)
            def _():
                owner = owner_ref[a, e]
                for n in range(BASES):
                    block = None
                    for q in range(LANES // SIDE):
                        x = base_ref[n, pl.ds(a * SIDE + q, 8, stride=4), :]
                        x = pltpu.roll(x, (q - e) % 4 * SIDE, 1) if q != e else x
                        block = x if block is None else jnp.where(lane // SIDE == q, x, block)
                    out_ref[owner, 8 * n : 8 * n + 8] = block


def terms_of(base):
    u, v, vort, strain, stretch = base
    return [u, v, vort, strain, stretch, vort * vort, vort * strain, vort * stretch, strain * strain, stretch * stretch,
            strain * stretch, u * vort, v * vort, u * strain, v * stretch, u * v]


def library_kernel(x_ref, out_hbm, gram_ref, out_ref, sem):
    slots = x_ref.shape[0] // BLOCK_ROWS
    copies = []
    for k in range(8):
        base = [x_ref[pl.ds(8 * n + k, slots, stride=BLOCK_ROWS), :] for n in range(BASES)]
        for n, x in enumerate(terms_of(base)):
            out_ref[k, pl.ds(n, slots, stride=TERMS), :] = x
        copies.append(pltpu.make_async_copy(out_ref.at[k], out_hbm.at[:, pl.ds(k * LANES, LANES)], sem.at[k]))
        copies[k].start()
    totals = [jnp.sum(x_ref[pl.ds(40 + half, slots, stride=BLOCK_ROWS), :], axis=0, keepdims=True) for half in range(2)]
    for n in range(TERMS):
        row = totals[n // 8]
        row = pltpu.roll(row, LANES - n % 8 * TERMS, 1) if n % 8 else row
        for c in range(gram_ref.shape[0]):
            gram_ref[c, n : n + 1] = row
    for copy in copies:
        copy.wait()


VMEM = pl.BlockSpec(memory_space=pltpu.VMEM)
HBM = pl.BlockSpec(memory_space=pltpu.HBM)
SMEM = pl.BlockSpec(memory_space=pltpu.SMEM)
PARAMS = pltpu.CompilerParams(vmem_limit_bytes=48 << 20)


def struct(*shape):
    return jax.ShapeDtypeStruct(shape, F32)


def per_device(u_velocity, v_velocity, ocean_mask, tile_owner, lower_edge_quarter_turns):
    tiles, columns = lax.axis_size("tile"), lax.axis_size("col")
    onward = lambda count: [(i, (i + 1) % count) for i in range(count)]
    back = lambda count: [((i + 1) % count, i) for i in range(count)]
    here = lax.axis_index("tile").astype(jnp.int32)[None]
    in_hbm = lambda x: pltpu.with_memory_space_constraint(x, pltpu.HBM)
    up, down = pl.pallas_call(
        send_kernel,
        out_shape=[struct(2 * HALO, POOL * CELLS)] * 2,
        in_specs=[SMEM] + [HBM] * 3,
        out_specs=[VMEM] * 2,
        scratch_shapes=[pltpu.VMEM((2, 2, 16, POOL * CELLS), F32), pltpu.SMEM((tiles,), jnp.int32),
                        pltpu.SemaphoreType.DMA((2, 2)), pltpu.SemaphoreType.DMA],
        compiler_params=PARAMS,
        name="send_rows",
    )(here, *[in_hbm(x) for x in (lower_edge_quarter_turns, u_velocity, v_velocity)])
    up, down, u_velocity, v_velocity = lax.optimization_barrier((up, down, u_velocity, v_velocity))
    above = lax.ppermute(down, "tile", onward(tiles))
    below = lax.ppermute(up, "tile", back(tiles))
    weights = jnp.asarray(column_weights())
    column = lambda c: pl.BlockSpec((POOL * CELLS, LANES), lambda i: (0, c))
    whole = lambda *shape: pl.BlockSpec(shape, lambda i: (0,) * len(shape))
    halo = whole(2 * HALO, POOL * CELLS)
    to_left, to_right, own = pl.pallas_call(
        rim_kernel,
        out_shape=[struct(8, FULL), struct(8, FULL), struct(16, FULL)],
        grid=(1,),
        in_specs=[column(0), column(3)] * 2 + [halo] * 2 + [pl.BlockSpec((2 * LANES, LANES), lambda i: (0, 9))],
        out_specs=[whole(8, FULL), whole(8, FULL), whole(16, FULL)],
        scratch_shapes=[pltpu.VMEM((2 * POOL * FULL, 2 * LANES), BF16), pltpu.VMEM((POOL, FULL, LANES), F32),
                        pltpu.VMEM((POOL, FULL, LANES), F32), pltpu.VMEM((16, LANES), F32)],
        compiler_params=PARAMS,
        name="rim_columns",
    )(u_velocity, u_velocity, v_velocity, v_velocity, above, below, weights)
    from_right = lax.ppermute(to_left, "col", back(columns))
    from_left = lax.ppermute(to_right, "col", onward(columns))
    main = pl.pallas_call(
        main_kernel,
        out_shape=struct(2, FULL, LANES),
        grid=(1,),
        in_specs=[column(c) for c in range(4)] * 2 + [halo] * 2 + [whole(POOL * CELLS, 10 * LANES), whole(16, FULL)],
        out_specs=whole(2, FULL, LANES),
        scratch_shapes=[pltpu.VMEM((2 * POOL * FULL, 2 * POOL * CELLS), BF16), pltpu.VMEM((2, POOL, FULL, LANES), F32),
                        pltpu.VMEM((16, LANES), F32)],
        compiler_params=PARAMS,
        name="main_columns",
    )(*[u_velocity] * 4, *[v_velocity] * 4, above, below, weights, own)
    blocks = pl.pallas_call(
        base_kernel,
        out_shape=struct(tiles, BLOCK_ROWS, LANES),
        in_specs=[SMEM] * 2 + [VMEM] * 5,
        out_specs=VMEM,
        scratch_shapes=[pltpu.VMEM((2, FULL, LANES), F32), pltpu.VMEM((BASES, CELLS, LANES), F32),
                        pltpu.VMEM((TERMS, CELLS, LANES), F32), pltpu.VMEM((TERMS * TERMS, LANES), F32)],
        compiler_params=PARAMS,
        name="base_fields",
    )(ocean_mask, tile_owner, main, own, from_left, from_right, jnp.asarray(place_matrix()))
    blocks = lax.all_to_all(blocks, "tile", split_axis=0, concat_axis=0, tiled=True)
    library, gram = pl.pallas_call(
        library_kernel,
        out_shape=[struct(tiles * TERMS, SIDE * SIDE), struct(columns, TERMS, LANES)],
        in_specs=[VMEM],
        out_specs=[HBM, VMEM],
        scratch_shapes=[pltpu.VMEM((8, tiles * TERMS, LANES), F32), pltpu.SemaphoreType.DMA((8,))],
        compiler_params=PARAMS,
        name="library_terms",
    )(blocks.reshape(tiles * BLOCK_ROWS, LANES))
    gram = lax.all_to_all(gram, "col", split_axis=0, concat_axis=0, tiled=True)
    gram = jnp.sum(gram, axis=0)[:, :TERMS] / (CELLS * CELLS)
    return library.reshape(1, 1, tiles, TERMS, SIDE * SIDE), gram


def solution(mesh):
    in_specs = (P("tile", "col"), P("tile", "col"), P("tile", "col"), P("tile", "col"), P())
    out_specs = (P("tile", "col", None, None, None), P())
    return jax.shard_map(
        per_device, mesh=mesh, in_specs=in_specs, out_specs=out_specs, check_vma=False
    )
```

time: 54.7 us -> 51.4 us (0.940)
  Pallas kernels: 12.2 us -> 10 us
  waiting for transfers between devices: 2.63 us -> 1.81 us
    pallas_call x2 -> x3, Pallas kernels: 8.23 us -> 5.97 us  [the longest x1 3.62 us: per_device(): pl.pallas_call(main_kernel, out_shape=struct(2, FULL, LANES), grid=(1,),...]
    ppermute x2, waiting for transfers between devices: 0.01 us -> 1.8 us  [the longest x1 1.8 us: per_device(): above = lax.ppermute(down, 'tile', onward(tiles))]
    ppermute x1, waiting for transfers between devices: 1.55 us -> 0.01 us  [per_device(): from_left = lax.ppermute(to_right, 'col', onward(columns))]
    ppermute x1, waiting for transfers between devices: 1.08 us -> 0.01 us  [per_device(): from_right = lax.ppermute(to_left, 'col', back(columns))]
    all_to_all x1, blocking collectives: 12.4 us -> 13.4 us  [per_device(): lax.all_to_all(blocks, 'tile', split_axis=0, concat_axis=0, tiled=True)]
    all_to_all x1, blocking collectives: 13.8 us -> 12.8 us  [per_device(): gram = lax.all_to_all(gram, 'col', split_axis=0, concat_axis=0, tiled=True)]
    slice x1 -> x0, local copies, waits for them, and re-layouts: 0.82 us -> none  [per_device(): u_velocity[:HALO]]
    unnamed x12, local copies, waits for them, and re-layouts: 0.65 us -> 1.33 us
  transfers between devices with their start and end apart: 4 -> 4, of which waited for: 2 -> 1; matrix products, arithmetic and copies ran while one was open for 0% -> 0% of each run, Pallas kernels for 11% -> 7%
where the time goes in v3:
time: 51.4 us; the launch traced here: 51.2 us
  blocking collectives  26.2 us (51%)
  starting transfers between devices  10.5 us (20%)
  Pallas kernels  10 us (19%)
  waiting for transfers between devices  1.81 us (4%)
  local copies, waits for them, and re-layouts  1.33 us (3%)
  between operations  0.75 us (1%)
  other arithmetic  0.61 us (1%)
    all_to_all x1, blocking collectives, per_device(): lax.all_to_all(blocks, 'tile', split_axis=0, concat_axis=0, tiled=True)  13.4 us
    all_to_all x1, blocking collectives, per_device(): gram = lax.all_to_all(gram, 'col', split_axis=0, concat_axis=0, tiled=True)  12.8 us
    ppermute x1, starting transfers between devices, per_device(): from_left = lax.ppermute(to_right, 'col', onward(columns))  4.06 us
    ppermute x1, starting transfers between devices, per_device(): below = lax.ppermute(up, 'tile', back(tiles))  3.84 us
    pallas_call x1, Pallas kernels, per_device(): pl.pallas_call(main_kernel, out_shape=struct(2, FULL, LANES), grid=(1,),...  3.62 us
    pallas_call x1, Pallas kernels, per_device(): pl.pallas_call(base_kernel, out_shape=struct(tiles, BLOCK_ROWS, LANES), i...  2.92 us
    ppermute x1, starting transfers between devices, per_device(): from_right = lax.ppermute(to_left, 'col', back(columns))  2.5 us
    ppermute x1, waiting for transfers between devices, per_device(): above = lax.ppermute(down, 'tile', onward(tiles))  1.8 us
  transfers between devices with their start and end apart: 4, of which 1 were waited for; matrix products, arithmetic and copies ran while one was open for 0% of the time, Pallas kernels for 7%

profile of v3, /device:TPU:0, one launch (start us, length us, event | category | flops | bytes accessed | tf_op | source)
XLA Modules:
  0.0 51.2 jit_solution(13463346901021327544)
XLA Ops:
  0.6 0.0 copy-start.1
  0.6 0.0 copy-start
  0.7 1.0 %send_rows.1 = (f32[24,512]{1,0:T(8,128)S(1)}, f32[24,512]{1,0:T(8,128)S(1)}) custom-call(s32[1]{0:T(128)} %bitcast.here_ref, s32[16]{0:T(128)} %turns_hbm.1, f32[512,512]{1,0:T(8,128)} %refs_3_, f32[512,512]{1,0:T(8,128)} %refs_7_), custom_call_target="tpu_custom_call" | custom-call | tf_op jit(solution)/shard_map/send_rows/pallas_call | solution.py:308
  1.7 0.1 collective-permute-start
  1.8 3.8 %collective-permute-start.1 = (f32[24,512]{1,0:T(8,128)S(1)}, f32[24,512]{1,0:T(8,128)S(1)}, u32[]{:S(2)}, u32[]{:S(2)}) collective-permute-start(f32[24,512]{1,0:T(8,128)S(1)} %get-tuple-element.18), channel_id=1, source_target_pairs={{8,0},{16,8},{24,16},{32,24},{40,32},{48,40},{56,48},{64,56},{72,6... | collective-permute-start | bytes 147464 | tf_op jit(solution)/shard_map/ppermute | solution.py:320
  5.6 1.8 %collective-permute-done.above_ref.refs_8_ = f32[24,512]{1,0:T(8,128)S(1)} collective-permute-done((f32[24,512]{1,0:T(8,128)S(1)}, f32[24,512]{1,0:T(8,128)S(1)}, u32[]{:S(2)}, u32[]{:S(2)}) %collective-permute-start) | collective-permute-done | bytes 49184 | tf_op jit(solution)/shard_map/ppermute | solution.py:319
  7.4 0.0 collective-permute-done.1.below_ref.refs_9_
  7.4 0.0 copy-done.1
  7.4 0.0 copy-done
  7.4 0.0 copy-start.2
  7.4 1.3 %copy-done.2 = bf16[512,1280]{1,0:T(8,128)(2,1)S(1)} copy-done((bf16[512,1280]{1,0:T(8,128)(2,1)S(1)}, bf16[512,1280]{1,0:T(8,128)(2,1)}, u32[]{:S(2)}) %copy-start.2) | copy-done | bytes 1310744
  8.7 1.3 %rim_columns.1 = (f32[8,144]{1,0:T(8,128)S(1)}, f32[8,144]{1,0:T(8,128)S(1)}, f32[16,144]{1,0:T(8,128)S(1)}) custom-call(f32[512,512]{1,0:T(8,128)S(1)} %copy-done, f32[512,512]{1,0:T(8,128)S(1)} %copy-done, f32[512,512]{1,0:T(8,128)S(1)} %copy-done.1, f32[512,512]{1,0:T(8,128)S(1)} %copy-done.1, f32[24,512]{1,0:T(8,128)S(1)} %collective-permute-done.above_ref.refs_8_, ...), custom_call_target="tpu_custom_call" | custom-call | tf_op jit(solution)/shard_map/rim_columns/pallas_call | solution.py:325
  10.1 4.1 %collective-permute-start.2 = (f32[8,144]{1,0:T(8,128)S(1)}, f32[8,144]{1,0:T(8,128)S(1)}, u32[]{:S(2)}, u32[]{:S(2)}) collective-permute-start(f32[8,144]{1,0:T(8,128)S(1)} %get-tuple-element.20), channel_id=1, source_target_pairs={{0,1},{1,2},{2,3},{3,4},{4,5},{5,6},{6,7},{7,0},{8,9},{9,10},{10,1... | collective-permute-start | bytes 13832 | tf_op jit(solution)/shard_map/ppermute | solution.py:337
  14.1 2.5 %collective-permute-start.3 = (f32[8,144]{1,0:T(8,128)S(1)}, f32[8,144]{1,0:T(8,128)S(1)}, u32[]{:S(2)}, u32[]{:S(2)}) collective-permute-start(f32[8,144]{1,0:T(8,128)S(1)} %get-tuple-element.21), channel_id=1, source_target_pairs={{1,0},{2,1},{3,2},{4,3},{5,4},{6,5},{7,6},{0,7},{9,8},{10,9},{11,1... | collective-permute-start | bytes 13832 | tf_op jit(solution)/shard_map/ppermute | solution.py:336
  16.6 0.0 copy-start.3
  16.6 0.0 copy-start.4
  16.6 0.0 copy-start.5
  16.6 3.6 %main_columns.1.main_ref = f32[2,144,128]{2,1,0:T(8,128)S(1)} custom-call(f32[512,512]{1,0:T(8,128)S(1)} %copy-done, f32[512,512]{1,0:T(8,128)S(1)} %copy-done, f32[512,512]{1,0:T(8,128)S(1)} %copy-done, f32[512,512]{1,0:T(8,128)S(1)} %copy-done, f32[512,512]{1,0:T(8,128)S(1)} %copy-done.1, f32[512,512]{1,0:T(8,128)S(1)} %copy-done.1, ...), custom_call_target="tpu_custom_call" | custom-call | tf_op jit(solution)/shard_map/main_columns/pallas_call | solution.py:338
  20.3 0.0 collective-permute-done.2.from_left_ref
  20.3 0.0 collective-permute-done.3.from_right_ref
  20.3 0.0 copy-done.3
  20.3 0.0 copy-done.4
  20.3 0.0 copy-done.5
  20.3 2.9 %base_fields.1 = f32[16,48,128]{2,1,0:T(8,128)S(1)} custom-call(s32[4,4]{1,0:T(4,128)S(1)} %copy-done.4, s32[4,4]{1,0:T(4,128)S(1)} %copy-done.5, f32[2,144,128]{2,1,0:T(8,128)S(1)} %main_columns.1.main_ref, f32[16,144]{1,0:T(8,128)S(1)} %get-tuple-element.19.refs_11_.own_ref, f32[8,144]{1,0:T(8,128)S(1)} %collective-permute-done.2.from_left_ref, ...), custom_call_target="tpu_custom_call" | custom-call | tf_op jit(solution)/shard_map/base_fields/pallas_call | solution.py:349
  23.2 13.4 %all_to_all.10 = f32[16,48,128]{2,1,0:T(8,128)S(1)} all-to-all(f32[16,48,128]{2,1,0:T(8,128)S(1)} %base_fields.1), channel_id=1, replica_groups=mesh['tile'=16,'col'=8] {'tile'}, dimensions={0} | all-to-all | bytes 786432 | tf_op jit(solution)/shard_map/all_to_all | solution.py:359
  36.6 1.1 %library_terms.1 = (f32[256,1024]{1,0:T(8,128)}, f32[8,16,128]{2,1,0:T(8,128)S(1)}) custom-call(f32[768,128]{1,0:T(8,128)S(1)} %bitcast.3), custom_call_target="tpu_custom_call" | custom-call | tf_op jit(solution)/shard_map/library_terms/pallas_call | solution.py:360
  37.8 12.8 %all_to_all.11 = f32[8,16,128]{2,1,0:T(8,128)S(1)} all-to-all(f32[8,16,128]{2,1,0:T(8,128)S(1)} %get-tuple-element.23), channel_id=1, replica_groups=mesh['tile'=16,'col'=8] {'col'}, dimensions={0} | all-to-all | bytes 131072 | tf_op jit(solution)/shard_map/all_to_all | solution.py:369
  50.6 0.6 %slice_multiply_fusion = f32[16,16]{1,0:T(8,128)} fusion(f32[16,128]{1,0:T(8,128)S(1)} %reduce_sum.9), kind=kLoop, calls=%fused_computation | loop fusion | flops 256 | bytes 2048 | tf_op jit(solution)/shard_map/div | solution.py:370
  (1 shorter events, 0.0 us)
Async XLA Ops:
  0.6 6.8 %copy-start.1 = (f32[512,512]{1,0:T(8,128)S(1)}, f32[512,512]{1,0:T(8,128)}, u32[]{:S(2)}) copy-start(f32[512,512]{1,0:T(8,128)} %refs_7_) | copy-start | bytes 3145732
  0.6 6.8 %copy-start = (f32[512,512]{1,0:T(8,128)S(1)}, f32[512,512]{1,0:T(8,128)}, u32[]{:S(2)}) copy-start(f32[512,512]{1,0:T(8,128)} %refs_3_) | copy-start | bytes 3145732
  1.7 5.7 %collective-permute-start = (f32[24,512]{1,0:T(8,128)S(1)}, f32[24,512]{1,0:T(8,128)S(1)}, u32[]{:S(2)}, u32[]{:S(2)}) collective-permute-start(f32[24,512]{1,0:T(8,128)S(1)} %get-tuple-element.17), channel_id=1, source_target_pairs={{0,8},{8,16},{16,24},{24,32},{32,40},{40,48},{48,56},{56,64},{64,7... | collective-permute-start | bytes 147464 | tf_op jit(solution)/shard_map/ppermute | solution.py:319
  1.8 5.6 %collective-permute-start.1 = (f32[24,512]{1,0:T(8,128)S(1)}, f32[24,512]{1,0:T(8,128)S(1)}, u32[]{:S(2)}, u32[]{:S(2)}) collective-permute-start(f32[24,512]{1,0:T(8,128)S(1)} %get-tuple-element.18), channel_id=1, source_target_pairs={{8,0},{16,8},{24,16},{32,24},{40,32},{48,40},{56,48},{64,56},{72,6... | collective-permute-start | bytes 147464 | tf_op jit(solution)/shard_map/ppermute | solution.py:320
  7.4 1.3 %copy-start.2 = (bf16[512,1280]{1,0:T(8,128)(2,1)S(1)}, bf16[512,1280]{1,0:T(8,128)(2,1)}, u32[]{:S(2)}) copy-start(bf16[512,1280]{1,0:T(8,128)(2,1)} %constant.15.clone.w_ref.refs_10_) | copy-start | bytes 3932164
  10.1 10.2 %collective-permute-start.2 = (f32[8,144]{1,0:T(8,128)S(1)}, f32[8,144]{1,0:T(8,128)S(1)}, u32[]{:S(2)}, u32[]{:S(2)}) collective-permute-start(f32[8,144]{1,0:T(8,128)S(1)} %get-tuple-element.20), channel_id=1, source_target_pairs={{0,1},{1,2},{2,3},{3,4},{4,5},{5,6},{6,7},{7,0},{8,9},{9,10},{10,1... | collective-permute-start | bytes 13832 | tf_op jit(solution)/shard_map/ppermute | solution.py:337
  14.1 6.1 %collective-permute-start.3 = (f32[8,144]{1,0:T(8,128)S(1)}, f32[8,144]{1,0:T(8,128)S(1)}, u32[]{:S(2)}, u32[]{:S(2)}) collective-permute-start(f32[8,144]{1,0:T(8,128)S(1)} %get-tuple-element.21), channel_id=1, source_target_pairs={{1,0},{2,1},{3,2},{4,3},{5,4},{6,5},{7,6},{0,7},{9,8},{10,9},{11,1... | collective-permute-start | bytes 13832 | tf_op jit(solution)/shard_map/ppermute | solution.py:336
  16.6 3.7 %copy-start.3 = (bf16[96,512]{1,0:T(8,128)(2,1)S(1)}, bf16[96,512]{1,0:T(8,128)(2,1)}, u32[]{:S(2)}) copy-start(bf16[96,512]{1,0:T(8,128)(2,1)} %constant.16.clone.place_ref) | copy-start | bytes 294916
  16.6 3.7 %copy-start.4 = (s32[4,4]{1,0:T(4,128)S(1)}, s32[4,4]{1,0:T(4,128)}, u32[]{:S(2)}) copy-start(s32[4,4]{1,0:T(4,128)} %mask_ref.1) | copy-start | bytes 196
  16.6 3.7 %copy-start.5 = (s32[4,4]{1,0:T(4,128)S(1)}, s32[4,4]{1,0:T(4,128)}, u32[]{:S(2)}) copy-start(s32[4,4]{1,0:T(4,128)} %owner_ref.1) | copy-start | bytes 196

commit v4 on v3

--- a/solution.py
+++ b/solution.py
@@ -141,61 +141,104 @@
             to_ref[f * HALO : (f + 1) * HALO] = x[start : start + HALO]
 
 
-def phase_rows(p, own, above_ref, below_ref, f, cut, strip_ref):
-    strip_ref[...] = jnp.zeros_like(strip_ref)
-    for m in range(3):
-        strip_ref[5 + m : 6 + m] = above_ref[f * HALO + 4 * m + p : f * HALO + 4 * m + p + 1, cut]
-        strip_ref[8 + m : 9 + m] = below_ref[f * HALO + 4 * m + p : f * HALO + 4 * m + p + 1, cut]
-    return jnp.concatenate([strip_ref[:8], own, strip_ref[8:]], axis=0)
-
-
-def rim_kernel(u_first, u_last, v_first, v_last, above_ref, below_ref, w_ref, left_ref, right_ref, own_ref,
-               parts_ref, first_ref, last_ref, strip_ref):
+EARLY = 4
+
+
+def prepare_kernel(*refs):
+    w_hbm, parts_ref, w_out, rim_ref, early_ref, rim_parts_ref, first_ref, last_ref, sem = refs[8:]
+    copy = pltpu.make_async_copy(w_hbm, w_out, sem)
+    copy.start()
     lane = lax.broadcasted_iota(jnp.int32, (1, LANES), 1)
-    for f, (head_ref, tail_ref) in enumerate(((u_first, u_last), (v_first, v_last))):
+    fine = POOL * CELLS
+    for f in range(2):
         for p in range(POOL):
-            spot = pl.ds(p, CELLS, stride=POOL)
-            ends = [phase_rows(p, ref[spot, :], above_ref, below_ref, f, slice(c * LANES, (c + 1) * LANES), strip_ref)
-                    for c, ref in ((0, head_ref), (3, tail_ref))]
-            parts = jnp.concatenate(two_parts(jnp.where(lane < 64, *ends)), axis=1)
-            parts_ref[(f * POOL + p) * FULL : (f * POOL + p + 1) * FULL] = parts
-    z = dot(parts_ref[...], w_ref[...])
+            spot = slice((f * POOL + p) * CELLS, (f * POOL + p + 1) * CELLS)
+            pieces = [two_parts(refs[4 * f + c][pl.ds(p, CELLS, stride=POOL), :]) for c in range(4)]
+            for part in range(2):
+                for c in range(4):
+                    parts_ref[spot, part * fine + c * LANES : part * fine + (c + 1) * LANES] = pieces[c][part]
+                rim_parts_ref[spot, part * LANES : (part + 1) * LANES] = jnp.where(
+                    lane < 64, pieces[0][part], pieces[3][part])
+    copy.wait()
+    z = dot(rim_parts_ref[...], w_out[: 2 * LANES, 9 * LANES :])
     for p in range(POOL):
-        u, v = [z[(f * POOL + p) * FULL : (f * POOL + p + 1) * FULL] for f in range(2)]
+        u, v = [z[(f * POOL + p) * CELLS : (f * POOL + p + 1) * CELLS] for f in range(2)]
         both = jnp.where(lane < 64, u, pltpu.roll(v, 64, 1))
-        first_ref[p] = both
-        last_ref[p] = both
+        for to_ref in (first_ref, last_ref):
+            to_ref[p, :PAD] = jnp.zeros((PAD, LANES), F32)
+            to_ref[p, PAD:] = both
     for _ in range(PASSES):
         new = three_rows([pltpu.roll(last_ref[p], LANES - 6, 1) for p in range(POOL)])
         for p in range(POOL):
             last_ref[p] = new[p] + first_ref[p]
     pooled = ((last_ref[0] + last_ref[1]) + (last_ref[2] + last_ref[3])) * SCALE
-    out = dot(rim_selector(), jnp.concatenate(three_parts(pooled), axis=1), (((1,), (1,)), ((), ())))
-    left_ref[...] = out[:8]
-    right_ref[...] = out[8:16]
-    own_ref[...] = out[16:]
-
-
-def main_kernel(*refs):
-    above_ref, below_ref, w_ref, _, main_ref, parts_ref, sum_ref, strip_ref = refs[8:]
-    fine = POOL * CELLS
-    for f in range(2):
+    rim_ref[: PAD + CELLS] = pooled
+    rim_ref[PAD + CELLS :] = pooled[:PAD]
+    for start in range(0, EARLY, 2):
+        cut = slice(start * LANES, (start + 2) * LANES)
+        early_ref[:, cut] = dot(parts_ref[:, :fine], w_out[:, cut]) + dot(parts_ref[:, fine:], w_out[:, cut])
+
+
+def rim_kernel(above_ref, below_ref, w_ref, rim_in, left_ref, right_ref, own_ref, rows_ref, strip_ref, rim_ref):
+    lane = lax.broadcasted_iota(jnp.int32, (1, LANES), 1)
+    strip_ref[...] = jnp.zeros_like(strip_ref)
+    for s, (x_ref, start) in enumerate(((above_ref, 1), (below_ref, 4))):
+        ends = jnp.where(lane < 64, x_ref[:, :LANES], x_ref[:, 3 * LANES :])
+        rows_ref[s] = ends
+        for f in range(2):
+            for p in range(POOL):
+                spot = ((f * 2 + s) * POOL + p) * 8 + start
+                strip_ref[spot : spot + 3] = rows_ref[s, pl.ds(f * HALO + p, 3, stride=POOL), :]
+    z = dot(jnp.concatenate(two_parts(strip_ref[...]), axis=1), w_ref[...])
+    rim_ref[...] = rim_in[...]
+    for s, (spot, start) in enumerate(((7, 3), (PAD + CELLS - 2, 2))):
+        first = []
+        for p in range(POOL):
+            u, v = [z[((f * 2 + s) * POOL + p) * 8 : ((f * 2 + s) * POOL + p + 1) * 8] for f in range(2)]
+            first.append(jnp.where(lane < 64, u, pltpu.roll(v, 64, 1)))
+        last = first
+        for _ in range(PASSES):
+            last = [a + b for a, b in zip(three_rows([pltpu.roll(x, LANES - 6, 1) for x in last]), first)]
+        pooled = ((last[0] + last[1]) + (last[2] + last[3])) * SCALE
+        rim_ref[spot : spot + 3] = rim_ref[spot : spot + 3] + pooled[start : start + 3]
+    turned = jnp.transpose(rim_ref[...])
+    for to_ref, columns in ((left_ref, (0, 1, 2)), (right_ref, (3, 4, 5)), (own_ref, (1, 4))):
+        to_ref[...] = jnp.zeros_like(to_ref)
+        for f in range(2):
+            for place, c in enumerate(columns):
+                spot = len(columns) * f + place
+                to_ref[spot : spot + 1] = turned[64 * f + c : 64 * f + c + 1]
+
+
+def main_kernel(parts_ref, early_ref, w_ref, above_ref, below_ref, _, main_ref, rows_ref, strip_ref, sum_ref):
+    strip_ref[...] = jnp.zeros_like(strip_ref)
+    for s, (x_ref, start) in enumerate(((above_ref, 5), (below_ref, 8))):
         for c in range(4):
             cut = slice(c * LANES, (c + 1) * LANES)
-            for p in range(POOL):
-                own = refs[4 * f + c][pl.ds(p, CELLS, stride=POOL), :]
-                high, low = two_parts(phase_rows(p, own, above_ref, below_ref, f, cut, strip_ref))
-                spot = slice((f * POOL + p) * FULL, (f * POOL + p + 1) * FULL)
-                parts_ref[spot, cut] = high
-                parts_ref[spot, fine + c * LANES : fine + (c + 1) * LANES] = low
+            rows_ref[s, c] = x_ref[:, cut]
+            for f in range(2):
+                for p in range(POOL):
+                    spot = (f * POOL + p) * 16 + start
+                    strip_ref[spot : spot + 3, cut] = rows_ref[s, c, pl.ds(f * HALO + p, 3, stride=POOL), :]
+    strips = jnp.concatenate(two_parts(strip_ref[...]), axis=1)
+    fine = POOL * CELLS
     for start in range(0, 9, 2):
         wide = min(2, 9 - start)
         w = w_ref[:, start * LANES : (start + wide) * LANES]
-        z = dot(parts_ref[:, :fine], w) + dot(parts_ref[:, fine:], w)
+        if start < EARLY:
+            z = early_ref[:, start * LANES : (start + wide) * LANES]
+        else:
+            z = dot(parts_ref[:, :fine], w) + dot(parts_ref[:, fine:], w)
+        z_strip = dot(strips[:, :fine], w) + dot(strips[:, fine:], w)
         for stage in range(start, start + wide):
-            part = z[:, (stage - start) * LANES : (stage - start + 1) * LANES]
+            cut = slice((stage - start) * LANES, (stage - start + 1) * LANES)
             for f in range(2):
-                own = [part[(f * POOL + p) * FULL : (f * POOL + p + 1) * FULL] for p in range(POOL)]
+                own = []
+                for p in range(POOL):
+                    block = f * POOL + p
+                    own.append(jnp.concatenate([
+                        z_strip[block * 16 : block * 16 + 8, cut], z[block * CELLS : (block + 1) * CELLS, cut],
+                        z_strip[block * 16 + 8 : block * 16 + 16, cut]], axis=0))
                 if stage:
                     own = [a + b for a, b in zip(three_rows([sum_ref[f, p] for p in range(POOL)]), own)]
                 for p in range(POOL):
@@ -205,7 +248,7 @@
 
 
 def base_kernel(mask_ref, owner_ref, main_ref, own_ref, from_left_ref, from_right_ref, place_ref, out_ref, field_ref,
-                base_ref, term_ref, gram_ref):
+                base_ref, term_ref, gram_ref, pack_ref, tile_ref):
     lane = lax.broadcasted_iota(jnp.int32, (1, LANES), 1)
     received = jnp.concatenate([from_left_ref[...], from_right_ref[...], own_ref[...]], axis=0)
     placed = dot(jnp.concatenate(three_parts(received), axis=0), place_ref[...], (((0,), (0,)), ((), ())))
@@ -242,26 +285,31 @@
             gram_ref[n * TERMS + m : n * TERMS + m + 1] = total
             if m > n:
                 gram_ref[m * TERMS + n : m * TERMS + n + 1] = total
-    sums = jnp.concatenate(three_parts(gram_ref[...]), axis=1)
-    gram = dot(jnp.ones((8, 3 * LANES), BF16), sums, (((1,), (1,)), ((), ())))
+    totals = jnp.sum(gram_ref[...], axis=1, keepdims=True)
+    row = lax.broadcasted_iota(jnp.int32, (TERMS * TERMS, 1), 0)
+    spread = jnp.where(row % LANES == lane, totals, 0.0)
+    halves = [jnp.sum(spread[h * LANES : (h + 1) * LANES], axis=0, keepdims=True) for h in range(2)]
     owners = out_ref.shape[0]
-    out_ref[...] = jnp.zeros_like(out_ref)
-    for o in range(owners):
-        for half in range(2):
-            out_ref[o, 40 + half : 41 + half] = gram[:1, half * LANES : (half + 1) * LANES]
+    nothing = grid * grid
+    for o in range(owners + 1):
+        tile_ref[o] = nothing
     for a in range(grid):
         for e in range(grid):
-
-            @pl.when(mask_ref[a, e] == 1)
-            def _():
-                owner = owner_ref[a, e]
-                for n in range(BASES):
-                    block = None
-                    for q in range(LANES // SIDE):
-                        x = base_ref[n, pl.ds(a * SIDE + q, 8, stride=4), :]
-                        x = pltpu.roll(x, (q - e) % 4 * SIDE, 1) if q != e else x
-                        block = x if block is None else jnp.where(lane // SIDE == q, x, block)
-                    out_ref[owner, 8 * n : 8 * n + 8] = block
+            tile_ref[jnp.where(mask_ref[a, e] == 1, owner_ref[a, e], owners)] = a * grid + e
+    pack_ref[nothing] = jnp.zeros((8 * BASES, LANES), F32)
+    for a in range(grid):
+        for n in range(BASES):
+            pieces = [base_ref[n, pl.ds(a * SIDE + q, 8, stride=4), :] for q in range(grid)]
+            for e in range(grid):
+                block = None
+                for q in range(grid):
+                    x = pltpu.roll(pieces[q], (q - e) % grid * SIDE, 1) if q != e else pieces[q]
+                    block = x if block is None else jnp.where(lane // SIDE == q, x, block)
+                pack_ref[a * grid + e, 8 * n : 8 * n + 8] = block
+    for o in range(owners):
+        out_ref[o, : 8 * BASES] = pack_ref[tile_ref[o]]
+        for h in range(2):
+            out_ref[o, 8 * BASES + h : 8 * BASES + h + 1] = halves[h]
 
 
 def terms_of(base):
@@ -292,7 +340,7 @@
 VMEM = pl.BlockSpec(memory_space=pltpu.VMEM)
 HBM = pl.BlockSpec(memory_space=pltpu.HBM)
 SMEM = pl.BlockSpec(memory_space=pltpu.SMEM)
-PARAMS = pltpu.CompilerParams(vmem_limit_bytes=48 << 20)
+PARAMS = pltpu.CompilerParams(vmem_limit_bytes=24 << 20)
 
 
 def struct(*shape):
@@ -318,41 +366,54 @@
     up, down, u_velocity, v_velocity = lax.optimization_barrier((up, down, u_velocity, v_velocity))
     above = lax.ppermute(down, "tile", onward(tiles))
     below = lax.ppermute(up, "tile", back(tiles))
-    weights = jnp.asarray(column_weights())
     column = lambda c: pl.BlockSpec((POOL * CELLS, LANES), lambda i: (0, c))
     whole = lambda *shape: pl.BlockSpec(shape, lambda i: (0,) * len(shape))
     halo = whole(2 * HALO, POOL * CELLS)
+    rows = 2 * POOL * CELLS
+    parts, weights, rim, early = pl.pallas_call(
+        prepare_kernel,
+        out_shape=[jax.ShapeDtypeStruct((rows, 2 * POOL * CELLS), BF16),
+                   jax.ShapeDtypeStruct((POOL * CELLS, 10 * LANES), BF16), struct(FULL, LANES),
+                   struct(rows, EARLY * LANES)],
+        grid=(1,),
+        in_specs=[column(c) for c in range(4)] * 2 + [HBM],
+        out_specs=[VMEM] * 4,
+        scratch_shapes=[pltpu.VMEM((rows, 2 * LANES), BF16)] + [pltpu.VMEM((POOL, PAD + CELLS, LANES), F32)] * 2
+        + [pltpu.SemaphoreType.DMA],
+        compiler_params=PARAMS,
+        name="prepare_rows",
+    )(*[u_velocity] * 4, *[v_velocity] * 4, in_hbm(jnp.asarray(column_weights())))
     to_left, to_right, own = pl.pallas_call(
         rim_kernel,
         out_shape=[struct(8, FULL), struct(8, FULL), struct(16, FULL)],
         grid=(1,),
-        in_specs=[column(0), column(3)] * 2 + [halo] * 2 + [pl.BlockSpec((2 * LANES, LANES), lambda i: (0, 9))],
+        in_specs=[halo] * 2 + [pl.BlockSpec((2 * LANES, LANES), lambda i: (0, 9)), whole(FULL, LANES)],
         out_specs=[whole(8, FULL), whole(8, FULL), whole(16, FULL)],
-        scratch_shapes=[pltpu.VMEM((2 * POOL * FULL, 2 * LANES), BF16), pltpu.VMEM((POOL, FULL, LANES), F32),
-                        pltpu.VMEM((POOL, FULL, LANES), F32), pltpu.VMEM((16, LANES), F32)],
+        scratch_shapes=[pltpu.VMEM((2, 2 * HALO, LANES), F32), pltpu.VMEM((2 * 2 * POOL * 8, LANES), F32),
+                        pltpu.VMEM((FULL, LANES), F32)],
         compiler_params=PARAMS,
         name="rim_columns",
-    )(u_velocity, u_velocity, v_velocity, v_velocity, above, below, weights)
+    )(above, below, weights, rim)
     from_right = lax.ppermute(to_left, "col", back(columns))
     from_left = lax.ppermute(to_right, "col", onward(columns))
     main = pl.pallas_call(
         main_kernel,
         out_shape=struct(2, FULL, LANES),
-        grid=(1,),
-        in_specs=[column(c) for c in range(4)] * 2 + [halo] * 2 + [whole(POOL * CELLS, 10 * LANES), whole(16, FULL)],
-        out_specs=whole(2, FULL, LANES),
-        scratch_shapes=[pltpu.VMEM((2 * POOL * FULL, 2 * POOL * CELLS), BF16), pltpu.VMEM((2, POOL, FULL, LANES), F32),
-                        pltpu.VMEM((16, LANES), F32)],
+        in_specs=[VMEM] * 6,
+        out_specs=VMEM,
+        scratch_shapes=[pltpu.VMEM((2, 4, 2 * HALO, LANES), F32), pltpu.VMEM((2 * POOL * 16, POOL * CELLS), F32),
+                        pltpu.VMEM((2, POOL, FULL, LANES), F32)],
         compiler_params=PARAMS,
         name="main_columns",
-    )(*[u_velocity] * 4, *[v_velocity] * 4, above, below, weights, own)
+    )(parts, early, weights, above, below, own)
     blocks = pl.pallas_call(
         base_kernel,
         out_shape=struct(tiles, BLOCK_ROWS, LANES),
         in_specs=[SMEM] * 2 + [VMEM] * 5,
         out_specs=VMEM,
         scratch_shapes=[pltpu.VMEM((2, FULL, LANES), F32), pltpu.VMEM((BASES, CELLS, LANES), F32),
-                        pltpu.VMEM((TERMS, CELLS, LANES), F32), pltpu.VMEM((TERMS * TERMS, LANES), F32)],
+                        pltpu.VMEM((TERMS, CELLS, LANES), F32), pltpu.VMEM((TERMS * TERMS, LANES), F32),
+                        pltpu.VMEM((17, 8 * BASES, LANES), F32), pltpu.SMEM((tiles + 1,), jnp.int32)],
         compiler_params=PARAMS,
         name="base_fields",
     )(ocean_mask, tile_owner, main, own, from_left, from_right, jnp.asarray(place_matrix()))

time: 51.4 us -> 48.3 us (0.940)
  waiting for transfers between devices: 1.81 us -> 0.08 us
  local copies, waits for them, and re-layouts: 1.33 us -> 0.02 us
    ppermute x1, waiting for transfers between devices: 1.8 us -> 0.01 us  [per_device(): above = lax.ppermute(down, 'tile', onward(tiles))]
    pallas_call x1 -> x2, Pallas kernels: 3.62 us -> 5.26 us  [the longest x1 2.73 us: per_device(): pl.pallas_call(prepare_kernel, out_shape=[jax.ShapeDtypeStruct((rows, 2 *...]
    unnamed x12 -> x10, local copies, waits for them, and re-layouts: 1.33 us -> 0.02 us
    all_to_all x1, blocking collectives: 13.4 us -> 12.3 us  [per_device(): lax.all_to_all(blocks, 'tile', split_axis=0, concat_axis=0, tiled=True)]
    pallas_call x1, Pallas kernels: 2.92 us -> 1.86 us  [per_device(): pl.pallas_call(base_kernel, out_shape=struct(tiles, BLOCK_ROWS, LANES), i...]
    all_to_all x1, blocking collectives: 12.8 us -> 13.7 us  [per_device(): gram = lax.all_to_all(gram, 'col', split_axis=0, concat_axis=0, tiled=True)]
  transfers between devices with their start and end apart: 4 -> 4, of which waited for: 1 -> 1; matrix products, arithmetic and copies ran while one was open for 0% -> 0% of each run, Pallas kernels for 7% -> 11%
where the time goes in v4:
time: 48.3 us; the launch traced here: 48.1 us
  blocking collectives  26 us (54%)
  starting transfers between devices  10.5 us (22%)
  Pallas kernels  10.2 us (21%)
  between operations  0.73 us (2%)
  other arithmetic  0.61 us (1%)
    all_to_all x1, blocking collectives, per_device(): gram = lax.all_to_all(gram, 'col', split_axis=0, concat_axis=0, tiled=True)  13.7 us
    all_to_all x1, blocking collectives, per_device(): lax.all_to_all(blocks, 'tile', split_axis=0, concat_axis=0, tiled=True)  12.3 us
    ppermute x1, starting transfers between devices, per_device(): from_left = lax.ppermute(to_right, 'col', onward(columns))  4.03 us
    ppermute x1, starting transfers between devices, per_device(): below = lax.ppermute(up, 'tile', back(tiles))  3.84 us
    pallas_call x1, Pallas kernels, per_device(): pl.pallas_call(prepare_kernel, out_shape=[jax.ShapeDtypeStruct((rows, 2 *...  2.73 us
    ppermute x1, starting transfers between devices, per_device(): from_right = lax.ppermute(to_left, 'col', back(columns))  2.53 us
    pallas_call x1, Pallas kernels, per_device(): pl.pallas_call(main_kernel, out_shape=struct(2, FULL, LANES), in_specs=[V...  2.53 us
    pallas_call x1, Pallas kernels, per_device(): pl.pallas_call(base_kernel, out_shape=struct(tiles, BLOCK_ROWS, LANES), i...  1.86 us
  transfers between devices with their start and end apart: 4, of which 1 were waited for; matrix products, arithmetic and copies ran while one was open for 0% of the time, Pallas kernels for 11%

profile of v4, /device:TPU:0, one launch (start us, length us, event | category | flops | bytes accessed | tf_op | source)
XLA Modules:
  0.0 48.1 jit_solution(13837579259050766202)
XLA Ops:
  0.6 0.0 copy-start.1
  0.6 0.0 copy-start
  0.7 1.0 %send_rows.1 = (f32[24,512]{1,0:T(8,128)S(1)}, f32[24,512]{1,0:T(8,128)S(1)}) custom-call(s32[1]{0:T(128)} %bitcast.here_ref, s32[16]{0:T(128)} %turns_hbm.1, f32[512,512]{1,0:T(8,128)} %refs_3_, f32[512,512]{1,0:T(8,128)} %refs_7_), custom_call_target="tpu_custom_call" | custom-call | tf_op jit(solution)/shard_map/send_rows/pallas_call | solution.py:356
  1.7 0.1 collective-permute-start
  1.8 3.8 %collective-permute-start.1 = (f32[24,512]{1,0:T(8,128)S(1)}, f32[24,512]{1,0:T(8,128)S(1)}, u32[]{:S(2)}, u32[]{:S(2)}) collective-permute-start(f32[24,512]{1,0:T(8,128)S(1)} %get-tuple-element.25), channel_id=1, source_target_pairs={{8,0},{16,8},{24,16},{32,24},{40,32},{48,40},{56,48},{64,56},{72,6... | collective-permute-start | bytes 147464 | tf_op jit(solution)/shard_map/ppermute | solution.py:368
  5.6 0.0 copy-done.1
  5.6 0.0 copy-done
  5.6 2.7 %prepare_rows.1 = (bf16[1024,1024]{1,0:T(8,128)(2,1)S(1)}, bf16[512,1280]{1,0:T(8,128)(2,1)S(1)}, f32[144,128]{1,0:T(8,128)S(1)}, f32[1024,512]{1,0:T(8,128)S(1)}) custom-call(f32[512,512]{1,0:T(8,128)S(1)} %copy-done, f32[512,512]{1,0:T(8,128)S(1)} %copy-done, f32[512,512]{1,0:T(8,128)S(1)} %copy-done, f32[512,512]{1,0:T(8,128)S(1)} %copy-done, ...), custom_call_target="tpu_custom_call" | custom-call | tf_op jit(solution)/shard_map/prepare_rows/pallas_call | solution.py:373
  8.4 0.0 collective-permute-done.above_ref
  8.4 0.0 collective-permute-done.1.below_ref
  8.4 0.9 %rim_columns.1 = (f32[8,144]{1,0:T(8,128)S(1)}, f32[8,144]{1,0:T(8,128)S(1)}, f32[16,144]{1,0:T(8,128)S(1)}) custom-call(f32[24,512]{1,0:T(8,128)S(1)} %collective-permute-done.above_ref, f32[24,512]{1,0:T(8,128)S(1)} %collective-permute-done.1.below_ref, bf16[512,1280]{1,0:T(8,128)(2,1)S(1)} %get-tuple-element.23.w_ref, f32[144,128]{1,0:T(8,128)S(1)} %get-tuple-element.26.rim_in), custom_call_target="tpu_custom_call" | custom-call | tf_op jit(solution)/shard_map/rim_columns/pallas_call | solution.py:386
  9.3 4.0 %collective-permute-start.2 = (f32[8,144]{1,0:T(8,128)S(1)}, f32[8,144]{1,0:T(8,128)S(1)}, u32[]{:S(2)}, u32[]{:S(2)}) collective-permute-start(f32[8,144]{1,0:T(8,128)S(1)} %get-tuple-element.28), channel_id=1, source_target_pairs={{0,1},{1,2},{2,3},{3,4},{4,5},{5,6},{6,7},{7,0},{8,9},{9,10},{10,1... | collective-permute-start | bytes 13832 | tf_op jit(solution)/shard_map/ppermute | solution.py:398
  13.3 2.5 %collective-permute-start.3 = (f32[8,144]{1,0:T(8,128)S(1)}, f32[8,144]{1,0:T(8,128)S(1)}, u32[]{:S(2)}, u32[]{:S(2)}) collective-permute-start(f32[8,144]{1,0:T(8,128)S(1)} %get-tuple-element.29), channel_id=1, source_target_pairs={{1,0},{2,1},{3,2},{4,3},{5,4},{6,5},{7,6},{0,7},{9,8},{10,9},{11,1... | collective-permute-start | bytes 13832 | tf_op jit(solution)/shard_map/ppermute | solution.py:397
  15.8 0.0 copy-start.2
  15.9 0.0 copy-start.3
  15.9 0.0 copy-start.4
  15.9 2.5 %main_columns.1.main_ref = f32[2,144,128]{2,1,0:T(8,128)S(1)} custom-call(bf16[1024,1024]{1,0:T(8,128)(2,1)S(1)} %get-tuple-element.21.parts_ref, f32[1024,512]{1,0:T(8,128)S(1)} %get-tuple-element.22.early_ref, bf16[512,1280]{1,0:T(8,128)(2,1)S(1)} %get-tuple-element.23.w_ref, f32[24,512]{1,0:T(8,128)S(1)} %collective-permute-done.above_ref, ...), custom_call_target="tpu_custom_call" | custom-call | tf_op jit(solution)/shard_map/main_columns/pallas_call | solution.py:399
  18.4 0.0 collective-permute-done.2.from_left_ref
  18.4 0.1 collective-permute-done.3.from_right_ref
  18.5 0.0 copy-done.2
  18.5 0.0 copy-done.3
  18.5 0.0 copy-done.4
  18.5 1.9 %base_fields.1 = f32[16,48,128]{2,1,0:T(8,128)S(1)} custom-call(s32[4,4]{1,0:T(4,128)S(1)} %copy-done.3, s32[4,4]{1,0:T(4,128)S(1)} %copy-done.4, f32[2,144,128]{2,1,0:T(8,128)S(1)} %main_columns.1.main_ref, f32[16,144]{1,0:T(8,128)S(1)} %get-tuple-element.27._.own_ref, f32[8,144]{1,0:T(8,128)S(1)} %collective-permute-done.2.from_left_ref, ...), custom_call_target="tpu_custom_call" | custom-call | tf_op jit(solution)/shard_map/base_fields/pallas_call | solution.py:409
  20.4 12.3 %all_to_all.10 = f32[16,48,128]{2,1,0:T(8,128)S(1)} all-to-all(f32[16,48,128]{2,1,0:T(8,128)S(1)} %base_fields.1), channel_id=1, replica_groups=mesh['tile'=16,'col'=8] {'tile'}, dimensions={0} | all-to-all | bytes 786432 | tf_op jit(solution)/shard_map/all_to_all | solution.py:420
  32.7 1.1 %library_terms.1 = (f32[256,1024]{1,0:T(8,128)}, f32[8,16,128]{2,1,0:T(8,128)S(1)}) custom-call(f32[768,128]{1,0:T(8,128)S(1)} %bitcast.3), custom_call_target="tpu_custom_call" | custom-call | tf_op jit(solution)/shard_map/library_terms/pallas_call | solution.py:421
  33.8 13.7 %all_to_all.11 = f32[8,16,128]{2,1,0:T(8,128)S(1)} all-to-all(f32[8,16,128]{2,1,0:T(8,128)S(1)} %get-tuple-element.31), channel_id=1, replica_groups=mesh['tile'=16,'col'=8] {'col'}, dimensions={0} | all-to-all | bytes 131072 | tf_op jit(solution)/shard_map/all_to_all | solution.py:430
  47.5 0.6 %slice_multiply_fusion = f32[16,16]{1,0:T(8,128)} fusion(f32[16,128]{1,0:T(8,128)S(1)} %reduce_sum.9), kind=kLoop, calls=%fused_computation | loop fusion | flops 256 | bytes 2048 | tf_op jit(solution)/shard_map/div | solution.py:431
  (1 shorter events, 0.0 us)
Async XLA Ops:
  0.6 5.0 %copy-start.1 = (f32[512,512]{1,0:T(8,128)S(1)}, f32[512,512]{1,0:T(8,128)}, u32[]{:S(2)}) copy-start(f32[512,512]{1,0:T(8,128)} %refs_7_) | copy-start | bytes 3145732
  0.6 5.0 %copy-start = (f32[512,512]{1,0:T(8,128)S(1)}, f32[512,512]{1,0:T(8,128)}, u32[]{:S(2)}) copy-start(f32[512,512]{1,0:T(8,128)} %refs_3_) | copy-start | bytes 3145732
  1.7 6.7 %collective-permute-start = (f32[24,512]{1,0:T(8,128)S(1)}, f32[24,512]{1,0:T(8,128)S(1)}, u32[]{:S(2)}, u32[]{:S(2)}) collective-permute-start(f32[24,512]{1,0:T(8,128)S(1)} %get-tuple-element.24), channel_id=1, source_target_pairs={{0,8},{8,16},{16,24},{24,32},{32,40},{40,48},{48,56},{56,64},{64,7... | collective-permute-start | bytes 147464 | tf_op jit(solution)/shard_map/ppermute | solution.py:367
  1.8 6.6 %collective-permute-start.1 = (f32[24,512]{1,0:T(8,128)S(1)}, f32[24,512]{1,0:T(8,128)S(1)}, u32[]{:S(2)}, u32[]{:S(2)}) collective-permute-start(f32[24,512]{1,0:T(8,128)S(1)} %get-tuple-element.25), channel_id=1, source_target_pairs={{8,0},{16,8},{24,16},{32,24},{40,32},{48,40},{56,48},{64,56},{72,6... | collective-permute-start | bytes 147464 | tf_op jit(solution)/shard_map/ppermute | solution.py:368
  9.3 9.1 %collective-permute-start.2 = (f32[8,144]{1,0:T(8,128)S(1)}, f32[8,144]{1,0:T(8,128)S(1)}, u32[]{:S(2)}, u32[]{:S(2)}) collective-permute-start(f32[8,144]{1,0:T(8,128)S(1)} %get-tuple-element.28), channel_id=1, source_target_pairs={{0,1},{1,2},{2,3},{3,4},{4,5},{5,6},{6,7},{7,0},{8,9},{9,10},{10,1... | collective-permute-start | bytes 13832 | tf_op jit(solution)/shard_map/ppermute | solution.py:398
  13.3 5.2 %collective-permute-start.3 = (f32[8,144]{1,0:T(8,128)S(1)}, f32[8,144]{1,0:T(8,128)S(1)}, u32[]{:S(2)}, u32[]{:S(2)}) collective-permute-start(f32[8,144]{1,0:T(8,128)S(1)} %get-tuple-element.29), channel_id=1, source_target_pairs={{1,0},{2,1},{3,2},{4,3},{5,4},{6,5},{7,6},{0,7},{9,8},{10,9},{11,1... | collective-permute-start | bytes 13832 | tf_op jit(solution)/shard_map/ppermute | solution.py:397
  15.8 2.6 %copy-start.2 = (bf16[96,512]{1,0:T(8,128)(2,1)S(1)}, bf16[96,512]{1,0:T(8,128)(2,1)}, u32[]{:S(2)}) copy-start(bf16[96,512]{1,0:T(8,128)(2,1)} %constant.16.clone.place_ref) | copy-start | bytes 294916
  15.9 2.6 %copy-start.3 = (s32[4,4]{1,0:T(4,128)S(1)}, s32[4,4]{1,0:T(4,128)}, u32[]{:S(2)}) copy-start(s32[4,4]{1,0:T(4,128)} %mask_ref.1) | copy-start | bytes 196
  15.9 2.6 %copy-start.4 = (s32[4,4]{1,0:T(4,128)S(1)}, s32[4,4]{1,0:T(4,128)}, u32[]{:S(2)}) copy-start(s32[4,4]{1,0:T(4,128)} %owner_ref.1) | copy-start | bytes 196

commit v5 on v4

--- a/solution.py
+++ b/solution.py
@@ -20,7 +20,8 @@
 FULL = CELLS + 2 * PAD
 LANES = 128
 BASES = 5
-BLOCK_ROWS = 48
+BLOCK_ROWS = 24
+SIDES, ENDS, GRAM = 16, 17, 18
 F32 = jnp.float32
 BF16 = jnp.bfloat16
 
@@ -248,7 +249,7 @@
 
 
 def base_kernel(mask_ref, owner_ref, main_ref, own_ref, from_left_ref, from_right_ref, place_ref, out_ref, field_ref,
-                base_ref, term_ref, gram_ref, pack_ref, tile_ref):
+                base_ref, term_ref, gram_ref, pack_ref, tile_ref, side_ref):
     lane = lax.broadcasted_iota(jnp.int32, (1, LANES), 1)
     received = jnp.concatenate([from_left_ref[...], from_right_ref[...], own_ref[...]], axis=0)
     placed = dot(jnp.concatenate(three_parts(received), axis=0), place_ref[...], (((0,), (0,)), ((), ())))
@@ -261,6 +262,8 @@
         centre = full[inner]
         left = jnp.where(lane == 0, rim, pltpu.roll(centre, 1, 1))
         right = jnp.where(lane == LANES - 1, rim, pltpu.roll(centre, LANES - 1, 1))
+        side_ref[f, 0] = left
+        side_ref[f, 1] = right
         dx = (right - left) * 0.5
         dy = (field_ref[f, PAD + 1 : PAD + 1 + CELLS] - field_ref[f, PAD - 1 : PAD - 1 + CELLS]) * 0.5
         slopes.append((centre, dx, dy))
@@ -296,20 +299,39 @@
     for a in range(grid):
         for e in range(grid):
             tile_ref[jnp.where(mask_ref[a, e] == 1, owner_ref[a, e], owners)] = a * grid + e
-    pack_ref[nothing] = jnp.zeros((8 * BASES, LANES), F32)
+    pack_ref[nothing] = jnp.zeros((BLOCK_ROWS, LANES), F32)
+    group = lane // SIDE
+    rows_of = lax.broadcasted_iota(jnp.int32, (8, LANES), 0)
     for a in range(grid):
-        for n in range(BASES):
-            pieces = [base_ref[n, pl.ds(a * SIDE + q, 8, stride=4), :] for q in range(grid)]
+        sides = [jnp.zeros((8, LANES), F32)] * grid
+        ends = []
+        for f in range(2):
+            pieces = [field_ref[f, pl.ds(PAD + a * SIDE + q, 8, stride=4), :] for q in range(grid)]
             for e in range(grid):
                 block = None
                 for q in range(grid):
                     x = pltpu.roll(pieces[q], (q - e) % grid * SIDE, 1) if q != e else pieces[q]
-                    block = x if block is None else jnp.where(lane // SIDE == q, x, block)
-                pack_ref[a * grid + e, 8 * n : 8 * n + 8] = block
+                    block = x if block is None else jnp.where(group == q, x, block)
+                pack_ref[a * grid + e, 8 * f : 8 * f + 8] = block
+            for side in range(2):
+                ends.append(field_ref[f, PAD + a * SIDE - 1 + side * (SIDE + 1) : PAD + a * SIDE + side * (SIDE + 1)])
+                for q in range(grid):
+                    x = side_ref[f, side, pl.ds(a * SIDE + q, 8, stride=4), :]
+                    here = lane == rows_of + (q * SIDE + 8 * side + 16 * f)
+                    for e in range(grid):
+                        at = e * SIDE + side * (SIDE - 1)
+                        sides[e] = jnp.where(here, x[:, at : at + 1], sides[e])
+        for e in range(grid):
+            pack_ref[a * grid + e, SIDES : SIDES + 1] = jnp.sum(sides[e], axis=0, keepdims=True)
+            row = None
+            for q in range(4):
+                x = pltpu.roll(ends[q], (q - e) % grid * SIDE, 1) if q != e else ends[q]
+                row = x if row is None else jnp.where(group == q, x, row)
+            pack_ref[a * grid + e, ENDS : ENDS + 1] = row
     for o in range(owners):
-        out_ref[o, : 8 * BASES] = pack_ref[tile_ref[o]]
+        out_ref[o] = pack_ref[tile_ref[o]]
         for h in range(2):
-            out_ref[o, 8 * BASES + h : 8 * BASES + h + 1] = halves[h]
+            out_ref[o, GRAM + h : GRAM + h + 1] = halves[h]
 
 
 def terms_of(base):
@@ -320,14 +342,33 @@
 
 def library_kernel(x_ref, out_hbm, gram_ref, out_ref, sem):
     slots = x_ref.shape[0] // BLOCK_ROWS
+    rows = lambda at: x_ref[pl.ds(at, slots, stride=BLOCK_ROWS), :]
+    turn_by = lambda x, count: pltpu.roll(x, count % LANES, 1) if count % LANES else x
+    lane = lax.broadcasted_iota(jnp.int32, (1, LANES), 1)
+    sides, ends = rows(SIDES), rows(ENDS)
+    fields = [[rows(8 * f + k) for k in range(8)] for f in range(2)]
+    lower = [[turn_by(x, SIDE) for x in field] for field in fields]
+    higher = [[turn_by(x, -SIDE) for x in field] for field in fields]
+
+    def slopes(f, k):
+        x = fields[f][k]
+        left = jnp.where(lane % SIDE == 0, turn_by(sides, -(k + 16 * f)), turn_by(x, 1))
+        right = jnp.where(lane % SIDE == SIDE - 1, turn_by(sides, SIDE - 1 - (k + 8 + 16 * f)), turn_by(x, -1))
+        before = lower[f][k - 1] if k else turn_by(ends, -64 * f)
+        after = higher[f][k + 1] if k < 7 else turn_by(ends, 64 - 64 * f)
+        up = jnp.where(lane < SIDE, before, lower[f][k])
+        down = jnp.where(lane >= LANES - SIDE, after, higher[f][k])
+        return (right - left) * 0.5, (down - up) * 0.5
+
     copies = []
     for k in range(8):
-        base = [x_ref[pl.ds(8 * n + k, slots, stride=BLOCK_ROWS), :] for n in range(BASES)]
+        (u_dx, u_dy), (v_dx, v_dy) = slopes(0, k), slopes(1, k)
+        base = [fields[0][k], fields[1][k], v_dx - u_dy, u_dy + v_dx, u_dx - v_dy]
         for n, x in enumerate(terms_of(base)):
             out_ref[k, pl.ds(n, slots, stride=TERMS), :] = x
         copies.append(pltpu.make_async_copy(out_ref.at[k], out_hbm.at[:, pl.ds(k * LANES, LANES)], sem.at[k]))
         copies[k].start()
-    totals = [jnp.sum(x_ref[pl.ds(40 + half, slots, stride=BLOCK_ROWS), :], axis=0, keepdims=True) for half in range(2)]
+    totals = [jnp.sum(rows(GRAM + half), axis=0, keepdims=True) for half in range(2)]
     for n in range(TERMS):
         row = totals[n // 8]
         row = pltpu.roll(row, LANES - n % 8 * TERMS, 1) if n % 8 else row
@@ -413,7 +454,8 @@
         out_specs=VMEM,
         scratch_shapes=[pltpu.VMEM((2, FULL, LANES), F32), pltpu.VMEM((BASES, CELLS, LANES), F32),
                         pltpu.VMEM((TERMS, CELLS, LANES), F32), pltpu.VMEM((TERMS * TERMS, LANES), F32),
-                        pltpu.VMEM((17, 8 * BASES, LANES), F32), pltpu.SMEM((tiles + 1,), jnp.int32)],
+                        pltpu.VMEM((17, BLOCK_ROWS, LANES), F32), pltpu.SMEM((tiles + 1,), jnp.int32),
+                        pltpu.VMEM((2, 2, CELLS, LANES), F32)],
         compiler_params=PARAMS,
         name="base_fields",
     )(ocean_mask, tile_owner, main, own, from_left, from_right, jnp.asarray(place_matrix()))

time: 48.3 us -> 46.6 us (0.965)
  blocking collectives: 26 us -> 23.9 us
    all_to_all x1, blocking collectives: 12.3 us -> 10.2 us  [per_device(): lax.all_to_all(blocks, 'tile', split_axis=0, concat_axis=0, tiled=True)]
where the time goes in v5:
time: 46.6 us; the launch traced here: 46.4 us
  blocking collectives  23.9 us (51%)
  Pallas kernels  10.6 us (23%)
  starting transfers between devices  10.5 us (23%)
  between operations  0.74 us (2%)
  other arithmetic  0.61 us (1%)
    all_to_all x1, blocking collectives, per_device(): gram = lax.all_to_all(gram, 'col', split_axis=0, concat_axis=0, tiled=True)  13.7 us
    all_to_all x1, blocking collectives, per_device(): lax.all_to_all(blocks, 'tile', split_axis=0, concat_axis=0, tiled=True)  10.2 us
    ppermute x1, starting transfers between devices, per_device(): from_left = lax.ppermute(to_right, 'col', onward(columns))  4.03 us
    ppermute x1, starting transfers between devices, per_device(): below = lax.ppermute(up, 'tile', back(tiles))  3.84 us
    pallas_call x1, Pallas kernels, per_device(): pl.pallas_call(prepare_kernel, out_shape=[jax.ShapeDtypeStruct((rows, 2 *...  2.73 us
    ppermute x1, starting transfers between devices, per_device(): from_right = lax.ppermute(to_left, 'col', back(columns))  2.53 us
    pallas_call x1, Pallas kernels, per_device(): pl.pallas_call(main_kernel, out_shape=struct(2, FULL, LANES), in_specs=[V...  2.53 us
    pallas_call x1, Pallas kernels, per_device(): pl.pallas_call(base_kernel, out_shape=struct(tiles, BLOCK_ROWS, LANES), i...  2.18 us
  transfers between devices with their start and end apart: 4, of which 1 were waited for; matrix products, arithmetic and copies ran while one was open for 0% of the time, Pallas kernels for 11%

profile of v5, /device:TPU:0, one launch (start us, length us, event | category | flops | bytes accessed | tf_op | source)
XLA Modules:
  0.0 46.4 jit_solution(1398515739632350030)
XLA Ops:
  0.6 0.0 copy-start.1
  0.6 0.0 copy-start
  0.7 1.0 %send_rows.1 = (f32[24,512]{1,0:T(8,128)S(1)}, f32[24,512]{1,0:T(8,128)S(1)}) custom-call(s32[1]{0:T(128)} %bitcast.here_ref, s32[16]{0:T(128)} %turns_hbm.1, f32[512,512]{1,0:T(8,128)} %refs_3_, f32[512,512]{1,0:T(8,128)} %refs_7_), custom_call_target="tpu_custom_call" | custom-call | tf_op jit(solution)/shard_map/send_rows/pallas_call | solution.py:397
  1.7 0.1 collective-permute-start
  1.8 3.8 %collective-permute-start.1 = (f32[24,512]{1,0:T(8,128)S(1)}, f32[24,512]{1,0:T(8,128)S(1)}, u32[]{:S(2)}, u32[]{:S(2)}) collective-permute-start(f32[24,512]{1,0:T(8,128)S(1)} %get-tuple-element.25), channel_id=1, source_target_pairs={{8,0},{16,8},{24,16},{32,24},{40,32},{48,40},{56,48},{64,56},{72,6... | collective-permute-start | bytes 147464 | tf_op jit(solution)/shard_map/ppermute | solution.py:409
  5.6 0.0 copy-done.1
  5.6 0.0 copy-done
  5.6 2.7 %prepare_rows.1 = (bf16[1024,1024]{1,0:T(8,128)(2,1)S(1)}, bf16[512,1280]{1,0:T(8,128)(2,1)S(1)}, f32[144,128]{1,0:T(8,128)S(1)}, f32[1024,512]{1,0:T(8,128)S(1)}) custom-call(f32[512,512]{1,0:T(8,128)S(1)} %copy-done, f32[512,512]{1,0:T(8,128)S(1)} %copy-done, f32[512,512]{1,0:T(8,128)S(1)} %copy-done, f32[512,512]{1,0:T(8,128)S(1)} %copy-done, ...), custom_call_target="tpu_custom_call" | custom-call | tf_op jit(solution)/shard_map/prepare_rows/pallas_call | solution.py:414
  8.4 0.0 collective-permute-done.above_ref
  8.4 0.0 collective-permute-done.1.below_ref
  8.4 0.9 %rim_columns.1 = (f32[8,144]{1,0:T(8,128)S(1)}, f32[8,144]{1,0:T(8,128)S(1)}, f32[16,144]{1,0:T(8,128)S(1)}) custom-call(f32[24,512]{1,0:T(8,128)S(1)} %collective-permute-done.above_ref, f32[24,512]{1,0:T(8,128)S(1)} %collective-permute-done.1.below_ref, bf16[512,1280]{1,0:T(8,128)(2,1)S(1)} %get-tuple-element.23.w_ref, f32[144,128]{1,0:T(8,128)S(1)} %get-tuple-element.26.rim_in), custom_call_target="tpu_custom_call" | custom-call | tf_op jit(solution)/shard_map/rim_columns/pallas_call | solution.py:427
  9.3 4.0 %collective-permute-start.2 = (f32[8,144]{1,0:T(8,128)S(1)}, f32[8,144]{1,0:T(8,128)S(1)}, u32[]{:S(2)}, u32[]{:S(2)}) collective-permute-start(f32[8,144]{1,0:T(8,128)S(1)} %get-tuple-element.28), channel_id=1, source_target_pairs={{0,1},{1,2},{2,3},{3,4},{4,5},{5,6},{6,7},{7,0},{8,9},{9,10},{10,1... | collective-permute-start | bytes 13832 | tf_op jit(solution)/shard_map/ppermute | solution.py:439
  13.3 2.5 %collective-permute-start.3 = (f32[8,144]{1,0:T(8,128)S(1)}, f32[8,144]{1,0:T(8,128)S(1)}, u32[]{:S(2)}, u32[]{:S(2)}) collective-permute-start(f32[8,144]{1,0:T(8,128)S(1)} %get-tuple-element.29), channel_id=1, source_target_pairs={{1,0},{2,1},{3,2},{4,3},{5,4},{6,5},{7,6},{0,7},{9,8},{10,9},{11,1... | collective-permute-start | bytes 13832 | tf_op jit(solution)/shard_map/ppermute | solution.py:438
  15.8 0.0 copy-start.2
  15.9 0.0 copy-start.3
  15.9 0.0 copy-start.4
  15.9 2.5 %main_columns.1.main_ref = f32[2,144,128]{2,1,0:T(8,128)S(1)} custom-call(bf16[1024,1024]{1,0:T(8,128)(2,1)S(1)} %get-tuple-element.21.parts_ref, f32[1024,512]{1,0:T(8,128)S(1)} %get-tuple-element.22.early_ref, bf16[512,1280]{1,0:T(8,128)(2,1)S(1)} %get-tuple-element.23.w_ref, f32[24,512]{1,0:T(8,128)S(1)} %collective-permute-done.above_ref, ...), custom_call_target="tpu_custom_call" | custom-call | tf_op jit(solution)/shard_map/main_columns/pallas_call | solution.py:440
  18.4 0.0 collective-permute-done.2.from_left_ref
  18.4 0.1 collective-permute-done.3.from_right_ref
  18.5 0.0 copy-done.2
  18.5 0.0 copy-done.3
  18.5 0.0 copy-done.4
  18.5 2.2 %base_fields.1 = f32[16,24,128]{2,1,0:T(8,128)S(1)} custom-call(s32[4,4]{1,0:T(4,128)S(1)} %copy-done.3, s32[4,4]{1,0:T(4,128)S(1)} %copy-done.4, f32[2,144,128]{2,1,0:T(8,128)S(1)} %main_columns.1.main_ref, f32[16,144]{1,0:T(8,128)S(1)} %get-tuple-element.27._.own_ref, f32[8,144]{1,0:T(8,128)S(1)} %collective-permute-done.2.from_left_ref, ...), custom_call_target="tpu_custom_call" | custom-call | tf_op jit(solution)/shard_map/base_fields/pallas_call | solution.py:450
  20.7 10.2 %all_to_all.10 = f32[16,24,128]{2,1,0:T(8,128)S(1)} all-to-all(f32[16,24,128]{2,1,0:T(8,128)S(1)} %base_fields.1), channel_id=1, replica_groups=mesh['tile'=16,'col'=8] {'tile'}, dimensions={0} | all-to-all | bytes 393216 | tf_op jit(solution)/shard_map/all_to_all | solution.py:462
  30.9 1.2 %library_terms.1 = (f32[256,1024]{1,0:T(8,128)}, f32[8,16,128]{2,1,0:T(8,128)S(1)}) custom-call(f32[384,128]{1,0:T(8,128)S(1)} %bitcast.3), custom_call_target="tpu_custom_call" | custom-call | tf_op jit(solution)/shard_map/library_terms/pallas_call | solution.py:463
  32.1 13.7 %all_to_all.11 = f32[8,16,128]{2,1,0:T(8,128)S(1)} all-to-all(f32[8,16,128]{2,1,0:T(8,128)S(1)} %get-tuple-element.31), channel_id=1, replica_groups=mesh['tile'=16,'col'=8] {'col'}, dimensions={0} | all-to-all | bytes 131072 | tf_op jit(solution)/shard_map/all_to_all | solution.py:472
  45.8 0.6 %slice_multiply_fusion = f32[16,16]{1,0:T(8,128)} fusion(f32[16,128]{1,0:T(8,128)S(1)} %reduce_sum.9), kind=kLoop, calls=%fused_computation | loop fusion | flops 256 | bytes 2048 | tf_op jit(solution)/shard_map/div | solution.py:473
  (1 shorter events, 0.0 us)
Async XLA Ops:
  0.6 5.0 %copy-start.1 = (f32[512,512]{1,0:T(8,128)S(1)}, f32[512,512]{1,0:T(8,128)}, u32[]{:S(2)}) copy-start(f32[512,512]{1,0:T(8,128)} %refs_7_) | copy-start | bytes 3145732
  0.6 5.0 %copy-start = (f32[512,512]{1,0:T(8,128)S(1)}, f32[512,512]{1,0:T(8,128)}, u32[]{:S(2)}) copy-start(f32[512,512]{1,0:T(8,128)} %refs_3_) | copy-start | bytes 3145732
  1.7 6.7 %collective-permute-start = (f32[24,512]{1,0:T(8,128)S(1)}, f32[24,512]{1,0:T(8,128)S(1)}, u32[]{:S(2)}, u32[]{:S(2)}) collective-permute-start(f32[24,512]{1,0:T(8,128)S(1)} %get-tuple-element.24), channel_id=1, source_target_pairs={{0,8},{8,16},{16,24},{24,32},{32,40},{40,48},{48,56},{56,64},{64,7... | collective-permute-start | bytes 147464 | tf_op jit(solution)/shard_map/ppermute | solution.py:408
  1.8 6.6 %collective-permute-start.1 = (f32[24,512]{1,0:T(8,128)S(1)}, f32[24,512]{1,0:T(8,128)S(1)}, u32[]{:S(2)}, u32[]{:S(2)}) collective-permute-start(f32[24,512]{1,0:T(8,128)S(1)} %get-tuple-element.25), channel_id=1, source_target_pairs={{8,0},{16,8},{24,16},{32,24},{40,32},{48,40},{56,48},{64,56},{72,6... | collective-permute-start | bytes 147464 | tf_op jit(solution)/shard_map/ppermute | solution.py:409
  9.3 9.1 %collective-permute-start.2 = (f32[8,144]{1,0:T(8,128)S(1)}, f32[8,144]{1,0:T(8,128)S(1)}, u32[]{:S(2)}, u32[]{:S(2)}) collective-permute-start(f32[8,144]{1,0:T(8,128)S(1)} %get-tuple-element.28), channel_id=1, source_target_pairs={{0,1},{1,2},{2,3},{3,4},{4,5},{5,6},{6,7},{7,0},{8,9},{9,10},{10,1... | collective-permute-start | bytes 13832 | tf_op jit(solution)/shard_map/ppermute | solution.py:439
  13.3 5.2 %collective-permute-start.3 = (f32[8,144]{1,0:T(8,128)S(1)}, f32[8,144]{1,0:T(8,128)S(1)}, u32[]{:S(2)}, u32[]{:S(2)}) collective-permute-start(f32[8,144]{1,0:T(8,128)S(1)} %get-tuple-element.29), channel_id=1, source_target_pairs={{1,0},{2,1},{3,2},{4,3},{5,4},{6,5},{7,6},{0,7},{9,8},{10,9},{11,1... | collective-permute-start | bytes 13832 | tf_op jit(solution)/shard_map/ppermute | solution.py:438
  15.8 2.6 %copy-start.2 = (bf16[96,512]{1,0:T(8,128)(2,1)S(1)}, bf16[96,512]{1,0:T(8,128)(2,1)}, u32[]{:S(2)}) copy-start(bf16[96,512]{1,0:T(8,128)(2,1)} %constant.16.clone.place_ref) | copy-start | bytes 294916
  15.9 2.6 %copy-start.3 = (s32[4,4]{1,0:T(4,128)S(1)}, s32[4,4]{1,0:T(4,128)}, u32[]{:S(2)}) copy-start(s32[4,4]{1,0:T(4,128)} %mask_ref.1) | copy-start | bytes 196
  15.9 2.6 %copy-start.4 = (s32[4,4]{1,0:T(4,128)S(1)}, s32[4,4]{1,0:T(4,128)}, u32[]{:S(2)}) copy-start(s32[4,4]{1,0:T(4,128)} %owner_ref.1) | copy-start | bytes 196

commit v6 on v5

--- a/solution.py
+++ b/solution.py
@@ -142,7 +142,7 @@
             to_ref[f * HALO : (f + 1) * HALO] = x[start : start + HALO]
 
 
-EARLY = 4
+EARLY = 8
 
 
 def prepare_kernel(*refs):
@@ -190,7 +190,7 @@
             for p in range(POOL):
                 spot = ((f * 2 + s) * POOL + p) * 8 + start
                 strip_ref[spot : spot + 3] = rows_ref[s, pl.ds(f * HALO + p, 3, stride=POOL), :]
-    z = dot(jnp.concatenate(two_parts(strip_ref[...]), axis=1), w_ref[...])
+    z = dot(jnp.concatenate(two_parts(strip_ref[...]), axis=1), w_ref[: 2 * LANES, 9 * LANES :])
     rim_ref[...] = rim_in[...]
     for s, (spot, start) in enumerate(((7, 3), (PAD + CELLS - 2, 2))):
         first = []
@@ -211,7 +211,18 @@
                 to_ref[spot : spot + 1] = turned[64 * f + c : 64 * f + c + 1]
 
 
-def main_kernel(parts_ref, early_ref, w_ref, above_ref, below_ref, _, main_ref, rows_ref, strip_ref, sum_ref):
+PAIRS = [(n, m) for n in range(TERMS) for m in range(n, TERMS)]
+REACH = 3
+
+
+def slopes_of(ref, f, left, right):
+    up = ref[f, PAD - 1 : PAD - 1 + CELLS]
+    down = ref[f, PAD + 1 : PAD + 1 + CELLS]
+    return (right - left) * 0.5, (down - up) * 0.5
+
+
+def main_kernel(mask_ref, parts_ref, early_ref, w_ref, above_ref, below_ref, _, main_ref, live_ref, inner_ref, rows_ref,
+                strip_ref, sum_ref, term_ref):
     strip_ref[...] = jnp.zeros_like(strip_ref)
     for s, (x_ref, start) in enumerate(((above_ref, 5), (below_ref, 8))):
         for c in range(4):
@@ -246,10 +257,33 @@
                     sum_ref[f, p] = own[p]
     for f in range(2):
         main_ref[f] = ((sum_ref[f, 0] + sum_ref[f, 1]) + (sum_ref[f, 2] + sum_ref[f, 3])) * SCALE
-
-
-def base_kernel(mask_ref, owner_ref, main_ref, own_ref, from_left_ref, from_right_ref, place_ref, out_ref, field_ref,
-                base_ref, term_ref, gram_ref, pack_ref, tile_ref, side_ref):
+    lane = lax.broadcasted_iota(jnp.int32, (1, LANES), 1)
+    grid = CELLS // SIDE
+    for a in range(grid):
+        row = jnp.zeros((1, LANES), F32)
+        for e in range(grid):
+            row = jnp.where(lane // SIDE == e, (mask_ref[a, e] == 1).astype(F32), row)
+        live_ref[a * SIDE : (a + 1) * SIDE] = jnp.broadcast_to(row, (SIDE, LANES))
+    keep = (live_ref[...] > 0.5) & (lane >= REACH) & (lane < LANES - REACH)
+    u, v = [main_ref[f, PAD : PAD + CELLS] for f in range(2)]
+    (u_dx, u_dy), (v_dx, v_dy) = [slopes_of(main_ref, f, pltpu.roll(x, 1, 1), pltpu.roll(x, LANES - 1, 1))
+                                  for f, x in enumerate((u, v))]
+    for n, x in enumerate((u, v, v_dx - u_dy, u_dy + v_dx, u_dx - v_dy)):
+        term_ref[n] = jnp.where(keep, x, 0.0)
+    for n, x in enumerate(terms_of([term_ref[n] for n in range(BASES)])):
+        if n >= BASES:
+            term_ref[n] = x
+    for place, (n, m) in enumerate(PAIRS):
+        product = (term_ref[n] * term_ref[m]).reshape(CELLS // 8, 8, LANES)
+        inner_ref[place] = jnp.sum(product, axis=0)
+
+
+def base_kernel(mask_vmem, owner_vmem, main_ref, live_ref, inner_ref, own_ref, from_left_ref, from_right_ref, place_ref,
+                out_ref, field_ref, gram_ref, pack_ref, tile_ref, side_ref, mask_ref, owner_ref, sem):
+    tables = [pltpu.make_async_copy(mask_vmem, mask_ref, sem.at[0]),
+              pltpu.make_async_copy(owner_vmem, owner_ref, sem.at[1])]
+    for table in tables:
+        table.start()
     lane = lax.broadcasted_iota(jnp.int32, (1, LANES), 1)
     received = jnp.concatenate([from_left_ref[...], from_right_ref[...], own_ref[...]], axis=0)
     placed = dot(jnp.concatenate(three_parts(received), axis=0), place_ref[...], (((0,), (0,)), ((), ())))
@@ -264,36 +298,31 @@
         right = jnp.where(lane == LANES - 1, rim, pltpu.roll(centre, LANES - 1, 1))
         side_ref[f, 0] = left
         side_ref[f, 1] = right
-        dx = (right - left) * 0.5
-        dy = (field_ref[f, PAD + 1 : PAD + 1 + CELLS] - field_ref[f, PAD - 1 : PAD - 1 + CELLS]) * 0.5
-        slopes.append((centre, dx, dy))
+        slopes.append((centre, *slopes_of(field_ref, f, left, right)))
     (u, u_dx, u_dy), (v, v_dx, v_dy) = slopes
-    grid = CELLS // SIDE
-    rows = []
-    for a in range(grid):
-        row = jnp.zeros((1, LANES), F32)
-        for e in range(grid):
-            row = jnp.where(lane // SIDE == e, (mask_ref[a, e] == 1).astype(F32), row)
-        rows.append(jnp.broadcast_to(row, (SIDE, LANES)))
-    live = jnp.concatenate(rows, axis=0) > 0.5
-    for n, x in enumerate((u, v, v_dx - u_dy, u_dy + v_dx, u_dx - v_dy)):
-        base_ref[n] = jnp.where(live, x, 0.0)
-    for n, x in enumerate(terms_of([base_ref[n] for n in range(BASES)])):
-        term_ref[n] = x
-    for n in range(TERMS):
-        first = term_ref[n]
-        for m in range(n, TERMS):
-            product = (first * term_ref[m]).reshape(CELLS // 8, 8, LANES)
-            total = jnp.sum(jnp.sum(product, axis=0), axis=0, keepdims=True)
-            gram_ref[n * TERMS + m : n * TERMS + m + 1] = total
-            if m > n:
-                gram_ref[m * TERMS + n : m * TERMS + n + 1] = total
+    live = live_ref[...] > 0.5
+    outer = []
+    for x in (u, v, v_dx - u_dy, u_dy + v_dx, u_dx - v_dy):
+        x = jnp.where(live, x, 0.0)
+        tile = jnp.zeros((8, LANES), F32)
+        for b in range(CELLS // 8):
+            tile = jnp.where(lane // 8 == b, pltpu.roll(x[8 * b : 8 * b + 8], (REACH + 8 * b) % LANES, 1), tile)
+        outer.append(jnp.where(lane % 8 < 2 * REACH, tile, 0.0))
+    outer = terms_of(outer)
+    for place, (n, m) in enumerate(PAIRS):
+        total = jnp.sum(inner_ref[place] + outer[n] * outer[m], axis=0, keepdims=True)
+        gram_ref[n * TERMS + m : n * TERMS + m + 1] = total
+        if m > n:
+            gram_ref[m * TERMS + n : m * TERMS + n + 1] = total
     totals = jnp.sum(gram_ref[...], axis=1, keepdims=True)
     row = lax.broadcasted_iota(jnp.int32, (TERMS * TERMS, 1), 0)
     spread = jnp.where(row % LANES == lane, totals, 0.0)
     halves = [jnp.sum(spread[h * LANES : (h + 1) * LANES], axis=0, keepdims=True) for h in range(2)]
     owners = out_ref.shape[0]
+    grid = CELLS // SIDE
     nothing = grid * grid
+    for table in tables:
+        table.wait()
     for o in range(owners + 1):
         tile_ref[o] = nothing
     for a in range(grid):
@@ -408,8 +437,6 @@
     above = lax.ppermute(down, "tile", onward(tiles))
     below = lax.ppermute(up, "tile", back(tiles))
     column = lambda c: pl.BlockSpec((POOL * CELLS, LANES), lambda i: (0, c))
-    whole = lambda *shape: pl.BlockSpec(shape, lambda i: (0,) * len(shape))
-    halo = whole(2 * HALO, POOL * CELLS)
     rows = 2 * POOL * CELLS
     parts, weights, rim, early = pl.pallas_call(
         prepare_kernel,
@@ -427,9 +454,8 @@
     to_left, to_right, own = pl.pallas_call(
         rim_kernel,
         out_shape=[struct(8, FULL), struct(8, FULL), struct(16, FULL)],
-        grid=(1,),
-        in_specs=[halo] * 2 + [pl.BlockSpec((2 * LANES, LANES), lambda i: (0, 9)), whole(FULL, LANES)],
-        out_specs=[whole(8, FULL), whole(8, FULL), whole(16, FULL)],
+        in_specs=[VMEM] * 4,
+        out_specs=[VMEM] * 3,
         scratch_shapes=[pltpu.VMEM((2, 2 * HALO, LANES), F32), pltpu.VMEM((2 * 2 * POOL * 8, LANES), F32),
                         pltpu.VMEM((FULL, LANES), F32)],
         compiler_params=PARAMS,
@@ -437,28 +463,28 @@
     )(above, below, weights, rim)
     from_right = lax.ppermute(to_left, "col", back(columns))
     from_left = lax.ppermute(to_right, "col", onward(columns))
-    main = pl.pallas_call(
+    main, live, inner = pl.pallas_call(
         main_kernel,
-        out_shape=struct(2, FULL, LANES),
-        in_specs=[VMEM] * 6,
-        out_specs=VMEM,
+        out_shape=[struct(2, FULL, LANES), struct(CELLS, LANES), struct(len(PAIRS), 8, LANES)],
+        in_specs=[SMEM] + [VMEM] * 6,
+        out_specs=[VMEM] * 3,
         scratch_shapes=[pltpu.VMEM((2, 4, 2 * HALO, LANES), F32), pltpu.VMEM((2 * POOL * 16, POOL * CELLS), F32),
-                        pltpu.VMEM((2, POOL, FULL, LANES), F32)],
+                        pltpu.VMEM((2, POOL, FULL, LANES), F32), pltpu.VMEM((TERMS, CELLS, LANES), F32)],
         compiler_params=PARAMS,
         name="main_columns",
-    )(parts, early, weights, above, below, own)
+    )(ocean_mask, parts, early, weights, above, below, own)
     blocks = pl.pallas_call(
         base_kernel,
         out_shape=struct(tiles, BLOCK_ROWS, LANES),
-        in_specs=[SMEM] * 2 + [VMEM] * 5,
+        in_specs=[VMEM] * 9,
         out_specs=VMEM,
-        scratch_shapes=[pltpu.VMEM((2, FULL, LANES), F32), pltpu.VMEM((BASES, CELLS, LANES), F32),
-                        pltpu.VMEM((TERMS, CELLS, LANES), F32), pltpu.VMEM((TERMS * TERMS, LANES), F32),
+        scratch_shapes=[pltpu.VMEM((2, FULL, LANES), F32), pltpu.VMEM((TERMS * TERMS, LANES), F32),
                         pltpu.VMEM((17, BLOCK_ROWS, LANES), F32), pltpu.SMEM((tiles + 1,), jnp.int32),
-                        pltpu.VMEM((2, 2, CELLS, LANES), F32)],
+                        pltpu.VMEM((2, 2, CELLS, LANES), F32), pltpu.SMEM(ocean_mask.shape, jnp.int32),
+                        pltpu.SMEM(tile_owner.shape, jnp.int32), pltpu.SemaphoreType.DMA((2,))],
         compiler_params=PARAMS,
         name="base_fields",
-    )(ocean_mask, tile_owner, main, own, from_left, from_right, jnp.asarray(place_matrix()))
+    )(ocean_mask, tile_owner, main, live, inner, own, from_left, from_right, jnp.asarray(place_matrix()))
     blocks = lax.all_to_all(blocks, "tile", split_axis=0, concat_axis=0, tiled=True)
     library, gram = pl.pallas_call(
         library_kernel,

time: 46.6 us -> 47.2 us (1.013)
  Pallas kernels: 10.6 us -> 11.2 us
    pallas_call x1, Pallas kernels: 2.73 us -> 3.82 us  [per_device(): pl.pallas_call(prepare_kernel, out_shape=[jax.ShapeDtypeStruct((rows, 2 *...]
    pallas_call x1, Pallas kernels: 2.18 us -> 1.65 us  [per_device(): pl.pallas_call(base_kernel, out_shape=struct(tiles, BLOCK_ROWS, LANES), i...]
  transfers between devices with their start and end apart: 4 -> 4, of which waited for: 1 -> 0; matrix products, arithmetic and copies ran while one was open for 0% -> 0% of each run, Pallas kernels for 11% -> 14%
where the time goes in v6:
time: 47.2 us; the launch traced here: 46.9 us
  blocking collectives  23.8 us (50%)
  Pallas kernels  11.2 us (24%)
  starting transfers between devices  10.5 us (22%)
  between operations  0.77 us (2%)
  other arithmetic  0.61 us (1%)
    all_to_all x1, blocking collectives, per_device(): gram = lax.all_to_all(gram, 'col', split_axis=0, concat_axis=0, tiled=True)  13.8 us
    all_to_all x1, blocking collectives, per_device(): lax.all_to_all(blocks, 'tile', split_axis=0, concat_axis=0, tiled=True)  10.1 us
    ppermute x1, starting transfers between devices, per_device(): from_left = lax.ppermute(to_right, 'col', onward(columns))  4.03 us
    ppermute x1, starting transfers between devices, per_device(): below = lax.ppermute(up, 'tile', back(tiles))  3.84 us
    pallas_call x1, Pallas kernels, per_device(): pl.pallas_call(prepare_kernel, out_shape=[jax.ShapeDtypeStruct((rows, 2 *...  3.82 us
    pallas_call x1, Pallas kernels, per_device(): pl.pallas_call(main_kernel, out_shape=[struct(2, FULL, LANES), struct(CEL...  2.6 us
    ppermute x1, starting transfers between devices, per_device(): from_right = lax.ppermute(to_left, 'col', back(columns))  2.53 us
    pallas_call x1, Pallas kernels, per_device(): pl.pallas_call(base_kernel, out_shape=struct(tiles, BLOCK_ROWS, LANES), i...  1.65 us
  transfers between devices with their start and end apart: 4, of which 0 were waited for; matrix products, arithmetic and copies ran while one was open for 0% of the time, Pallas kernels for 14%

profile of v6, /device:TPU:0, one launch (start us, length us, event | category | flops | bytes accessed | tf_op | source)
XLA Modules:
  0.0 46.9 jit_solution(8351777107929285232)
XLA Ops:
  0.6 0.0 copy-start.1
  0.6 0.0 copy-start
  0.7 1.0 %send_rows.1 = (f32[24,512]{1,0:T(8,128)S(1)}, f32[24,512]{1,0:T(8,128)S(1)}) custom-call(s32[1]{0:T(128)} %bitcast.here_ref, s32[16]{0:T(128)} %turns_hbm.1, f32[512,512]{1,0:T(8,128)} %refs_3_, f32[512,512]{1,0:T(8,128)} %refs_7_), custom_call_target="tpu_custom_call" | custom-call | tf_op jit(solution)/shard_map/send_rows/pallas_call | solution.py:426
  1.7 0.0 copy-start.3
  1.7 0.1 collective-permute-start
  1.8 3.8 %collective-permute-start.1 = (f32[24,512]{1,0:T(8,128)S(1)}, f32[24,512]{1,0:T(8,128)S(1)}, u32[]{:S(2)}, u32[]{:S(2)}) collective-permute-start(f32[24,512]{1,0:T(8,128)S(1)} %get-tuple-element.28), channel_id=1, source_target_pairs={{8,0},{16,8},{24,16},{32,24},{40,32},{48,40},{56,48},{64,56},{72,6... | collective-permute-start | bytes 147464 | tf_op jit(solution)/shard_map/ppermute | solution.py:438
  5.6 0.0 copy-done.1
  5.6 0.0 copy-done
  5.6 3.8 %prepare_rows.1 = (bf16[1024,1024]{1,0:T(8,128)(2,1)S(1)}, bf16[512,1280]{1,0:T(8,128)(2,1)S(1)}, f32[144,128]{1,0:T(8,128)S(1)}, f32[1024,1024]{1,0:T(8,128)S(1)}) custom-call(f32[512,512]{1,0:T(8,128)S(1)} %copy-done, f32[512,512]{1,0:T(8,128)S(1)} %copy-done, f32[512,512]{1,0:T(8,128)S(1)} %copy-done, f32[512,512]{1,0:T(8,128)S(1)} %copy-done, ...), custom_call_target="tpu_custom_call" | custom-call | tf_op jit(solution)/shard_map/prepare_rows/pallas_call | solution.py:441
  9.4 0.0 collective-permute-done.above_ref
  9.5 0.0 collective-permute-done.1.below_ref
  9.5 0.9 %rim_columns.1 = (f32[8,144]{1,0:T(8,128)S(1)}, f32[8,144]{1,0:T(8,128)S(1)}, f32[16,144]{1,0:T(8,128)S(1)}) custom-call(f32[24,512]{1,0:T(8,128)S(1)} %collective-permute-done.above_ref, f32[24,512]{1,0:T(8,128)S(1)} %collective-permute-done.1.below_ref, bf16[512,1280]{1,0:T(8,128)(2,1)S(1)} %get-tuple-element.26.w_ref, f32[144,128]{1,0:T(8,128)S(1)} %get-tuple-element.29.rim_in), custom_call_target="tpu_custom_call" | custom-call | tf_op jit(solution)/shard_map/rim_columns/pallas_call | solution.py:454
  10.4 4.0 %collective-permute-start.2 = (f32[8,144]{1,0:T(8,128)S(1)}, f32[8,144]{1,0:T(8,128)S(1)}, u32[]{:S(2)}, u32[]{:S(2)}) collective-permute-start(f32[8,144]{1,0:T(8,128)S(1)} %get-tuple-element.34), channel_id=1, source_target_pairs={{0,1},{1,2},{2,3},{3,4},{4,5},{5,6},{6,7},{7,0},{8,9},{9,10},{10,1... | collective-permute-start | bytes 13832 | tf_op jit(solution)/shard_map/ppermute | solution.py:465
  14.4 2.5 %collective-permute-start.3 = (f32[8,144]{1,0:T(8,128)S(1)}, f32[8,144]{1,0:T(8,128)S(1)}, u32[]{:S(2)}, u32[]{:S(2)}) collective-permute-start(f32[8,144]{1,0:T(8,128)S(1)} %get-tuple-element.35), channel_id=1, source_target_pairs={{1,0},{2,1},{3,2},{4,3},{5,4},{6,5},{7,6},{0,7},{9,8},{10,9},{11,1... | collective-permute-start | bytes 13832 | tf_op jit(solution)/shard_map/ppermute | solution.py:464
  16.9 0.0 copy-done.3
  16.9 0.0 copy-start.2
  16.9 0.0 copy-start.4
  16.9 2.6 %main_columns.1 = (f32[2,144,128]{2,1,0:T(8,128)S(1)}, f32[128,128]{1,0:T(8,128)S(1)}, f32[136,8,128]{2,1,0:T(8,128)S(1)}) custom-call(s32[4,4]{1,0:T(4,128)S(1)} %copy-done.3, bf16[1024,1024]{1,0:T(8,128)(2,1)S(1)} %get-tuple-element.24.parts_ref, f32[1024,1024]{1,0:T(8,128)S(1)} %get-tuple-element.25.early_ref, ...), custom_call_target="tpu_custom_call" | custom-call | tf_op jit(solution)/shard_map/main_columns/pallas_call | solution.py:466
  19.6 0.0 collective-permute-done.2.from_left_ref
  19.6 0.0 collective-permute-done.3.from_right_ref
  19.6 0.0 copy-done.2
  19.6 0.0 copy-done.4
  19.6 1.7 %base_fields.1 = f32[16,24,128]{2,1,0:T(8,128)S(1)} custom-call(s32[4,4]{1,0:T(4,128)S(1)} %copy-done.3, s32[4,4]{1,0:T(4,128)S(1)} %copy-done.4, f32[2,144,128]{2,1,0:T(8,128)S(1)} %get-tuple-element.31.main_ref, f32[128,128]{1,0:T(8,128)S(1)} %get-tuple-element.32.live_ref, f32[136,8,128]{2,1,0:T(8,128)S(1)} %get-tuple-element.33.inner_ref, ...), custom_call_target="tpu_custom_call" | custom-call | tf_op jit(solution)/shard_map/base_fields/pallas_call | solution.py:476
  21.3 10.1 %all_to_all.10 = f32[16,24,128]{2,1,0:T(8,128)S(1)} all-to-all(f32[16,24,128]{2,1,0:T(8,128)S(1)} %base_fields.1), channel_id=1, replica_groups=mesh['tile'=16,'col'=8] {'tile'}, dimensions={0} | all-to-all | bytes 393216 | tf_op jit(solution)/shard_map/all_to_all | solution.py:488
  31.3 1.2 %library_terms.1 = (f32[256,1024]{1,0:T(8,128)}, f32[8,16,128]{2,1,0:T(8,128)S(1)}) custom-call(f32[384,128]{1,0:T(8,128)S(1)} %bitcast.3), custom_call_target="tpu_custom_call" | custom-call | tf_op jit(solution)/shard_map/library_terms/pallas_call | solution.py:489
  32.5 13.8 %all_to_all.11 = f32[8,16,128]{2,1,0:T(8,128)S(1)} all-to-all(f32[8,16,128]{2,1,0:T(8,128)S(1)} %get-tuple-element.37), channel_id=1, replica_groups=mesh['tile'=16,'col'=8] {'col'}, dimensions={0} | all-to-all | bytes 131072 | tf_op jit(solution)/shard_map/all_to_all | solution.py:498
  46.3 0.6 %slice_multiply_fusion = f32[16,16]{1,0:T(8,128)} fusion(f32[16,128]{1,0:T(8,128)S(1)} %reduce_sum.9), kind=kLoop, calls=%fused_computation | loop fusion | flops 256 | bytes 2048 | tf_op jit(solution)/shard_map/div | solution.py:499
  (1 shorter events, 0.0 us)
Async XLA Ops:
  0.6 5.0 %copy-start.1 = (f32[512,512]{1,0:T(8,128)S(1)}, f32[512,512]{1,0:T(8,128)}, u32[]{:S(2)}) copy-start(f32[512,512]{1,0:T(8,128)} %refs_7_) | copy-start | bytes 3145732
  0.6 5.0 %copy-start = (f32[512,512]{1,0:T(8,128)S(1)}, f32[512,512]{1,0:T(8,128)}, u32[]{:S(2)}) copy-start(f32[512,512]{1,0:T(8,128)} %refs_3_) | copy-start | bytes 3145732
  1.7 15.3 %copy-start.3 = (s32[4,4]{1,0:T(4,128)S(1)}, s32[4,4]{1,0:T(4,128)}, u32[]{:S(2)}) copy-start(s32[4,4]{1,0:T(4,128)} %mask_vmem.1) | copy-start | bytes 196
  1.7 7.8 %collective-permute-start = (f32[24,512]{1,0:T(8,128)S(1)}, f32[24,512]{1,0:T(8,128)S(1)}, u32[]{:S(2)}, u32[]{:S(2)}) collective-permute-start(f32[24,512]{1,0:T(8,128)S(1)} %get-tuple-element.27), channel_id=1, source_target_pairs={{0,8},{8,16},{16,24},{24,32},{32,40},{40,48},{48,56},{56,64},{64,7... | collective-permute-start | bytes 147464 | tf_op jit(solution)/shard_map/ppermute | solution.py:437
  1.8 7.7 %collective-permute-start.1 = (f32[24,512]{1,0:T(8,128)S(1)}, f32[24,512]{1,0:T(8,128)S(1)}, u32[]{:S(2)}, u32[]{:S(2)}) collective-permute-start(f32[24,512]{1,0:T(8,128)S(1)} %get-tuple-element.28), channel_id=1, source_target_pairs={{8,0},{16,8},{24,16},{32,24},{40,32},{48,40},{56,48},{64,56},{72,6... | collective-permute-start | bytes 147464 | tf_op jit(solution)/shard_map/ppermute | solution.py:438
  10.4 9.2 %collective-permute-start.2 = (f32[8,144]{1,0:T(8,128)S(1)}, f32[8,144]{1,0:T(8,128)S(1)}, u32[]{:S(2)}, u32[]{:S(2)}) collective-permute-start(f32[8,144]{1,0:T(8,128)S(1)} %get-tuple-element.34), channel_id=1, source_target_pairs={{0,1},{1,2},{2,3},{3,4},{4,5},{5,6},{6,7},{7,0},{8,9},{9,10},{10,1... | collective-permute-start | bytes 13832 | tf_op jit(solution)/shard_map/ppermute | solution.py:465
  14.4 5.2 %collective-permute-start.3 = (f32[8,144]{1,0:T(8,128)S(1)}, f32[8,144]{1,0:T(8,128)S(1)}, u32[]{:S(2)}, u32[]{:S(2)}) collective-permute-start(f32[8,144]{1,0:T(8,128)S(1)} %get-tuple-element.35), channel_id=1, source_target_pairs={{1,0},{2,1},{3,2},{4,3},{5,4},{6,5},{7,6},{0,7},{9,8},{10,9},{11,1... | collective-permute-start | bytes 13832 | tf_op jit(solution)/shard_map/ppermute | solution.py:464
  16.9 2.6 %copy-start.2 = (bf16[96,512]{1,0:T(8,128)(2,1)S(1)}, bf16[96,512]{1,0:T(8,128)(2,1)}, u32[]{:S(2)}) copy-start(bf16[96,512]{1,0:T(8,128)(2,1)} %constant.16.clone.place_ref) | copy-start | bytes 294916
  16.9 2.6 %copy-start.4 = (s32[4,4]{1,0:T(4,128)S(1)}, s32[4,4]{1,0:T(4,128)}, u32[]{:S(2)}) copy-start(s32[4,4]{1,0:T(4,128)} %owner_vmem.1) | copy-start | bytes 196

commit v7 on v6

--- a/solution.py
+++ b/solution.py
@@ -142,7 +142,7 @@
             to_ref[f * HALO : (f + 1) * HALO] = x[start : start + HALO]
 
 
-EARLY = 8
+EARLY = 6
 
 
 def prepare_kernel(*refs):
@@ -369,7 +369,7 @@
             strain * stretch, u * vort, v * vort, u * strain, v * stretch, u * v]
 
 
-def library_kernel(x_ref, out_hbm, gram_ref, out_ref, sem):
+def library_kernel(x_ref, out_hbm, out_ref, sem):
     slots = x_ref.shape[0] // BLOCK_ROWS
     rows = lambda at: x_ref[pl.ds(at, slots, stride=BLOCK_ROWS), :]
     turn_by = lambda x, count: pltpu.roll(x, count % LANES, 1) if count % LANES else x
@@ -397,12 +397,6 @@
             out_ref[k, pl.ds(n, slots, stride=TERMS), :] = x
         copies.append(pltpu.make_async_copy(out_ref.at[k], out_hbm.at[:, pl.ds(k * LANES, LANES)], sem.at[k]))
         copies[k].start()
-    totals = [jnp.sum(rows(GRAM + half), axis=0, keepdims=True) for half in range(2)]
-    for n in range(TERMS):
-        row = totals[n // 8]
-        row = pltpu.roll(row, LANES - n % 8 * TERMS, 1) if n % 8 else row
-        for c in range(gram_ref.shape[0]):
-            gram_ref[c, n : n + 1] = row
     for copy in copies:
         copy.wait()
 
@@ -486,17 +480,20 @@
         name="base_fields",
     )(ocean_mask, tile_owner, main, live, inner, own, from_left, from_right, jnp.asarray(place_matrix()))
     blocks = lax.all_to_all(blocks, "tile", split_axis=0, concat_axis=0, tiled=True)
-    library, gram = pl.pallas_call(
+    gram = jnp.sum(blocks[:, GRAM : GRAM + 2], axis=0)
+    gram = lax.all_to_all(jnp.broadcast_to(gram, (columns, 2, LANES)), "col", split_axis=0, concat_axis=0, tiled=True)
+    library = pl.pallas_call(
         library_kernel,
-        out_shape=[struct(tiles * TERMS, SIDE * SIDE), struct(columns, TERMS, LANES)],
+        out_shape=struct(tiles * TERMS, SIDE * SIDE),
         in_specs=[VMEM],
-        out_specs=[HBM, VMEM],
+        out_specs=HBM,
         scratch_shapes=[pltpu.VMEM((8, tiles * TERMS, LANES), F32), pltpu.SemaphoreType.DMA((8,))],
         compiler_params=PARAMS,
+        cost_estimate=pl.CostEstimate(flops=2 * tiles * TERMS * SIDE * SIDE, transcendentals=0,
+                                      bytes_accessed=5 * tiles * TERMS * SIDE * SIDE),
         name="library_terms",
     )(blocks.reshape(tiles * BLOCK_ROWS, LANES))
-    gram = lax.all_to_all(gram, "col", split_axis=0, concat_axis=0, tiled=True)
-    gram = jnp.sum(gram, axis=0)[:, :TERMS] / (CELLS * CELLS)
+    gram = jnp.sum(gram, axis=0).reshape(TERMS, TERMS) / (CELLS * CELLS)
     return library.reshape(1, 1, tiles, TERMS, SIDE * SIDE), gram
 
 

time: 47.2 us -> 46.3 us (0.981)
  blocking collectives: 23.8 us -> 10.1 us
  waiting for transfers between devices: 0.01 us -> 6.48 us
  starting transfers between devices: 10.5 us -> 16.1 us
  local copies, waits for them, and re-layouts: 0.02 us -> 1.31 us
  other arithmetic: 0.61 us -> 0.05 us
    all_to_all x1 -> x0, blocking collectives: 13.8 us -> none  [per_device(): gram = lax.all_to_all(gram, 'col', split_axis=0, concat_axis=0, tiled=True)]
    all_to_all x0 -> x1, waiting for transfers between devices: none -> 6.47 us  [per_device(): lax.all_to_all(jnp.broadcast_to(gram, (columns, 2, LANES)), 'col', split_...]
    all_to_all x0 -> x1, starting transfers between devices: none -> 5.67 us  [per_device(): lax.all_to_all(jnp.broadcast_to(gram, (columns, 2, LANES)), 'col', split_...]
    div x0 -> x1, local copies, waits for them, and re-layouts: none -> 0.68 us  [per_device(): gram = jnp.sum(gram, axis=0).reshape(TERMS, TERMS) / (CELLS * CELLS)]
    broadcast_in_dim x0 -> x1, local copies, waits for them, and re-layouts: none -> 0.6 us  [per_device(): jnp.broadcast_to(gram, (columns, 2, LANES))]
    div x1, other arithmetic: 0.6 us -> 0.01 us  [per_device(): gram = jnp.sum(gram, axis=0).reshape(TERMS, TERMS) / (CELLS * CELLS)]
    pallas_call x1, Pallas kernels: 2.6 us -> 3.14 us  [per_device(): pl.pallas_call(main_kernel, out_shape=[struct(2, FULL, LANES), struct(CEL...]
    pallas_call x1, Pallas kernels: 3.82 us -> 3.31 us  [per_device(): pl.pallas_call(prepare_kernel, out_shape=[jax.ShapeDtypeStruct((rows, 2 *...]
  transfers between devices with their start and end apart: 4 -> 5, of which waited for: 0 -> 1; matrix products, arithmetic and copies ran while one was open for 0% -> 0% of each run, Pallas kernels for 14% -> 17%
where the time goes in v7:
time: 46.3 us; the launch traced here: 46.1 us
  starting transfers between devices  16.1 us (35%)
  Pallas kernels  11.2 us (24%)
  blocking collectives  10.1 us (22%)
  waiting for transfers between devices  6.48 us (14%)
  local copies, waits for them, and re-layouts  1.31 us (3%)
  between operations  0.77 us (2%)
    all_to_all x1, blocking collectives, per_device(): lax.all_to_all(blocks, 'tile', split_axis=0, concat_axis=0, tiled=True)  10.1 us
    all_to_all x1, waiting for transfers between devices, per_device(): lax.all_to_all(jnp.broadcast_to(gram, (columns, 2, LANES)), 'col', split_...  6.47 us
    all_to_all x1, starting transfers between devices, per_device(): lax.all_to_all(jnp.broadcast_to(gram, (columns, 2, LANES)), 'col', split_...  5.67 us
    ppermute x1, starting transfers between devices, per_device(): from_left = lax.ppermute(to_right, 'col', onward(columns))  4.03 us
    ppermute x1, starting transfers between devices, per_device(): below = lax.ppermute(up, 'tile', back(tiles))  3.84 us
    pallas_call x1, Pallas kernels, per_device(): pl.pallas_call(prepare_kernel, out_shape=[jax.ShapeDtypeStruct((rows, 2 *...  3.31 us
    pallas_call x1, Pallas kernels, per_device(): pl.pallas_call(main_kernel, out_shape=[struct(2, FULL, LANES), struct(CEL...  3.14 us
    ppermute x1, starting transfers between devices, per_device(): from_right = lax.ppermute(to_left, 'col', back(columns))  2.53 us
  transfers between devices with their start and end apart: 5, of which 1 were waited for; matrix products, arithmetic and copies ran while one was open for 0% of the time, Pallas kernels for 17%

profile of v7, /device:TPU:0, one launch (start us, length us, event | category | flops | bytes accessed | tf_op | source)
XLA Modules:
  0.0 46.1 jit_solution(11961092212716250736)
XLA Ops:
  0.6 0.0 copy-start.1
  0.6 0.0 copy-start
  0.7 1.0 %send_rows.1 = (f32[24,512]{1,0:T(8,128)S(1)}, f32[24,512]{1,0:T(8,128)S(1)}) custom-call(s32[1]{0:T(128)} %bitcast.here_ref, s32[16]{0:T(128)} %turns_hbm.1, f32[512,512]{1,0:T(8,128)} %refs_3_, f32[512,512]{1,0:T(8,128)} %refs_7_), custom_call_target="tpu_custom_call" | custom-call | tf_op jit(solution)/shard_map/send_rows/pallas_call | solution.py:420
  1.7 0.0 copy-start.3
  1.7 0.1 collective-permute-start
  1.8 3.8 %collective-permute-start.1 = (f32[24,512]{1,0:T(8,128)S(1)}, f32[24,512]{1,0:T(8,128)S(1)}, u32[]{:S(2)}, u32[]{:S(2)}) collective-permute-start(f32[24,512]{1,0:T(8,128)S(1)} %get-tuple-element.26), channel_id=1, source_target_pairs={{8,0},{16,8},{24,16},{32,24},{40,32},{48,40},{56,48},{64,56},{72,6... | collective-permute-start | bytes 147464 | tf_op jit(solution)/shard_map/ppermute | solution.py:432
  5.6 0.0 copy-done.1
  5.6 0.0 copy-done
  5.6 3.3 %prepare_rows.1 = (bf16[1024,1024]{1,0:T(8,128)(2,1)S(1)}, bf16[512,1280]{1,0:T(8,128)(2,1)S(1)}, f32[144,128]{1,0:T(8,128)S(1)}, f32[1024,768]{1,0:T(8,128)S(1)}) custom-call(f32[512,512]{1,0:T(8,128)S(1)} %copy-done, f32[512,512]{1,0:T(8,128)S(1)} %copy-done, f32[512,512]{1,0:T(8,128)S(1)} %copy-done, f32[512,512]{1,0:T(8,128)S(1)} %copy-done, ...), custom_call_target="tpu_custom_call" | custom-call | tf_op jit(solution)/shard_map/prepare_rows/pallas_call | solution.py:435
  8.9 0.0 collective-permute-done.above_ref
  9.0 0.0 collective-permute-done.1.below_ref
  9.0 0.9 %rim_columns.1 = (f32[8,144]{1,0:T(8,128)S(1)}, f32[8,144]{1,0:T(8,128)S(1)}, f32[16,144]{1,0:T(8,128)S(1)}) custom-call(f32[24,512]{1,0:T(8,128)S(1)} %collective-permute-done.above_ref, f32[24,512]{1,0:T(8,128)S(1)} %collective-permute-done.1.below_ref, bf16[512,1280]{1,0:T(8,128)(2,1)S(1)} %get-tuple-element.24.w_ref, f32[144,128]{1,0:T(8,128)S(1)} %get-tuple-element.27.rim_in), custom_call_target="tpu_custom_call" | custom-call | tf_op jit(solution)/shard_map/rim_columns/pallas_call | solution.py:448
  9.9 4.0 %collective-permute-start.2 = (f32[8,144]{1,0:T(8,128)S(1)}, f32[8,144]{1,0:T(8,128)S(1)}, u32[]{:S(2)}, u32[]{:S(2)}) collective-permute-start(f32[8,144]{1,0:T(8,128)S(1)} %get-tuple-element.32), channel_id=1, source_target_pairs={{0,1},{1,2},{2,3},{3,4},{4,5},{5,6},{6,7},{7,0},{8,9},{9,10},{10,1... | collective-permute-start | bytes 13832 | tf_op jit(solution)/shard_map/ppermute | solution.py:459
  13.9 2.5 %collective-permute-start.3 = (f32[8,144]{1,0:T(8,128)S(1)}, f32[8,144]{1,0:T(8,128)S(1)}, u32[]{:S(2)}, u32[]{:S(2)}) collective-permute-start(f32[8,144]{1,0:T(8,128)S(1)} %get-tuple-element.33), channel_id=1, source_target_pairs={{1,0},{2,1},{3,2},{4,3},{5,4},{6,5},{7,6},{0,7},{9,8},{10,9},{11,1... | collective-permute-start | bytes 13832 | tf_op jit(solution)/shard_map/ppermute | solution.py:458
  16.4 0.0 copy-done.3
  16.4 0.0 copy-start.2
  16.4 0.0 copy-start.4
  16.4 3.1 %main_columns.1 = (f32[2,144,128]{2,1,0:T(8,128)S(1)}, f32[128,128]{1,0:T(8,128)S(1)}, f32[136,8,128]{2,1,0:T(8,128)S(1)}) custom-call(s32[4,4]{1,0:T(4,128)S(1)} %copy-done.3, bf16[1024,1024]{1,0:T(8,128)(2,1)S(1)} %get-tuple-element.22.parts_ref, f32[1024,768]{1,0:T(8,128)S(1)} %get-tuple-element.23.early_ref, ...), custom_call_target="tpu_custom_call" | custom-call | tf_op jit(solution)/shard_map/main_columns/pallas_call | solution.py:460
  19.6 0.0 collective-permute-done.2.from_left_ref
  19.6 0.0 collective-permute-done.3.from_right_ref
  19.6 0.0 copy-done.2
  19.6 0.0 copy-done.4
  19.6 1.7 %base_fields.1 = f32[16,24,128]{2,1,0:T(8,128)S(1)} custom-call(s32[4,4]{1,0:T(4,128)S(1)} %copy-done.3, s32[4,4]{1,0:T(4,128)S(1)} %copy-done.4, f32[2,144,128]{2,1,0:T(8,128)S(1)} %get-tuple-element.29.main_ref, f32[128,128]{1,0:T(8,128)S(1)} %get-tuple-element.30.live_ref, f32[136,8,128]{2,1,0:T(8,128)S(1)} %get-tuple-element.31.inner_ref, ...), custom_call_target="tpu_custom_call" | custom-call | tf_op jit(solution)/shard_map/base_fields/pallas_call | solution.py:470
  21.3 10.1 %all_to_all.10 = f32[16,24,128]{2,1,0:T(8,128)S(1)} all-to-all(f32[16,24,128]{2,1,0:T(8,128)S(1)} %base_fields.1), channel_id=1, replica_groups=mesh['tile'=16,'col'=8] {'tile'}, dimensions={0} | all-to-all | bytes 393216 | tf_op jit(solution)/shard_map/all_to_all | solution.py:482
  31.4 0.6 %broadcast_in_dim.7 = f32[8,2,128]{2,1,0:T(2,128)} broadcast(f32[2,128]{1,0:T(2,128)S(1)} %slice_reduce_fusion), dimensions={1,2} | broadcast | bytes 9216 | tf_op jit(solution)/shard_map/broadcast_in_dim | solution.py:484
  32.0 5.7 %all-to-all-start.1 = ((f32[8,2,128]{2,1,0:T(2,128)}), f32[8,2,128]{2,1,0:T(2,128)S(1)}, u32[]{:S(2)}, u32[]{:S(2)}) async-start(f32[8,2,128]{2,1,0:T(2,128)} %broadcast_in_dim.7), calls=%async_computation.1 | async-start | bytes 16384 | tf_op jit(solution)/shard_map/all_to_all | solution.py:484
  37.7 1.2 %library_terms.1 = f32[256,1024]{1,0:T(8,128)} custom-call(f32[384,128]{1,0:T(8,128)S(1)} %bitcast.3), custom_call_target="tpu_custom_call" | custom-call | flops 524288 | bytes 1310720 | tf_op jit(solution)/shard_map/library_terms/pallas_call | solution.py:485
  38.9 6.5 %all-to-all-done.1 = f32[8,2,128]{2,1,0:T(2,128)S(1)} async-done(((f32[8,2,128]{2,1,0:T(2,128)}), f32[8,2,128]{2,1,0:T(2,128)S(1)}, u32[]{:S(2)}, u32[]{:S(2)}) %all-to-all-start.1) | async-done | bytes 8224 | tf_op jit(solution)/shard_map/all_to_all | solution.py:484
  45.4 0.7 %div.10 = f32[16,16]{1,0:T(8,128)} reshape(f32[2,128]{1,0:T(2,128)S(1)} %broadcast_multiply_fusion) | data formatting | bytes 2048 | tf_op jit(solution)/shard_map/div | solution.py:496
  (3 shorter events, 0.1 us)
Async XLA Ops:
  0.6 5.0 %copy-start.1 = (f32[512,512]{1,0:T(8,128)S(1)}, f32[512,512]{1,0:T(8,128)}, u32[]{:S(2)}) copy-start(f32[512,512]{1,0:T(8,128)} %refs_7_) | copy-start | bytes 3145732
  0.6 5.0 %copy-start = (f32[512,512]{1,0:T(8,128)S(1)}, f32[512,512]{1,0:T(8,128)}, u32[]{:S(2)}) copy-start(f32[512,512]{1,0:T(8,128)} %refs_3_) | copy-start | bytes 3145732
  1.7 14.7 %copy-start.3 = (s32[4,4]{1,0:T(4,128)S(1)}, s32[4,4]{1,0:T(4,128)}, u32[]{:S(2)}) copy-start(s32[4,4]{1,0:T(4,128)} %mask_vmem.1) | copy-start | bytes 196
  1.7 7.3 %collective-permute-start = (f32[24,512]{1,0:T(8,128)S(1)}, f32[24,512]{1,0:T(8,128)S(1)}, u32[]{:S(2)}, u32[]{:S(2)}) collective-permute-start(f32[24,512]{1,0:T(8,128)S(1)} %get-tuple-element.25), channel_id=1, source_target_pairs={{0,8},{8,16},{16,24},{24,32},{32,40},{40,48},{48,56},{56,64},{64,7... | collective-permute-start | bytes 147464 | tf_op jit(solution)/shard_map/ppermute | solution.py:431
  1.8 7.2 %collective-permute-start.1 = (f32[24,512]{1,0:T(8,128)S(1)}, f32[24,512]{1,0:T(8,128)S(1)}, u32[]{:S(2)}, u32[]{:S(2)}) collective-permute-start(f32[24,512]{1,0:T(8,128)S(1)} %get-tuple-element.26), channel_id=1, source_target_pairs={{8,0},{16,8},{24,16},{32,24},{40,32},{48,40},{56,48},{64,56},{72,6... | collective-permute-start | bytes 147464 | tf_op jit(solution)/shard_map/ppermute | solution.py:432
  9.9 9.7 %collective-permute-start.2 = (f32[8,144]{1,0:T(8,128)S(1)}, f32[8,144]{1,0:T(8,128)S(1)}, u32[]{:S(2)}, u32[]{:S(2)}) collective-permute-start(f32[8,144]{1,0:T(8,128)S(1)} %get-tuple-element.32), channel_id=1, source_target_pairs={{0,1},{1,2},{2,3},{3,4},{4,5},{5,6},{6,7},{7,0},{8,9},{9,10},{10,1... | collective-permute-start | bytes 13832 | tf_op jit(solution)/shard_map/ppermute | solution.py:459
  13.9 5.7 %collective-permute-start.3 = (f32[8,144]{1,0:T(8,128)S(1)}, f32[8,144]{1,0:T(8,128)S(1)}, u32[]{:S(2)}, u32[]{:S(2)}) collective-permute-start(f32[8,144]{1,0:T(8,128)S(1)} %get-tuple-element.33), channel_id=1, source_target_pairs={{1,0},{2,1},{3,2},{4,3},{5,4},{6,5},{7,6},{0,7},{9,8},{10,9},{11,1... | collective-permute-start | bytes 13832 | tf_op jit(solution)/shard_map/ppermute | solution.py:458
  16.4 3.2 %copy-start.2 = (bf16[96,512]{1,0:T(8,128)(2,1)S(1)}, bf16[96,512]{1,0:T(8,128)(2,1)}, u32[]{:S(2)}) copy-start(bf16[96,512]{1,0:T(8,128)(2,1)} %constant.16.clone.place_ref) | copy-start | bytes 294916
  16.4 3.2 %copy-start.4 = (s32[4,4]{1,0:T(4,128)S(1)}, s32[4,4]{1,0:T(4,128)}, u32[]{:S(2)}) copy-start(s32[4,4]{1,0:T(4,128)} %owner_vmem.1) | copy-start | bytes 196
  32.0 13.4 %all-to-all-start.1 = ((f32[8,2,128]{2,1,0:T(2,128)}), f32[8,2,128]{2,1,0:T(2,128)S(1)}, u32[]{:S(2)}, u32[]{:S(2)}) async-start(f32[8,2,128]{2,1,0:T(2,128)} %broadcast_in_dim.7), calls=%async_computation.1 | async-start | bytes 16384 | tf_op jit(solution)/shard_map/all_to_all | solution.py:484

commit v8 on v7

--- a/solution.py
+++ b/solution.py
@@ -197,9 +197,10 @@
         for p in range(POOL):
             u, v = [z[((f * 2 + s) * POOL + p) * 8 : ((f * 2 + s) * POOL + p + 1) * 8] for f in range(2)]
             first.append(jnp.where(lane < 64, u, pltpu.roll(v, 64, 1)))
-        last = first
-        for _ in range(PASSES):
-            last = [a + b for a, b in zip(three_rows([pltpu.roll(x, LANES - 6, 1) for x in last]), first)]
+        powers = [first] + [[pltpu.roll(x, LANES - 6 * j, 1) for x in first] for j in range(1, PASSES + 1)]
+        last = powers[PASSES]
+        for j in range(PASSES - 1, -1, -1):
+            last = [a + b for a, b in zip(three_rows(last), powers[j])]
         pooled = ((last[0] + last[1]) + (last[2] + last[3])) * SCALE
         rim_ref[spot : spot + 3] = rim_ref[spot : spot + 3] + pooled[start : start + 3]
     turned = jnp.transpose(rim_ref[...])
@@ -288,7 +289,7 @@
     received = jnp.concatenate([from_left_ref[...], from_right_ref[...], own_ref[...]], axis=0)
     placed = dot(jnp.concatenate(three_parts(received), axis=0), place_ref[...], (((0,), (0,)), ((), ())))
     inner = slice(PAD, PAD + CELLS)
-    slopes = []
+    slopes, beside = [], []
     for f in range(2):
         full = main_ref[f] + placed[:, 2 * f * LANES : (2 * f + 1) * LANES]
         field_ref[f] = full
@@ -296,8 +297,7 @@
         centre = full[inner]
         left = jnp.where(lane == 0, rim, pltpu.roll(centre, 1, 1))
         right = jnp.where(lane == LANES - 1, rim, pltpu.roll(centre, LANES - 1, 1))
-        side_ref[f, 0] = left
-        side_ref[f, 1] = right
+        beside.append((left, right))
         slopes.append((centre, *slopes_of(field_ref, f, left, right)))
     (u, u_dx, u_dy), (v, v_dx, v_dy) = slopes
     live = live_ref[...] > 0.5
@@ -330,9 +330,10 @@
             tile_ref[jnp.where(mask_ref[a, e] == 1, owner_ref[a, e], owners)] = a * grid + e
     pack_ref[nothing] = jnp.zeros((BLOCK_ROWS, LANES), F32)
     group = lane // SIDE
-    rows_of = lax.broadcasted_iota(jnp.int32, (8, LANES), 0)
+    rims = jnp.where(lane % SIDE == 0, beside[0][0], pltpu.roll(beside[1][0], 1, 1))
+    rims = jnp.where(lane % SIDE == SIDE - 1, beside[0][1], rims)
+    side_ref[...] = jnp.transpose(jnp.where(lane % SIDE == SIDE - 2, pltpu.roll(beside[1][1], LANES - 1, 1), rims))
     for a in range(grid):
-        sides = [jnp.zeros((8, LANES), F32)] * grid
         ends = []
         for f in range(2):
             pieces = [field_ref[f, pl.ds(PAD + a * SIDE + q, 8, stride=4), :] for q in range(grid)]
@@ -344,19 +345,14 @@
                 pack_ref[a * grid + e, 8 * f : 8 * f + 8] = block
             for side in range(2):
                 ends.append(field_ref[f, PAD + a * SIDE - 1 + side * (SIDE + 1) : PAD + a * SIDE + side * (SIDE + 1)])
-                for q in range(grid):
-                    x = side_ref[f, side, pl.ds(a * SIDE + q, 8, stride=4), :]
-                    here = lane == rows_of + (q * SIDE + 8 * side + 16 * f)
-                    for e in range(grid):
-                        at = e * SIDE + side * (SIDE - 1)
-                        sides[e] = jnp.where(here, x[:, at : at + 1], sides[e])
         for e in range(grid):
-            pack_ref[a * grid + e, SIDES : SIDES + 1] = jnp.sum(sides[e], axis=0, keepdims=True)
-            row = None
-            for q in range(4):
-                x = pltpu.roll(ends[q], (q - e) % grid * SIDE, 1) if q != e else ends[q]
-                row = x if row is None else jnp.where(group == q, x, row)
-            pack_ref[a * grid + e, ENDS : ENDS + 1] = row
+            sides = [side_ref[e * SIDE + at : e * SIDE + at + 1] for at in (0, SIDE - 1, 1, SIDE - 2)]
+            for spot, parts, own in ((SIDES, sides, a), (ENDS, ends, e)):
+                row = None
+                for q in range(4):
+                    x = pltpu.roll(parts[q], (q - own) % 4 * SIDE, 1) if q != own else parts[q]
+                    row = x if row is None else jnp.where(group == q, x, row)
+                pack_ref[a * grid + e, spot : spot + 1] = row
     for o in range(owners):
         out_ref[o] = pack_ref[tile_ref[o]]
         for h in range(2):
@@ -381,8 +377,11 @@
 
     def slopes(f, k):
         x = fields[f][k]
-        left = jnp.where(lane % SIDE == 0, turn_by(sides, -(k + 16 * f)), turn_by(x, 1))
-        right = jnp.where(lane % SIDE == SIDE - 1, turn_by(sides, SIDE - 1 - (k + 8 + 16 * f)), turn_by(x, -1))
+        left, right = turn_by(x, 1), turn_by(x, -1)
+        for q in range(4):
+            start = 64 * f + 4 * k + q
+            left = jnp.where(lane == SIDE * q, turn_by(sides, SIDE * q - start), left)
+            right = jnp.where(lane == SIDE * (q + 1) - 1, turn_by(sides, SIDE * q - 1 - start), right)
         before = lower[f][k - 1] if k else turn_by(ends, -64 * f)
         after = higher[f][k + 1] if k < 7 else turn_by(ends, 64 - 64 * f)
         up = jnp.where(lane < SIDE, before, lower[f][k])
@@ -474,7 +473,7 @@
         out_specs=VMEM,
         scratch_shapes=[pltpu.VMEM((2, FULL, LANES), F32), pltpu.VMEM((TERMS * TERMS, LANES), F32),
                         pltpu.VMEM((17, BLOCK_ROWS, LANES), F32), pltpu.SMEM((tiles + 1,), jnp.int32),
-                        pltpu.VMEM((2, 2, CELLS, LANES), F32), pltpu.SMEM(ocean_mask.shape, jnp.int32),
+                        pltpu.VMEM((LANES, CELLS), F32), pltpu.SMEM(ocean_mask.shape, jnp.int32),
                         pltpu.SMEM(tile_owner.shape, jnp.int32), pltpu.SemaphoreType.DMA((2,))],
         compiler_params=PARAMS,
         name="base_fields",

time: 46.3 us -> 45.5 us (0.983)
  Pallas kernels: 11.2 us -> 10.5 us
where the time goes in v8:
time: 45.5 us; the launch traced here: 45.3 us
  starting transfers between devices  16.1 us (35%)
  Pallas kernels  10.5 us (23%)
  blocking collectives  10.1 us (22%)
  waiting for transfers between devices  6.4 us (14%)
  local copies, waits for them, and re-layouts  1.31 us (3%)
  between operations  0.77 us (2%)
    all_to_all x1, blocking collectives, per_device(): lax.all_to_all(blocks, 'tile', split_axis=0, concat_axis=0, tiled=True)  10.1 us
    all_to_all x1, waiting for transfers between devices, per_device(): lax.all_to_all(jnp.broadcast_to(gram, (columns, 2, LANES)), 'col', split_...  6.39 us
    all_to_all x1, starting transfers between devices, per_device(): lax.all_to_all(jnp.broadcast_to(gram, (columns, 2, LANES)), 'col', split_...  5.67 us
    ppermute x1, starting transfers between devices, per_device(): from_left = lax.ppermute(to_right, 'col', onward(columns))  4.03 us
    ppermute x1, starting transfers between devices, per_device(): below = lax.ppermute(up, 'tile', back(tiles))  3.84 us
    pallas_call x1, Pallas kernels, per_device(): pl.pallas_call(prepare_kernel, out_shape=[jax.ShapeDtypeStruct((rows, 2 *...  3.31 us
    pallas_call x1, Pallas kernels, per_device(): pl.pallas_call(main_kernel, out_shape=[struct(2, FULL, LANES), struct(CEL...  3.14 us
    ppermute x1, starting transfers between devices, per_device(): from_right = lax.ppermute(to_left, 'col', back(columns))  2.53 us
  transfers between devices with their start and end apart: 5, of which 1 were waited for; matrix products, arithmetic and copies ran while one was open for 0% of the time, Pallas kernels for 17%

profile of v8, /device:TPU:0, one launch (start us, length us, event | category | flops | bytes accessed | tf_op | source)
XLA Modules:
  0.0 45.3 jit_solution(9406514846245333784)
XLA Ops:
  0.6 0.0 copy-start.1
  0.6 0.0 copy-start
  0.7 1.0 %send_rows.1 = (f32[24,512]{1,0:T(8,128)S(1)}, f32[24,512]{1,0:T(8,128)S(1)}) custom-call(s32[1]{0:T(128)} %bitcast.here_ref, s32[16]{0:T(128)} %turns_hbm.1, f32[512,512]{1,0:T(8,128)} %refs_3_, f32[512,512]{1,0:T(8,128)} %refs_7_), custom_call_target="tpu_custom_call" | custom-call | tf_op jit(solution)/shard_map/send_rows/pallas_call | solution.py:419
  1.7 0.0 copy-start.3
  1.7 0.1 collective-permute-start
  1.8 3.8 %collective-permute-start.1 = (f32[24,512]{1,0:T(8,128)S(1)}, f32[24,512]{1,0:T(8,128)S(1)}, u32[]{:S(2)}, u32[]{:S(2)}) collective-permute-start(f32[24,512]{1,0:T(8,128)S(1)} %get-tuple-element.26), channel_id=1, source_target_pairs={{8,0},{16,8},{24,16},{32,24},{40,32},{48,40},{56,48},{64,56},{72,6... | collective-permute-start | bytes 147464 | tf_op jit(solution)/shard_map/ppermute | solution.py:431
  5.6 0.0 copy-done.1
  5.6 0.0 copy-done
  5.6 3.3 %prepare_rows.1 = (bf16[1024,1024]{1,0:T(8,128)(2,1)S(1)}, bf16[512,1280]{1,0:T(8,128)(2,1)S(1)}, f32[144,128]{1,0:T(8,128)S(1)}, f32[1024,768]{1,0:T(8,128)S(1)}) custom-call(f32[512,512]{1,0:T(8,128)S(1)} %copy-done, f32[512,512]{1,0:T(8,128)S(1)} %copy-done, f32[512,512]{1,0:T(8,128)S(1)} %copy-done, f32[512,512]{1,0:T(8,128)S(1)} %copy-done, ...), custom_call_target="tpu_custom_call" | custom-call | tf_op jit(solution)/shard_map/prepare_rows/pallas_call | solution.py:434
  8.9 0.0 collective-permute-done.above_ref
  9.0 0.0 collective-permute-done.1.below_ref
  9.0 0.4 rim_columns.1
  9.4 4.0 %collective-permute-start.2 = (f32[8,144]{1,0:T(8,128)S(1)}, f32[8,144]{1,0:T(8,128)S(1)}, u32[]{:S(2)}, u32[]{:S(2)}) collective-permute-start(f32[8,144]{1,0:T(8,128)S(1)} %get-tuple-element.32), channel_id=1, source_target_pairs={{0,1},{1,2},{2,3},{3,4},{4,5},{5,6},{6,7},{7,0},{8,9},{9,10},{10,1... | collective-permute-start | bytes 13832 | tf_op jit(solution)/shard_map/ppermute | solution.py:458
  13.4 2.5 %collective-permute-start.3 = (f32[8,144]{1,0:T(8,128)S(1)}, f32[8,144]{1,0:T(8,128)S(1)}, u32[]{:S(2)}, u32[]{:S(2)}) collective-permute-start(f32[8,144]{1,0:T(8,128)S(1)} %get-tuple-element.33), channel_id=1, source_target_pairs={{1,0},{2,1},{3,2},{4,3},{5,4},{6,5},{7,6},{0,7},{9,8},{10,9},{11,1... | collective-permute-start | bytes 13832 | tf_op jit(solution)/shard_map/ppermute | solution.py:457
  16.0 0.0 copy-done.3
  16.0 0.0 copy-start.2
  16.0 0.0 copy-start.4
  16.0 3.1 %main_columns.1 = (f32[2,144,128]{2,1,0:T(8,128)S(1)}, f32[128,128]{1,0:T(8,128)S(1)}, f32[136,8,128]{2,1,0:T(8,128)S(1)}) custom-call(s32[4,4]{1,0:T(4,128)S(1)} %copy-done.3, bf16[1024,1024]{1,0:T(8,128)(2,1)S(1)} %get-tuple-element.22.parts_ref, f32[1024,768]{1,0:T(8,128)S(1)} %get-tuple-element.23.early_ref, ...), custom_call_target="tpu_custom_call" | custom-call | tf_op jit(solution)/shard_map/main_columns/pallas_call | solution.py:459
  19.1 0.0 collective-permute-done.2.from_left_ref
  19.1 0.0 collective-permute-done.3.from_right_ref
  19.1 0.0 copy-done.2
  19.2 0.0 copy-done.4
  19.2 1.3 %base_fields.1 = f32[16,24,128]{2,1,0:T(8,128)S(1)} custom-call(s32[4,4]{1,0:T(4,128)S(1)} %copy-done.3, s32[4,4]{1,0:T(4,128)S(1)} %copy-done.4, f32[2,144,128]{2,1,0:T(8,128)S(1)} %get-tuple-element.29.main_ref, f32[128,128]{1,0:T(8,128)S(1)} %get-tuple-element.30.live_ref, f32[136,8,128]{2,1,0:T(8,128)S(1)} %get-tuple-element.31.inner_ref, ...), custom_call_target="tpu_custom_call" | custom-call | tf_op jit(solution)/shard_map/base_fields/pallas_call | solution.py:469
  20.5 10.1 %all_to_all.10 = f32[16,24,128]{2,1,0:T(8,128)S(1)} all-to-all(f32[16,24,128]{2,1,0:T(8,128)S(1)} %base_fields.1), channel_id=1, replica_groups=mesh['tile'=16,'col'=8] {'tile'}, dimensions={0} | all-to-all | bytes 393216 | tf_op jit(solution)/shard_map/all_to_all | solution.py:481
  30.6 0.6 %broadcast_in_dim.7 = f32[8,2,128]{2,1,0:T(2,128)} broadcast(f32[2,128]{1,0:T(2,128)S(1)} %slice_reduce_fusion), dimensions={1,2} | broadcast | bytes 9216 | tf_op jit(solution)/shard_map/broadcast_in_dim | solution.py:483
  31.2 5.7 %all-to-all-start.1 = ((f32[8,2,128]{2,1,0:T(2,128)}), f32[8,2,128]{2,1,0:T(2,128)S(1)}, u32[]{:S(2)}, u32[]{:S(2)}) async-start(f32[8,2,128]{2,1,0:T(2,128)} %broadcast_in_dim.7), calls=%async_computation.1 | async-start | bytes 16384 | tf_op jit(solution)/shard_map/all_to_all | solution.py:483
  36.9 1.3 %library_terms.1 = f32[256,1024]{1,0:T(8,128)} custom-call(f32[384,128]{1,0:T(8,128)S(1)} %bitcast.3), custom_call_target="tpu_custom_call" | custom-call | flops 524288 | bytes 1310720 | tf_op jit(solution)/shard_map/library_terms/pallas_call | solution.py:484
  38.2 6.4 %all-to-all-done.1 = f32[8,2,128]{2,1,0:T(2,128)S(1)} async-done(((f32[8,2,128]{2,1,0:T(2,128)}), f32[8,2,128]{2,1,0:T(2,128)S(1)}, u32[]{:S(2)}, u32[]{:S(2)}) %all-to-all-start.1) | async-done | bytes 8224 | tf_op jit(solution)/shard_map/all_to_all | solution.py:483
  44.6 0.7 %div.10 = f32[16,16]{1,0:T(8,128)} reshape(f32[2,128]{1,0:T(2,128)S(1)} %broadcast_multiply_fusion) | data formatting | bytes 2048 | tf_op jit(solution)/shard_map/div | solution.py:495
  (3 shorter events, 0.1 us)
Async XLA Ops:
  0.6 5.0 %copy-start.1 = (f32[512,512]{1,0:T(8,128)S(1)}, f32[512,512]{1,0:T(8,128)}, u32[]{:S(2)}) copy-start(f32[512,512]{1,0:T(8,128)} %refs_7_) | copy-start | bytes 3145732
  0.6 5.0 %copy-start = (f32[512,512]{1,0:T(8,128)S(1)}, f32[512,512]{1,0:T(8,128)}, u32[]{:S(2)}) copy-start(f32[512,512]{1,0:T(8,128)} %refs_3_) | copy-start | bytes 3145732
  1.7 14.3 %copy-start.3 = (s32[4,4]{1,0:T(4,128)S(1)}, s32[4,4]{1,0:T(4,128)}, u32[]{:S(2)}) copy-start(s32[4,4]{1,0:T(4,128)} %mask_vmem.1) | copy-start | bytes 196
  1.7 7.3 %collective-permute-start = (f32[24,512]{1,0:T(8,128)S(1)}, f32[24,512]{1,0:T(8,128)S(1)}, u32[]{:S(2)}, u32[]{:S(2)}) collective-permute-start(f32[24,512]{1,0:T(8,128)S(1)} %get-tuple-element.25), channel_id=1, source_target_pairs={{0,8},{8,16},{16,24},{24,32},{32,40},{40,48},{48,56},{56,64},{64,7... | collective-permute-start | bytes 147464 | tf_op jit(solution)/shard_map/ppermute | solution.py:430
  1.8 7.2 %collective-permute-start.1 = (f32[24,512]{1,0:T(8,128)S(1)}, f32[24,512]{1,0:T(8,128)S(1)}, u32[]{:S(2)}, u32[]{:S(2)}) collective-permute-start(f32[24,512]{1,0:T(8,128)S(1)} %get-tuple-element.26), channel_id=1, source_target_pairs={{8,0},{16,8},{24,16},{32,24},{40,32},{48,40},{56,48},{64,56},{72,6... | collective-permute-start | bytes 147464 | tf_op jit(solution)/shard_map/ppermute | solution.py:431
  9.4 9.7 %collective-permute-start.2 = (f32[8,144]{1,0:T(8,128)S(1)}, f32[8,144]{1,0:T(8,128)S(1)}, u32[]{:S(2)}, u32[]{:S(2)}) collective-permute-start(f32[8,144]{1,0:T(8,128)S(1)} %get-tuple-element.32), channel_id=1, source_target_pairs={{0,1},{1,2},{2,3},{3,4},{4,5},{5,6},{6,7},{7,0},{8,9},{9,10},{10,1... | collective-permute-start | bytes 13832 | tf_op jit(solution)/shard_map/ppermute | solution.py:458
  13.4 5.7 %collective-permute-start.3 = (f32[8,144]{1,0:T(8,128)S(1)}, f32[8,144]{1,0:T(8,128)S(1)}, u32[]{:S(2)}, u32[]{:S(2)}) collective-permute-start(f32[8,144]{1,0:T(8,128)S(1)} %get-tuple-element.33), channel_id=1, source_target_pairs={{1,0},{2,1},{3,2},{4,3},{5,4},{6,5},{7,6},{0,7},{9,8},{10,9},{11,1... | collective-permute-start | bytes 13832 | tf_op jit(solution)/shard_map/ppermute | solution.py:457
  16.0 3.2 %copy-start.2 = (bf16[96,512]{1,0:T(8,128)(2,1)S(1)}, bf16[96,512]{1,0:T(8,128)(2,1)}, u32[]{:S(2)}) copy-start(bf16[96,512]{1,0:T(8,128)(2,1)} %constant.16.clone.place_ref) | copy-start | bytes 294916
  16.0 3.2 %copy-start.4 = (s32[4,4]{1,0:T(4,128)S(1)}, s32[4,4]{1,0:T(4,128)}, u32[]{:S(2)}) copy-start(s32[4,4]{1,0:T(4,128)} %owner_vmem.1) | copy-start | bytes 196
  31.2 13.4 %all-to-all-start.1 = ((f32[8,2,128]{2,1,0:T(2,128)}), f32[8,2,128]{2,1,0:T(2,128)S(1)}, u32[]{:S(2)}, u32[]{:S(2)}) async-start(f32[8,2,128]{2,1,0:T(2,128)} %broadcast_in_dim.7), calls=%async_computation.1 | async-start | bytes 16384 | tf_op jit(solution)/shard_map/all_to_all | solution.py:483

commit v9 on v8

--- a/solution.py
+++ b/solution.py
@@ -233,7 +233,7 @@
                 for p in range(POOL):
                     spot = (f * POOL + p) * 16 + start
                     strip_ref[spot : spot + 3, cut] = rows_ref[s, c, pl.ds(f * HALO + p, 3, stride=POOL), :]
-    strips = jnp.concatenate(two_parts(strip_ref[...]), axis=1)
+    strips = jnp.concatenate(two_parts(strip_ref[...]), axis=0)
     fine = POOL * CELLS
     for start in range(0, 9, 2):
         wide = min(2, 9 - start)
@@ -242,7 +242,8 @@
             z = early_ref[:, start * LANES : (start + wide) * LANES]
         else:
             z = dot(parts_ref[:, :fine], w) + dot(parts_ref[:, fine:], w)
-        z_strip = dot(strips[:, :fine], w) + dot(strips[:, fine:], w)
+        both = dot(strips, w)
+        z_strip = both[: both.shape[0] // 2] + both[both.shape[0] // 2 :]
         for stage in range(start, start + wide):
             cut = slice((stage - start) * LANES, (stage - start + 1) * LANES)
             for f in range(2):

time: 45.5 us -> 45.5 us (level)
  no operation moved by 1% of the time
where the time goes in v9:
time: 45.5 us; the launch traced here: 45.3 us
  starting transfers between devices  16.2 us (36%)
  Pallas kernels  10.4 us (23%)
  blocking collectives  10.1 us (22%)
  waiting for transfers between devices  6.4 us (14%)
  local copies, waits for them, and re-layouts  1.31 us (3%)
  between operations  0.77 us (2%)
    all_to_all x1, blocking collectives, per_device(): lax.all_to_all(blocks, 'tile', split_axis=0, concat_axis=0, tiled=True)  10.1 us
    all_to_all x1, waiting for transfers between devices, per_device(): lax.all_to_all(jnp.broadcast_to(gram, (columns, 2, LANES)), 'col', split_...  6.39 us
    all_to_all x1, starting transfers between devices, per_device(): lax.all_to_all(jnp.broadcast_to(gram, (columns, 2, LANES)), 'col', split_...  5.74 us
    ppermute x1, starting transfers between devices, per_device(): from_left = lax.ppermute(to_right, 'col', onward(columns))  4.03 us
    ppermute x1, starting transfers between devices, per_device(): below = lax.ppermute(up, 'tile', back(tiles))  3.84 us
    pallas_call x1, Pallas kernels, per_device(): pl.pallas_call(prepare_kernel, out_shape=[jax.ShapeDtypeStruct((rows, 2 *...  3.31 us
    pallas_call x1, Pallas kernels, per_device(): pl.pallas_call(main_kernel, out_shape=[struct(2, FULL, LANES), struct(CEL...  3.08 us
    ppermute x1, starting transfers between devices, per_device(): from_right = lax.ppermute(to_left, 'col', back(columns))  2.53 us
  transfers between devices with their start and end apart: 5, of which 1 were waited for; matrix products, arithmetic and copies ran while one was open for 0% of the time, Pallas kernels for 17%

profile of v9, /device:TPU:0, one launch (start us, length us, event | category | flops | bytes accessed | tf_op | source)
XLA Modules:
  0.0 45.3 jit_solution(13071955366403330842)
XLA Ops:
  0.6 0.0 copy-start.1
  0.6 0.0 copy-start
  0.7 1.0 %send_rows.1 = (f32[24,512]{1,0:T(8,128)S(1)}, f32[24,512]{1,0:T(8,128)S(1)}) custom-call(s32[1]{0:T(128)} %bitcast.here_ref, s32[16]{0:T(128)} %turns_hbm.1, f32[512,512]{1,0:T(8,128)} %refs_3_, f32[512,512]{1,0:T(8,128)} %refs_7_), custom_call_target="tpu_custom_call" | custom-call | tf_op jit(solution)/shard_map/send_rows/pallas_call | solution.py:420
  1.7 0.0 copy-start.3
  1.7 0.1 collective-permute-start
  1.8 3.8 %collective-permute-start.1 = (f32[24,512]{1,0:T(8,128)S(1)}, f32[24,512]{1,0:T(8,128)S(1)}, u32[]{:S(2)}, u32[]{:S(2)}) collective-permute-start(f32[24,512]{1,0:T(8,128)S(1)} %get-tuple-element.26), channel_id=1, source_target_pairs={{8,0},{16,8},{24,16},{32,24},{40,32},{48,40},{56,48},{64,56},{72,6... | collective-permute-start | bytes 147464 | tf_op jit(solution)/shard_map/ppermute | solution.py:432
  5.6 0.0 copy-done.1
  5.6 0.0 copy-done
  5.6 3.3 %prepare_rows.1 = (bf16[1024,1024]{1,0:T(8,128)(2,1)S(1)}, bf16[512,1280]{1,0:T(8,128)(2,1)S(1)}, f32[144,128]{1,0:T(8,128)S(1)}, f32[1024,768]{1,0:T(8,128)S(1)}) custom-call(f32[512,512]{1,0:T(8,128)S(1)} %copy-done, f32[512,512]{1,0:T(8,128)S(1)} %copy-done, f32[512,512]{1,0:T(8,128)S(1)} %copy-done, f32[512,512]{1,0:T(8,128)S(1)} %copy-done, ...), custom_call_target="tpu_custom_call" | custom-call | tf_op jit(solution)/shard_map/prepare_rows/pallas_call | solution.py:435
  8.9 0.0 collective-permute-done.above_ref
  9.0 0.0 collective-permute-done.1.below_ref
  9.0 0.4 rim_columns.1
  9.4 4.0 %collective-permute-start.2 = (f32[8,144]{1,0:T(8,128)S(1)}, f32[8,144]{1,0:T(8,128)S(1)}, u32[]{:S(2)}, u32[]{:S(2)}) collective-permute-start(f32[8,144]{1,0:T(8,128)S(1)} %get-tuple-element.32), channel_id=1, source_target_pairs={{0,1},{1,2},{2,3},{3,4},{4,5},{5,6},{6,7},{7,0},{8,9},{9,10},{10,1... | collective-permute-start | bytes 13832 | tf_op jit(solution)/shard_map/ppermute | solution.py:459
  13.4 2.5 %collective-permute-start.3 = (f32[8,144]{1,0:T(8,128)S(1)}, f32[8,144]{1,0:T(8,128)S(1)}, u32[]{:S(2)}, u32[]{:S(2)}) collective-permute-start(f32[8,144]{1,0:T(8,128)S(1)} %get-tuple-element.33), channel_id=1, source_target_pairs={{1,0},{2,1},{3,2},{4,3},{5,4},{6,5},{7,6},{0,7},{9,8},{10,9},{11,1... | collective-permute-start | bytes 13832 | tf_op jit(solution)/shard_map/ppermute | solution.py:458
  16.0 0.0 copy-done.3
  16.0 0.0 copy-start.2
  16.0 0.0 copy-start.4
  16.0 3.1 %main_columns.1 = (f32[2,144,128]{2,1,0:T(8,128)S(1)}, f32[128,128]{1,0:T(8,128)S(1)}, f32[136,8,128]{2,1,0:T(8,128)S(1)}) custom-call(s32[4,4]{1,0:T(4,128)S(1)} %copy-done.3, bf16[1024,1024]{1,0:T(8,128)(2,1)S(1)} %get-tuple-element.22.parts_ref, f32[1024,768]{1,0:T(8,128)S(1)} %get-tuple-element.23.early_ref, ...), custom_call_target="tpu_custom_call" | custom-call | tf_op jit(solution)/shard_map/main_columns/pallas_call | solution.py:460
  19.1 0.0 collective-permute-done.2.from_left_ref
  19.1 0.0 collective-permute-done.3.from_right_ref
  19.1 0.0 copy-done.2
  19.1 0.0 copy-done.4
  19.1 1.3 %base_fields.1 = f32[16,24,128]{2,1,0:T(8,128)S(1)} custom-call(s32[4,4]{1,0:T(4,128)S(1)} %copy-done.3, s32[4,4]{1,0:T(4,128)S(1)} %copy-done.4, f32[2,144,128]{2,1,0:T(8,128)S(1)} %get-tuple-element.29.main_ref, f32[128,128]{1,0:T(8,128)S(1)} %get-tuple-element.30.live_ref, f32[136,8,128]{2,1,0:T(8,128)S(1)} %get-tuple-element.31.inner_ref, ...), custom_call_target="tpu_custom_call" | custom-call | tf_op jit(solution)/shard_map/base_fields/pallas_call | solution.py:470
  20.4 10.1 %all_to_all.10 = f32[16,24,128]{2,1,0:T(8,128)S(1)} all-to-all(f32[16,24,128]{2,1,0:T(8,128)S(1)} %base_fields.1), channel_id=1, replica_groups=mesh['tile'=16,'col'=8] {'tile'}, dimensions={0} | all-to-all | bytes 393216 | tf_op jit(solution)/shard_map/all_to_all | solution.py:482
  30.5 0.6 %broadcast_in_dim.7 = f32[8,2,128]{2,1,0:T(2,128)} broadcast(f32[2,128]{1,0:T(2,128)S(1)} %slice_reduce_fusion), dimensions={1,2} | broadcast | bytes 9216 | tf_op jit(solution)/shard_map/broadcast_in_dim | solution.py:484
  31.1 5.7 %all-to-all-start.1 = ((f32[8,2,128]{2,1,0:T(2,128)}), f32[8,2,128]{2,1,0:T(2,128)S(1)}, u32[]{:S(2)}, u32[]{:S(2)}) async-start(f32[8,2,128]{2,1,0:T(2,128)} %broadcast_in_dim.7), calls=%async_computation.1 | async-start | bytes 16384 | tf_op jit(solution)/shard_map/all_to_all | solution.py:484
  36.9 1.3 %library_terms.1 = f32[256,1024]{1,0:T(8,128)} custom-call(f32[384,128]{1,0:T(8,128)S(1)} %bitcast.3), custom_call_target="tpu_custom_call" | custom-call | flops 524288 | bytes 1310720 | tf_op jit(solution)/shard_map/library_terms/pallas_call | solution.py:485
  38.2 6.4 %all-to-all-done.1 = f32[8,2,128]{2,1,0:T(2,128)S(1)} async-done(((f32[8,2,128]{2,1,0:T(2,128)}), f32[8,2,128]{2,1,0:T(2,128)S(1)}, u32[]{:S(2)}, u32[]{:S(2)}) %all-to-all-start.1) | async-done | bytes 8224 | tf_op jit(solution)/shard_map/all_to_all | solution.py:484
  44.6 0.7 %div.10 = f32[16,16]{1,0:T(8,128)} reshape(f32[2,128]{1,0:T(2,128)S(1)} %broadcast_multiply_fusion) | data formatting | bytes 2048 | tf_op jit(solution)/shard_map/div | solution.py:496
  (3 shorter events, 0.1 us)
Async XLA Ops:
  0.6 5.0 %copy-start.1 = (f32[512,512]{1,0:T(8,128)S(1)}, f32[512,512]{1,0:T(8,128)}, u32[]{:S(2)}) copy-start(f32[512,512]{1,0:T(8,128)} %refs_7_) | copy-start | bytes 3145732
  0.6 5.0 %copy-start = (f32[512,512]{1,0:T(8,128)S(1)}, f32[512,512]{1,0:T(8,128)}, u32[]{:S(2)}) copy-start(f32[512,512]{1,0:T(8,128)} %refs_3_) | copy-start | bytes 3145732
  1.7 14.3 %copy-start.3 = (s32[4,4]{1,0:T(4,128)S(1)}, s32[4,4]{1,0:T(4,128)}, u32[]{:S(2)}) copy-start(s32[4,4]{1,0:T(4,128)} %mask_vmem.1) | copy-start | bytes 196
  1.7 7.3 %collective-permute-start = (f32[24,512]{1,0:T(8,128)S(1)}, f32[24,512]{1,0:T(8,128)S(1)}, u32[]{:S(2)}, u32[]{:S(2)}) collective-permute-start(f32[24,512]{1,0:T(8,128)S(1)} %get-tuple-element.25), channel_id=1, source_target_pairs={{0,8},{8,16},{16,24},{24,32},{32,40},{40,48},{48,56},{56,64},{64,7... | collective-permute-start | bytes 147464 | tf_op jit(solution)/shard_map/ppermute | solution.py:431
  1.8 7.2 %collective-permute-start.1 = (f32[24,512]{1,0:T(8,128)S(1)}, f32[24,512]{1,0:T(8,128)S(1)}, u32[]{:S(2)}, u32[]{:S(2)}) collective-permute-start(f32[24,512]{1,0:T(8,128)S(1)} %get-tuple-element.26), channel_id=1, source_target_pairs={{8,0},{16,8},{24,16},{32,24},{40,32},{48,40},{56,48},{64,56},{72,6... | collective-permute-start | bytes 147464 | tf_op jit(solution)/shard_map/ppermute | solution.py:432
  9.4 9.7 %collective-permute-start.2 = (f32[8,144]{1,0:T(8,128)S(1)}, f32[8,144]{1,0:T(8,128)S(1)}, u32[]{:S(2)}, u32[]{:S(2)}) collective-permute-start(f32[8,144]{1,0:T(8,128)S(1)} %get-tuple-element.32), channel_id=1, source_target_pairs={{0,1},{1,2},{2,3},{3,4},{4,5},{5,6},{6,7},{7,0},{8,9},{9,10},{10,1... | collective-permute-start | bytes 13832 | tf_op jit(solution)/shard_map/ppermute | solution.py:459
  13.4 5.6 %collective-permute-start.3 = (f32[8,144]{1,0:T(8,128)S(1)}, f32[8,144]{1,0:T(8,128)S(1)}, u32[]{:S(2)}, u32[]{:S(2)}) collective-permute-start(f32[8,144]{1,0:T(8,128)S(1)} %get-tuple-element.33), channel_id=1, source_target_pairs={{1,0},{2,1},{3,2},{4,3},{5,4},{6,5},{7,6},{0,7},{9,8},{10,9},{11,1... | collective-permute-start | bytes 13832 | tf_op jit(solution)/shard_map/ppermute | solution.py:458
  16.0 3.1 %copy-start.2 = (bf16[96,512]{1,0:T(8,128)(2,1)S(1)}, bf16[96,512]{1,0:T(8,128)(2,1)}, u32[]{:S(2)}) copy-start(bf16[96,512]{1,0:T(8,128)(2,1)} %constant.16.clone.place_ref) | copy-start | bytes 294916
  16.0 3.1 %copy-start.4 = (s32[4,4]{1,0:T(4,128)S(1)}, s32[4,4]{1,0:T(4,128)}, u32[]{:S(2)}) copy-start(s32[4,4]{1,0:T(4,128)} %owner_vmem.1) | copy-start | bytes 196
  31.1 13.4 %all-to-all-start.1 = ((f32[8,2,128]{2,1,0:T(2,128)}), f32[8,2,128]{2,1,0:T(2,128)S(1)}, u32[]{:S(2)}, u32[]{:S(2)}) async-start(f32[8,2,128]{2,1,0:T(2,128)} %broadcast_in_dim.7), calls=%async_computation.1 | async-start | bytes 16384 | tf_op jit(solution)/shard_map/all_to_all | solution.py:484

commit v10 on v9

--- a/solution.py
+++ b/solution.py
@@ -142,7 +142,7 @@
             to_ref[f * HALO : (f + 1) * HALO] = x[start : start + HALO]
 
 
-EARLY = 6
+EARLY = 8
 
 
 def prepare_kernel(*refs):

time: 45.5 us -> 46 us (1.011)
  starting transfers between devices: 16.2 us -> 16.7 us
    pallas_call x1, Pallas kernels: 3.08 us -> 2.56 us  [per_device(): pl.pallas_call(main_kernel, out_shape=[struct(2, FULL, LANES), struct(CEL...]
    pallas_call x1, Pallas kernels: 3.31 us -> 3.82 us  [per_device(): pl.pallas_call(prepare_kernel, out_shape=[jax.ShapeDtypeStruct((rows, 2 *...]
    all_to_all x1, starting transfers between devices: 5.74 us -> 6.23 us  [per_device(): lax.all_to_all(jnp.broadcast_to(gram, (columns, 2, LANES)), 'col', split_...]
where the time goes in v10:
time: 46 us; the launch traced here: 45.8 us
  starting transfers between devices  16.7 us (36%)
  Pallas kernels  10.4 us (23%)
  blocking collectives  10.1 us (22%)
  waiting for transfers between devices  6.44 us (14%)
  local copies, waits for them, and re-layouts  1.31 us (3%)
  between operations  0.75 us (2%)
    all_to_all x1, blocking collectives, per_device(): lax.all_to_all(blocks, 'tile', split_axis=0, concat_axis=0, tiled=True)  10.1 us
    all_to_all x1, waiting for transfers between devices, per_device(): lax.all_to_all(jnp.broadcast_to(gram, (columns, 2, LANES)), 'col', split_...  6.39 us
    all_to_all x1, starting transfers between devices, per_device(): lax.all_to_all(jnp.broadcast_to(gram, (columns, 2, LANES)), 'col', split_...  6.23 us
    ppermute x1, starting transfers between devices, per_device(): from_left = lax.ppermute(to_right, 'col', onward(columns))  4.03 us
    ppermute x1, starting transfers between devices, per_device(): below = lax.ppermute(up, 'tile', back(tiles))  3.84 us
    pallas_call x1, Pallas kernels, per_device(): pl.pallas_call(prepare_kernel, out_shape=[jax.ShapeDtypeStruct((rows, 2 *...  3.82 us
    pallas_call x1, Pallas kernels, per_device(): pl.pallas_call(main_kernel, out_shape=[struct(2, FULL, LANES), struct(CEL...  2.56 us
    ppermute x1, starting transfers between devices, per_device(): from_right = lax.ppermute(to_left, 'col', back(columns))  2.53 us
  transfers between devices with their start and end apart: 5, of which 1 were waited for; matrix products, arithmetic and copies ran while one was open for 0% of the time, Pallas kernels for 17%

profile of v10, /device:TPU:0, one launch (start us, length us, event | category | flops | bytes accessed | tf_op | source)
XLA Modules:
  0.0 45.8 jit_solution(2536271983321242026)
XLA Ops:
  0.6 0.0 copy-start.1
  0.6 0.0 copy-start
  0.7 1.0 %send_rows.1 = (f32[24,512]{1,0:T(8,128)S(1)}, f32[24,512]{1,0:T(8,128)S(1)}) custom-call(s32[1]{0:T(128)} %bitcast.here_ref, s32[16]{0:T(128)} %turns_hbm.1, f32[512,512]{1,0:T(8,128)} %refs_3_, f32[512,512]{1,0:T(8,128)} %refs_7_), custom_call_target="tpu_custom_call" | custom-call | tf_op jit(solution)/shard_map/send_rows/pallas_call | solution.py:420
  1.7 0.0 copy-start.3
  1.7 0.1 collective-permute-start
  1.8 3.8 %collective-permute-start.1 = (f32[24,512]{1,0:T(8,128)S(1)}, f32[24,512]{1,0:T(8,128)S(1)}, u32[]{:S(2)}, u32[]{:S(2)}) collective-permute-start(f32[24,512]{1,0:T(8,128)S(1)} %get-tuple-element.26), channel_id=1, source_target_pairs={{8,0},{16,8},{24,16},{32,24},{40,32},{48,40},{56,48},{64,56},{72,6... | collective-permute-start | bytes 147464 | tf_op jit(solution)/shard_map/ppermute | solution.py:432
  5.6 0.0 copy-done.1
  5.6 0.0 copy-done
  5.6 3.8 %prepare_rows.1 = (bf16[1024,1024]{1,0:T(8,128)(2,1)S(1)}, bf16[512,1280]{1,0:T(8,128)(2,1)S(1)}, f32[144,128]{1,0:T(8,128)S(1)}, f32[1024,1024]{1,0:T(8,128)S(1)}) custom-call(f32[512,512]{1,0:T(8,128)S(1)} %copy-done, f32[512,512]{1,0:T(8,128)S(1)} %copy-done, f32[512,512]{1,0:T(8,128)S(1)} %copy-done, f32[512,512]{1,0:T(8,128)S(1)} %copy-done, ...), custom_call_target="tpu_custom_call" | custom-call | tf_op jit(solution)/shard_map/prepare_rows/pallas_call | solution.py:435
  9.4 0.0 collective-permute-done.above_ref
  9.5 0.0 collective-permute-done.1.below_ref
  9.5 0.4 rim_columns.1
  9.9 4.0 %collective-permute-start.2 = (f32[8,144]{1,0:T(8,128)S(1)}, f32[8,144]{1,0:T(8,128)S(1)}, u32[]{:S(2)}, u32[]{:S(2)}) collective-permute-start(f32[8,144]{1,0:T(8,128)S(1)} %get-tuple-element.32), channel_id=1, source_target_pairs={{0,1},{1,2},{2,3},{3,4},{4,5},{5,6},{6,7},{7,0},{8,9},{9,10},{10,1... | collective-permute-start | bytes 13832 | tf_op jit(solution)/shard_map/ppermute | solution.py:459
  14.0 2.5 %collective-permute-start.3 = (f32[8,144]{1,0:T(8,128)S(1)}, f32[8,144]{1,0:T(8,128)S(1)}, u32[]{:S(2)}, u32[]{:S(2)}) collective-permute-start(f32[8,144]{1,0:T(8,128)S(1)} %get-tuple-element.33), channel_id=1, source_target_pairs={{1,0},{2,1},{3,2},{4,3},{5,4},{6,5},{7,6},{0,7},{9,8},{10,9},{11,1... | collective-permute-start | bytes 13832 | tf_op jit(solution)/shard_map/ppermute | solution.py:458
  16.5 0.0 copy-done.3
  16.5 0.0 copy-start.2
  16.5 0.0 copy-start.4
  16.5 2.6 %main_columns.1 = (f32[2,144,128]{2,1,0:T(8,128)S(1)}, f32[128,128]{1,0:T(8,128)S(1)}, f32[136,8,128]{2,1,0:T(8,128)S(1)}) custom-call(s32[4,4]{1,0:T(4,128)S(1)} %copy-done.3, bf16[1024,1024]{1,0:T(8,128)(2,1)S(1)} %get-tuple-element.22.parts_ref, f32[1024,1024]{1,0:T(8,128)S(1)} %get-tuple-element.23.early_ref, ...), custom_call_target="tpu_custom_call" | custom-call | tf_op jit(solution)/shard_map/main_columns/pallas_call | solution.py:460
  19.1 0.0 collective-permute-done.2.from_left_ref
  19.1 0.0 collective-permute-done.3.from_right_ref
  19.1 0.0 copy-done.2
  19.1 0.0 copy-done.4
  19.1 1.3 %base_fields.1 = f32[16,24,128]{2,1,0:T(8,128)S(1)} custom-call(s32[4,4]{1,0:T(4,128)S(1)} %copy-done.3, s32[4,4]{1,0:T(4,128)S(1)} %copy-done.4, f32[2,144,128]{2,1,0:T(8,128)S(1)} %get-tuple-element.29.main_ref, f32[128,128]{1,0:T(8,128)S(1)} %get-tuple-element.30.live_ref, f32[136,8,128]{2,1,0:T(8,128)S(1)} %get-tuple-element.31.inner_ref, ...), custom_call_target="tpu_custom_call" | custom-call | tf_op jit(solution)/shard_map/base_fields/pallas_call | solution.py:470
  20.4 10.1 %all_to_all.10 = f32[16,24,128]{2,1,0:T(8,128)S(1)} all-to-all(f32[16,24,128]{2,1,0:T(8,128)S(1)} %base_fields.1), channel_id=1, replica_groups=mesh['tile'=16,'col'=8] {'tile'}, dimensions={0} | all-to-all | bytes 393216 | tf_op jit(solution)/shard_map/all_to_all | solution.py:482
  30.6 0.6 %broadcast_in_dim.7 = f32[8,2,128]{2,1,0:T(2,128)} broadcast(f32[2,128]{1,0:T(2,128)S(1)} %slice_reduce_fusion), dimensions={1,2} | broadcast | bytes 9216 | tf_op jit(solution)/shard_map/broadcast_in_dim | solution.py:484
  31.2 6.2 %all-to-all-start.1 = ((f32[8,2,128]{2,1,0:T(2,128)}), f32[8,2,128]{2,1,0:T(2,128)S(1)}, u32[]{:S(2)}, u32[]{:S(2)}) async-start(f32[8,2,128]{2,1,0:T(2,128)} %broadcast_in_dim.7), calls=%async_computation.1 | async-start | bytes 16384 | tf_op jit(solution)/shard_map/all_to_all | solution.py:484
  37.4 1.3 %library_terms.1 = f32[256,1024]{1,0:T(8,128)} custom-call(f32[384,128]{1,0:T(8,128)S(1)} %bitcast.3), custom_call_target="tpu_custom_call" | custom-call | flops 524288 | bytes 1310720 | tf_op jit(solution)/shard_map/library_terms/pallas_call | solution.py:485
  38.7 6.4 %all-to-all-done.1 = f32[8,2,128]{2,1,0:T(2,128)S(1)} async-done(((f32[8,2,128]{2,1,0:T(2,128)}), f32[8,2,128]{2,1,0:T(2,128)S(1)}, u32[]{:S(2)}, u32[]{:S(2)}) %all-to-all-start.1) | async-done | bytes 8224 | tf_op jit(solution)/shard_map/all_to_all | solution.py:484
  45.1 0.7 %div.10 = f32[16,16]{1,0:T(8,128)} reshape(f32[2,128]{1,0:T(2,128)S(1)} %broadcast_multiply_fusion) | data formatting | bytes 2048 | tf_op jit(solution)/shard_map/div | solution.py:496
  (3 shorter events, 0.1 us)
Async XLA Ops:
  0.6 5.0 %copy-start.1 = (f32[512,512]{1,0:T(8,128)S(1)}, f32[512,512]{1,0:T(8,128)}, u32[]{:S(2)}) copy-start(f32[512,512]{1,0:T(8,128)} %refs_7_) | copy-start | bytes 3145732
  0.6 5.0 %copy-start = (f32[512,512]{1,0:T(8,128)S(1)}, f32[512,512]{1,0:T(8,128)}, u32[]{:S(2)}) copy-start(f32[512,512]{1,0:T(8,128)} %refs_3_) | copy-start | bytes 3145732
  1.7 14.8 %copy-start.3 = (s32[4,4]{1,0:T(4,128)S(1)}, s32[4,4]{1,0:T(4,128)}, u32[]{:S(2)}) copy-start(s32[4,4]{1,0:T(4,128)} %mask_vmem.1) | copy-start | bytes 196
  1.7 7.8 %collective-permute-start = (f32[24,512]{1,0:T(8,128)S(1)}, f32[24,512]{1,0:T(8,128)S(1)}, u32[]{:S(2)}, u32[]{:S(2)}) collective-permute-start(f32[24,512]{1,0:T(8,128)S(1)} %get-tuple-element.25), channel_id=1, source_target_pairs={{0,8},{8,16},{16,24},{24,32},{32,40},{40,48},{48,56},{56,64},{64,7... | collective-permute-start | bytes 147464 | tf_op jit(solution)/shard_map/ppermute | solution.py:431
  1.8 7.7 %collective-permute-start.1 = (f32[24,512]{1,0:T(8,128)S(1)}, f32[24,512]{1,0:T(8,128)S(1)}, u32[]{:S(2)}, u32[]{:S(2)}) collective-permute-start(f32[24,512]{1,0:T(8,128)S(1)} %get-tuple-element.26), channel_id=1, source_target_pairs={{8,0},{16,8},{24,16},{32,24},{40,32},{48,40},{56,48},{64,56},{72,6... | collective-permute-start | bytes 147464 | tf_op jit(solution)/shard_map/ppermute | solution.py:432
  9.9 9.1 %collective-permute-start.2 = (f32[8,144]{1,0:T(8,128)S(1)}, f32[8,144]{1,0:T(8,128)S(1)}, u32[]{:S(2)}, u32[]{:S(2)}) collective-permute-start(f32[8,144]{1,0:T(8,128)S(1)} %get-tuple-element.32), channel_id=1, source_target_pairs={{0,1},{1,2},{2,3},{3,4},{4,5},{5,6},{6,7},{7,0},{8,9},{9,10},{10,1... | collective-permute-start | bytes 13832 | tf_op jit(solution)/shard_map/ppermute | solution.py:459
  14.0 5.2 %collective-permute-start.3 = (f32[8,144]{1,0:T(8,128)S(1)}, f32[8,144]{1,0:T(8,128)S(1)}, u32[]{:S(2)}, u32[]{:S(2)}) collective-permute-start(f32[8,144]{1,0:T(8,128)S(1)} %get-tuple-element.33), channel_id=1, source_target_pairs={{1,0},{2,1},{3,2},{4,3},{5,4},{6,5},{7,6},{0,7},{9,8},{10,9},{11,1... | collective-permute-start | bytes 13832 | tf_op jit(solution)/shard_map/ppermute | solution.py:458
  16.5 2.6 %copy-start.2 = (bf16[96,512]{1,0:T(8,128)(2,1)S(1)}, bf16[96,512]{1,0:T(8,128)(2,1)}, u32[]{:S(2)}) copy-start(bf16[96,512]{1,0:T(8,128)(2,1)} %constant.16.clone.place_ref) | copy-start | bytes 294916
  16.5 2.6 %copy-start.4 = (s32[4,4]{1,0:T(4,128)S(1)}, s32[4,4]{1,0:T(4,128)}, u32[]{:S(2)}) copy-start(s32[4,4]{1,0:T(4,128)} %owner_vmem.1) | copy-start | bytes 196
  31.2 13.9 %all-to-all-start.1 = ((f32[8,2,128]{2,1,0:T(2,128)}), f32[8,2,128]{2,1,0:T(2,128)S(1)}, u32[]{:S(2)}, u32[]{:S(2)}) async-start(f32[8,2,128]{2,1,0:T(2,128)} %broadcast_in_dim.7), calls=%async_computation.1 | async-start | bytes 16384 | tf_op jit(solution)/shard_map/all_to_all | solution.py:484

commit v11 on v8

--- a/solution.py
+++ b/solution.py
@@ -314,7 +314,7 @@
         gram_ref[n * TERMS + m : n * TERMS + m + 1] = total
         if m > n:
             gram_ref[m * TERMS + n : m * TERMS + n + 1] = total
-    totals = jnp.sum(gram_ref[...], axis=1, keepdims=True)
+    totals = jnp.sum(gram_ref[...], axis=1, keepdims=True) * (1.0 / (CELLS * CELLS))
     row = lax.broadcasted_iota(jnp.int32, (TERMS * TERMS, 1), 0)
     spread = jnp.where(row % LANES == lane, totals, 0.0)
     halves = [jnp.sum(spread[h * LANES : (h + 1) * LANES], axis=0, keepdims=True) for h in range(2)]
@@ -492,7 +492,7 @@
                                       bytes_accessed=5 * tiles * TERMS * SIDE * SIDE),
         name="library_terms",
     )(blocks.reshape(tiles * BLOCK_ROWS, LANES))
-    gram = jnp.sum(gram, axis=0).reshape(TERMS, TERMS) / (CELLS * CELLS)
+    gram = jnp.sum(gram, axis=0).reshape(TERMS, TERMS)
     return library.reshape(1, 1, tiles, TERMS, SIDE * SIDE), gram
 
 

time: 45.5 us -> 45.5 us (level)
    div x1 -> x0, local copies, waits for them, and re-layouts: 0.68 us -> none  [per_device(): gram = jnp.sum(gram, axis=0).reshape(TERMS, TERMS) / (CELLS * CELLS)]
    reshape x0 -> x1, local copies, waits for them, and re-layouts: none -> 0.68 us  [per_device(): gram = jnp.sum(gram, axis=0).reshape(TERMS, TERMS)]
where the time goes in v11:
time: 45.5 us; the launch traced here: 45.3 us
  starting transfers between devices  16.1 us (35%)
  Pallas kernels  10.5 us (23%)
  blocking collectives  10.1 us (22%)
  waiting for transfers between devices  6.4 us (14%)
  local copies, waits for them, and re-layouts  1.31 us (3%)
  between operations  0.77 us (2%)
    all_to_all x1, blocking collectives, per_device(): lax.all_to_all(blocks, 'tile', split_axis=0, concat_axis=0, tiled=True)  10.1 us
    all_to_all x1, waiting for transfers between devices, per_device(): lax.all_to_all(jnp.broadcast_to(gram, (columns, 2, LANES)), 'col', split_...  6.39 us
    all_to_all x1, starting transfers between devices, per_device(): lax.all_to_all(jnp.broadcast_to(gram, (columns, 2, LANES)), 'col', split_...  5.67 us
    ppermute x1, starting transfers between devices, per_device(): from_left = lax.ppermute(to_right, 'col', onward(columns))  4.03 us
    ppermute x1, starting transfers between devices, per_device(): below = lax.ppermute(up, 'tile', back(tiles))  3.84 us
    pallas_call x1, Pallas kernels, per_device(): pl.pallas_call(prepare_kernel, out_shape=[jax.ShapeDtypeStruct((rows, 2 *...  3.31 us
    pallas_call x1, Pallas kernels, per_device(): pl.pallas_call(main_kernel, out_shape=[struct(2, FULL, LANES), struct(CEL...  3.14 us
    ppermute x1, starting transfers between devices, per_device(): from_right = lax.ppermute(to_left, 'col', back(columns))  2.53 us
  transfers between devices with their start and end apart: 5, of which 1 were waited for; matrix products, arithmetic and copies ran while one was open for 0% of the time, Pallas kernels for 17%

profile of v11, /device:TPU:0, one launch (start us, length us, event | category | flops | bytes accessed | tf_op | source)
XLA Modules:
  0.0 45.3 jit_solution(14400997879834260863)
XLA Ops:
  0.6 0.0 copy-start.1
  0.6 0.0 copy-start
  0.7 1.0 %send_rows.1 = (f32[24,512]{1,0:T(8,128)S(1)}, f32[24,512]{1,0:T(8,128)S(1)}) custom-call(s32[1]{0:T(128)} %bitcast.here_ref, s32[16]{0:T(128)} %turns_hbm.1, f32[512,512]{1,0:T(8,128)} %refs_3_, f32[512,512]{1,0:T(8,128)} %refs_7_), custom_call_target="tpu_custom_call" | custom-call | tf_op jit(solution)/shard_map/send_rows/pallas_call | solution.py:419
  1.7 0.0 copy-start.3
  1.7 0.1 collective-permute-start
  1.8 3.8 %collective-permute-start.1 = (f32[24,512]{1,0:T(8,128)S(1)}, f32[24,512]{1,0:T(8,128)S(1)}, u32[]{:S(2)}, u32[]{:S(2)}) collective-permute-start(f32[24,512]{1,0:T(8,128)S(1)} %get-tuple-element.26), channel_id=1, source_target_pairs={{8,0},{16,8},{24,16},{32,24},{40,32},{48,40},{56,48},{64,56},{72,6... | collective-permute-start | bytes 147464 | tf_op jit(solution)/shard_map/ppermute | solution.py:431
  5.6 0.0 copy-done.1
  5.6 0.0 copy-done
  5.6 3.3 %prepare_rows.1 = (bf16[1024,1024]{1,0:T(8,128)(2,1)S(1)}, bf16[512,1280]{1,0:T(8,128)(2,1)S(1)}, f32[144,128]{1,0:T(8,128)S(1)}, f32[1024,768]{1,0:T(8,128)S(1)}) custom-call(f32[512,512]{1,0:T(8,128)S(1)} %copy-done, f32[512,512]{1,0:T(8,128)S(1)} %copy-done, f32[512,512]{1,0:T(8,128)S(1)} %copy-done, f32[512,512]{1,0:T(8,128)S(1)} %copy-done, ...), custom_call_target="tpu_custom_call" | custom-call | tf_op jit(solution)/shard_map/prepare_rows/pallas_call | solution.py:434
  8.9 0.0 collective-permute-done.above_ref
  9.0 0.0 collective-permute-done.1.below_ref
  9.0 0.4 rim_columns.1
  9.4 4.0 %collective-permute-start.2 = (f32[8,144]{1,0:T(8,128)S(1)}, f32[8,144]{1,0:T(8,128)S(1)}, u32[]{:S(2)}, u32[]{:S(2)}) collective-permute-start(f32[8,144]{1,0:T(8,128)S(1)} %get-tuple-element.32), channel_id=1, source_target_pairs={{0,1},{1,2},{2,3},{3,4},{4,5},{5,6},{6,7},{7,0},{8,9},{9,10},{10,1... | collective-permute-start | bytes 13832 | tf_op jit(solution)/shard_map/ppermute | solution.py:458
  13.4 2.5 %collective-permute-start.3 = (f32[8,144]{1,0:T(8,128)S(1)}, f32[8,144]{1,0:T(8,128)S(1)}, u32[]{:S(2)}, u32[]{:S(2)}) collective-permute-start(f32[8,144]{1,0:T(8,128)S(1)} %get-tuple-element.33), channel_id=1, source_target_pairs={{1,0},{2,1},{3,2},{4,3},{5,4},{6,5},{7,6},{0,7},{9,8},{10,9},{11,1... | collective-permute-start | bytes 13832 | tf_op jit(solution)/shard_map/ppermute | solution.py:457
  16.0 0.0 copy-done.3
  16.0 0.0 copy-start.2
  16.0 0.0 copy-start.4
  16.0 3.1 %main_columns.1 = (f32[2,144,128]{2,1,0:T(8,128)S(1)}, f32[128,128]{1,0:T(8,128)S(1)}, f32[136,8,128]{2,1,0:T(8,128)S(1)}) custom-call(s32[4,4]{1,0:T(4,128)S(1)} %copy-done.3, bf16[1024,1024]{1,0:T(8,128)(2,1)S(1)} %get-tuple-element.22.parts_ref, f32[1024,768]{1,0:T(8,128)S(1)} %get-tuple-element.23.early_ref, ...), custom_call_target="tpu_custom_call" | custom-call | tf_op jit(solution)/shard_map/main_columns/pallas_call | solution.py:459
  19.1 0.0 collective-permute-done.2.from_left_ref
  19.1 0.0 collective-permute-done.3.from_right_ref
  19.1 0.0 copy-done.2
  19.2 0.0 copy-done.4
  19.2 1.3 %base_fields.1 = f32[16,24,128]{2,1,0:T(8,128)S(1)} custom-call(s32[4,4]{1,0:T(4,128)S(1)} %copy-done.3, s32[4,4]{1,0:T(4,128)S(1)} %copy-done.4, f32[2,144,128]{2,1,0:T(8,128)S(1)} %get-tuple-element.29.main_ref, f32[128,128]{1,0:T(8,128)S(1)} %get-tuple-element.30.live_ref, f32[136,8,128]{2,1,0:T(8,128)S(1)} %get-tuple-element.31.inner_ref, ...), custom_call_target="tpu_custom_call" | custom-call | tf_op jit(solution)/shard_map/base_fields/pallas_call | solution.py:469
  20.5 10.1 %all_to_all.10 = f32[16,24,128]{2,1,0:T(8,128)S(1)} all-to-all(f32[16,24,128]{2,1,0:T(8,128)S(1)} %base_fields.1), channel_id=1, replica_groups=mesh['tile'=16,'col'=8] {'tile'}, dimensions={0} | all-to-all | bytes 393216 | tf_op jit(solution)/shard_map/all_to_all | solution.py:481
  30.6 0.6 %broadcast_in_dim.7 = f32[8,2,128]{2,1,0:T(2,128)} broadcast(f32[2,128]{1,0:T(2,128)S(1)} %slice_reduce_fusion), dimensions={1,2} | broadcast | bytes 9216 | tf_op jit(solution)/shard_map/broadcast_in_dim | solution.py:483
  31.2 5.7 %all-to-all-start.1 = ((f32[8,2,128]{2,1,0:T(2,128)}), f32[8,2,128]{2,1,0:T(2,128)S(1)}, u32[]{:S(2)}, u32[]{:S(2)}) async-start(f32[8,2,128]{2,1,0:T(2,128)} %broadcast_in_dim.7), calls=%async_computation.1 | async-start | bytes 16384 | tf_op jit(solution)/shard_map/all_to_all | solution.py:483
  36.9 1.3 %library_terms.1 = f32[256,1024]{1,0:T(8,128)} custom-call(f32[384,128]{1,0:T(8,128)S(1)} %bitcast.3), custom_call_target="tpu_custom_call" | custom-call | flops 524288 | bytes 1310720 | tf_op jit(solution)/shard_map/library_terms/pallas_call | solution.py:484
  38.2 6.4 %all-to-all-done.1 = f32[8,2,128]{2,1,0:T(2,128)S(1)} async-done(((f32[8,2,128]{2,1,0:T(2,128)}), f32[8,2,128]{2,1,0:T(2,128)S(1)}, u32[]{:S(2)}, u32[]{:S(2)}) %all-to-all-start.1) | async-done | bytes 8224 | tf_op jit(solution)/shard_map/all_to_all | solution.py:483
  44.6 0.7 %reshape.15 = f32[16,16]{1,0:T(8,128)} reshape(f32[2,128]{1,0:T(2,128)S(1)} %reduce_sum.19) | data formatting | bytes 2048 | tf_op jit(solution)/shard_map/reshape | solution.py:495
  (2 shorter events, 0.0 us)
Async XLA Ops:
  0.6 5.0 %copy-start.1 = (f32[512,512]{1,0:T(8,128)S(1)}, f32[512,512]{1,0:T(8,128)}, u32[]{:S(2)}) copy-start(f32[512,512]{1,0:T(8,128)} %refs_7_) | copy-start | bytes 3145732
  0.6 5.0 %copy-start = (f32[512,512]{1,0:T(8,128)S(1)}, f32[512,512]{1,0:T(8,128)}, u32[]{:S(2)}) copy-start(f32[512,512]{1,0:T(8,128)} %refs_3_) | copy-start | bytes 3145732
  1.7 14.3 %copy-start.3 = (s32[4,4]{1,0:T(4,128)S(1)}, s32[4,4]{1,0:T(4,128)}, u32[]{:S(2)}) copy-start(s32[4,4]{1,0:T(4,128)} %mask_vmem.1) | copy-start | bytes 196
  1.7 7.3 %collective-permute-start = (f32[24,512]{1,0:T(8,128)S(1)}, f32[24,512]{1,0:T(8,128)S(1)}, u32[]{:S(2)}, u32[]{:S(2)}) collective-permute-start(f32[24,512]{1,0:T(8,128)S(1)} %get-tuple-element.25), channel_id=1, source_target_pairs={{0,8},{8,16},{16,24},{24,32},{32,40},{40,48},{48,56},{56,64},{64,7... | collective-permute-start | bytes 147464 | tf_op jit(solution)/shard_map/ppermute | solution.py:430
  1.8 7.2 %collective-permute-start.1 = (f32[24,512]{1,0:T(8,128)S(1)}, f32[24,512]{1,0:T(8,128)S(1)}, u32[]{:S(2)}, u32[]{:S(2)}) collective-permute-start(f32[24,512]{1,0:T(8,128)S(1)} %get-tuple-element.26), channel_id=1, source_target_pairs={{8,0},{16,8},{24,16},{32,24},{40,32},{48,40},{56,48},{64,56},{72,6... | collective-permute-start | bytes 147464 | tf_op jit(solution)/shard_map/ppermute | solution.py:431
  9.4 9.7 %collective-permute-start.2 = (f32[8,144]{1,0:T(8,128)S(1)}, f32[8,144]{1,0:T(8,128)S(1)}, u32[]{:S(2)}, u32[]{:S(2)}) collective-permute-start(f32[8,144]{1,0:T(8,128)S(1)} %get-tuple-element.32), channel_id=1, source_target_pairs={{0,1},{1,2},{2,3},{3,4},{4,5},{5,6},{6,7},{7,0},{8,9},{9,10},{10,1... | collective-permute-start | bytes 13832 | tf_op jit(solution)/shard_map/ppermute | solution.py:458
  13.4 5.7 %collective-permute-start.3 = (f32[8,144]{1,0:T(8,128)S(1)}, f32[8,144]{1,0:T(8,128)S(1)}, u32[]{:S(2)}, u32[]{:S(2)}) collective-permute-start(f32[8,144]{1,0:T(8,128)S(1)} %get-tuple-element.33), channel_id=1, source_target_pairs={{1,0},{2,1},{3,2},{4,3},{5,4},{6,5},{7,6},{0,7},{9,8},{10,9},{11,1... | collective-permute-start | bytes 13832 | tf_op jit(solution)/shard_map/ppermute | solution.py:457
  16.0 3.2 %copy-start.2 = (bf16[96,512]{1,0:T(8,128)(2,1)S(1)}, bf16[96,512]{1,0:T(8,128)(2,1)}, u32[]{:S(2)}) copy-start(bf16[96,512]{1,0:T(8,128)(2,1)} %constant.13.clone.place_ref) | copy-start | bytes 294916
  16.0 3.2 %copy-start.4 = (s32[4,4]{1,0:T(4,128)S(1)}, s32[4,4]{1,0:T(4,128)}, u32[]{:S(2)}) copy-start(s32[4,4]{1,0:T(4,128)} %owner_vmem.1) | copy-start | bytes 196
  31.2 13.4 %all-to-all-start.1 = ((f32[8,2,128]{2,1,0:T(2,128)}), f32[8,2,128]{2,1,0:T(2,128)S(1)}, u32[]{:S(2)}, u32[]{:S(2)}) async-start(f32[8,2,128]{2,1,0:T(2,128)} %broadcast_in_dim.7), calls=%async_computation.1 | async-start | bytes 16384 | tf_op jit(solution)/shard_map/all_to_all | solution.py:483

commit v12 on v9

--- a/solution.py
+++ b/solution.py
@@ -315,7 +315,7 @@
         gram_ref[n * TERMS + m : n * TERMS + m + 1] = total
         if m > n:
             gram_ref[m * TERMS + n : m * TERMS + n + 1] = total
-    totals = jnp.sum(gram_ref[...], axis=1, keepdims=True)
+    totals = jnp.sum(gram_ref[...], axis=1, keepdims=True) * (1.0 / (CELLS * CELLS))
     row = lax.broadcasted_iota(jnp.int32, (TERMS * TERMS, 1), 0)
     spread = jnp.where(row % LANES == lane, totals, 0.0)
     halves = [jnp.sum(spread[h * LANES : (h + 1) * LANES], axis=0, keepdims=True) for h in range(2)]
@@ -493,7 +493,7 @@
                                       bytes_accessed=5 * tiles * TERMS * SIDE * SIDE),
         name="library_terms",
     )(blocks.reshape(tiles * BLOCK_ROWS, LANES))
-    gram = jnp.sum(gram, axis=0).reshape(TERMS, TERMS) / (CELLS * CELLS)
+    gram = jnp.sum(gram, axis=0).reshape(TERMS, TERMS)
     return library.reshape(1, 1, tiles, TERMS, SIDE * SIDE), gram
 
 

time: 45.5 us -> 45.5 us (level)
    div x1 -> x0, local copies, waits for them, and re-layouts: 0.68 us -> none  [per_device(): gram = jnp.sum(gram, axis=0).reshape(TERMS, TERMS) / (CELLS * CELLS)]
    reshape x0 -> x1, local copies, waits for them, and re-layouts: none -> 0.68 us  [per_device(): gram = jnp.sum(gram, axis=0).reshape(TERMS, TERMS)]
where the time goes in v12:
time: 45.5 us; the launch traced here: 45.3 us
  starting transfers between devices  16.2 us (36%)
  Pallas kernels  10.4 us (23%)
  blocking collectives  10.1 us (22%)
  waiting for transfers between devices  6.4 us (14%)
  local copies, waits for them, and re-layouts  1.31 us (3%)
  between operations  0.77 us (2%)
    all_to_all x1, blocking collectives, per_device(): lax.all_to_all(blocks, 'tile', split_axis=0, concat_axis=0, tiled=True)  10.1 us
    all_to_all x1, waiting for transfers between devices, per_device(): lax.all_to_all(jnp.broadcast_to(gram, (columns, 2, LANES)), 'col', split_...  6.39 us
    all_to_all x1, starting transfers between devices, per_device(): lax.all_to_all(jnp.broadcast_to(gram, (columns, 2, LANES)), 'col', split_...  5.74 us
    ppermute x1, starting transfers between devices, per_device(): from_left = lax.ppermute(to_right, 'col', onward(columns))  4.03 us
    ppermute x1, starting transfers between devices, per_device(): below = lax.ppermute(up, 'tile', back(tiles))  3.84 us
    pallas_call x1, Pallas kernels, per_device(): pl.pallas_call(prepare_kernel, out_shape=[jax.ShapeDtypeStruct((rows, 2 *...  3.31 us
    pallas_call x1, Pallas kernels, per_device(): pl.pallas_call(main_kernel, out_shape=[struct(2, FULL, LANES), struct(CEL...  3.08 us
    ppermute x1, starting transfers between devices, per_device(): from_right = lax.ppermute(to_left, 'col', back(columns))  2.53 us
  transfers between devices with their start and end apart: 5, of which 1 were waited for; matrix products, arithmetic and copies ran while one was open for 0% of the time, Pallas kernels for 17%

profile of v12, /device:TPU:0, one launch (start us, length us, event | category | flops | bytes accessed | tf_op | source)
XLA Modules:
  0.0 45.3 jit_solution(457328848403706230)
XLA Ops:
  0.6 0.0 copy-start.1
  0.6 0.0 copy-start
  0.7 1.0 %send_rows.1 = (f32[24,512]{1,0:T(8,128)S(1)}, f32[24,512]{1,0:T(8,128)S(1)}) custom-call(s32[1]{0:T(128)} %bitcast.here_ref, s32[16]{0:T(128)} %turns_hbm.1, f32[512,512]{1,0:T(8,128)} %refs_3_, f32[512,512]{1,0:T(8,128)} %refs_7_), custom_call_target="tpu_custom_call" | custom-call | tf_op jit(solution)/shard_map/send_rows/pallas_call | solution.py:420
  1.7 0.0 copy-start.3
  1.7 0.1 collective-permute-start
  1.8 3.8 %collective-permute-start.1 = (f32[24,512]{1,0:T(8,128)S(1)}, f32[24,512]{1,0:T(8,128)S(1)}, u32[]{:S(2)}, u32[]{:S(2)}) collective-permute-start(f32[24,512]{1,0:T(8,128)S(1)} %get-tuple-element.26), channel_id=1, source_target_pairs={{8,0},{16,8},{24,16},{32,24},{40,32},{48,40},{56,48},{64,56},{72,6... | collective-permute-start | bytes 147464 | tf_op jit(solution)/shard_map/ppermute | solution.py:432
  5.6 0.0 copy-done.1
  5.6 0.0 copy-done
  5.6 3.3 %prepare_rows.1 = (bf16[1024,1024]{1,0:T(8,128)(2,1)S(1)}, bf16[512,1280]{1,0:T(8,128)(2,1)S(1)}, f32[144,128]{1,0:T(8,128)S(1)}, f32[1024,768]{1,0:T(8,128)S(1)}) custom-call(f32[512,512]{1,0:T(8,128)S(1)} %copy-done, f32[512,512]{1,0:T(8,128)S(1)} %copy-done, f32[512,512]{1,0:T(8,128)S(1)} %copy-done, f32[512,512]{1,0:T(8,128)S(1)} %copy-done, ...), custom_call_target="tpu_custom_call" | custom-call | tf_op jit(solution)/shard_map/prepare_rows/pallas_call | solution.py:435
  8.9 0.0 collective-permute-done.above_ref
  9.0 0.0 collective-permute-done.1.below_ref
  9.0 0.4 rim_columns.1
  9.4 4.0 %collective-permute-start.2 = (f32[8,144]{1,0:T(8,128)S(1)}, f32[8,144]{1,0:T(8,128)S(1)}, u32[]{:S(2)}, u32[]{:S(2)}) collective-permute-start(f32[8,144]{1,0:T(8,128)S(1)} %get-tuple-element.32), channel_id=1, source_target_pairs={{0,1},{1,2},{2,3},{3,4},{4,5},{5,6},{6,7},{7,0},{8,9},{9,10},{10,1... | collective-permute-start | bytes 13832 | tf_op jit(solution)/shard_map/ppermute | solution.py:459
  13.4 2.5 %collective-permute-start.3 = (f32[8,144]{1,0:T(8,128)S(1)}, f32[8,144]{1,0:T(8,128)S(1)}, u32[]{:S(2)}, u32[]{:S(2)}) collective-permute-start(f32[8,144]{1,0:T(8,128)S(1)} %get-tuple-element.33), channel_id=1, source_target_pairs={{1,0},{2,1},{3,2},{4,3},{5,4},{6,5},{7,6},{0,7},{9,8},{10,9},{11,1... | collective-permute-start | bytes 13832 | tf_op jit(solution)/shard_map/ppermute | solution.py:458
  16.0 0.0 copy-done.3
  16.0 0.0 copy-start.2
  16.0 0.0 copy-start.4
  16.0 3.1 %main_columns.1 = (f32[2,144,128]{2,1,0:T(8,128)S(1)}, f32[128,128]{1,0:T(8,128)S(1)}, f32[136,8,128]{2,1,0:T(8,128)S(1)}) custom-call(s32[4,4]{1,0:T(4,128)S(1)} %copy-done.3, bf16[1024,1024]{1,0:T(8,128)(2,1)S(1)} %get-tuple-element.22.parts_ref, f32[1024,768]{1,0:T(8,128)S(1)} %get-tuple-element.23.early_ref, ...), custom_call_target="tpu_custom_call" | custom-call | tf_op jit(solution)/shard_map/main_columns/pallas_call | solution.py:460
  19.1 0.0 collective-permute-done.2.from_left_ref
  19.1 0.0 collective-permute-done.3.from_right_ref
  19.1 0.0 copy-done.2
  19.1 0.0 copy-done.4
  19.1 1.3 %base_fields.1 = f32[16,24,128]{2,1,0:T(8,128)S(1)} custom-call(s32[4,4]{1,0:T(4,128)S(1)} %copy-done.3, s32[4,4]{1,0:T(4,128)S(1)} %copy-done.4, f32[2,144,128]{2,1,0:T(8,128)S(1)} %get-tuple-element.29.main_ref, f32[128,128]{1,0:T(8,128)S(1)} %get-tuple-element.30.live_ref, f32[136,8,128]{2,1,0:T(8,128)S(1)} %get-tuple-element.31.inner_ref, ...), custom_call_target="tpu_custom_call" | custom-call | tf_op jit(solution)/shard_map/base_fields/pallas_call | solution.py:470
  20.4 10.1 %all_to_all.10 = f32[16,24,128]{2,1,0:T(8,128)S(1)} all-to-all(f32[16,24,128]{2,1,0:T(8,128)S(1)} %base_fields.1), channel_id=1, replica_groups=mesh['tile'=16,'col'=8] {'tile'}, dimensions={0} | all-to-all | bytes 393216 | tf_op jit(solution)/shard_map/all_to_all | solution.py:482
  30.5 0.6 %broadcast_in_dim.7 = f32[8,2,128]{2,1,0:T(2,128)} broadcast(f32[2,128]{1,0:T(2,128)S(1)} %slice_reduce_fusion), dimensions={1,2} | broadcast | bytes 9216 | tf_op jit(solution)/shard_map/broadcast_in_dim | solution.py:484
  31.1 5.7 %all-to-all-start.1 = ((f32[8,2,128]{2,1,0:T(2,128)}), f32[8,2,128]{2,1,0:T(2,128)S(1)}, u32[]{:S(2)}, u32[]{:S(2)}) async-start(f32[8,2,128]{2,1,0:T(2,128)} %broadcast_in_dim.7), calls=%async_computation.1 | async-start | bytes 16384 | tf_op jit(solution)/shard_map/all_to_all | solution.py:484
  36.9 1.3 %library_terms.1 = f32[256,1024]{1,0:T(8,128)} custom-call(f32[384,128]{1,0:T(8,128)S(1)} %bitcast.3), custom_call_target="tpu_custom_call" | custom-call | flops 524288 | bytes 1310720 | tf_op jit(solution)/shard_map/library_terms/pallas_call | solution.py:485
  38.2 6.4 %all-to-all-done.1 = f32[8,2,128]{2,1,0:T(2,128)S(1)} async-done(((f32[8,2,128]{2,1,0:T(2,128)}), f32[8,2,128]{2,1,0:T(2,128)S(1)}, u32[]{:S(2)}, u32[]{:S(2)}) %all-to-all-start.1) | async-done | bytes 8224 | tf_op jit(solution)/shard_map/all_to_all | solution.py:484
  44.6 0.7 %reshape.15 = f32[16,16]{1,0:T(8,128)} reshape(f32[2,128]{1,0:T(2,128)S(1)} %reduce_sum.19) | data formatting | bytes 2048 | tf_op jit(solution)/shard_map/reshape | solution.py:496
  (2 shorter events, 0.0 us)
Async XLA Ops:
  0.6 5.0 %copy-start.1 = (f32[512,512]{1,0:T(8,128)S(1)}, f32[512,512]{1,0:T(8,128)}, u32[]{:S(2)}) copy-start(f32[512,512]{1,0:T(8,128)} %refs_7_) | copy-start | bytes 3145732
  0.6 5.0 %copy-start = (f32[512,512]{1,0:T(8,128)S(1)}, f32[512,512]{1,0:T(8,128)}, u32[]{:S(2)}) copy-start(f32[512,512]{1,0:T(8,128)} %refs_3_) | copy-start | bytes 3145732
  1.7 14.3 %copy-start.3 = (s32[4,4]{1,0:T(4,128)S(1)}, s32[4,4]{1,0:T(4,128)}, u32[]{:S(2)}) copy-start(s32[4,4]{1,0:T(4,128)} %mask_vmem.1) | copy-start | bytes 196
  1.7 7.3 %collective-permute-start = (f32[24,512]{1,0:T(8,128)S(1)}, f32[24,512]{1,0:T(8,128)S(1)}, u32[]{:S(2)}, u32[]{:S(2)}) collective-permute-start(f32[24,512]{1,0:T(8,128)S(1)} %get-tuple-element.25), channel_id=1, source_target_pairs={{0,8},{8,16},{16,24},{24,32},{32,40},{40,48},{48,56},{56,64},{64,7... | collective-permute-start | bytes 147464 | tf_op jit(solution)/shard_map/ppermute | solution.py:431
  1.8 7.2 %collective-permute-start.1 = (f32[24,512]{1,0:T(8,128)S(1)}, f32[24,512]{1,0:T(8,128)S(1)}, u32[]{:S(2)}, u32[]{:S(2)}) collective-permute-start(f32[24,512]{1,0:T(8,128)S(1)} %get-tuple-element.26), channel_id=1, source_target_pairs={{8,0},{16,8},{24,16},{32,24},{40,32},{48,40},{56,48},{64,56},{72,6... | collective-permute-start | bytes 147464 | tf_op jit(solution)/shard_map/ppermute | solution.py:432
  9.4 9.7 %collective-permute-start.2 = (f32[8,144]{1,0:T(8,128)S(1)}, f32[8,144]{1,0:T(8,128)S(1)}, u32[]{:S(2)}, u32[]{:S(2)}) collective-permute-start(f32[8,144]{1,0:T(8,128)S(1)} %get-tuple-element.32), channel_id=1, source_target_pairs={{0,1},{1,2},{2,3},{3,4},{4,5},{5,6},{6,7},{7,0},{8,9},{9,10},{10,1... | collective-permute-start | bytes 13832 | tf_op jit(solution)/shard_map/ppermute | solution.py:459
  13.4 5.6 %collective-permute-start.3 = (f32[8,144]{1,0:T(8,128)S(1)}, f32[8,144]{1,0:T(8,128)S(1)}, u32[]{:S(2)}, u32[]{:S(2)}) collective-permute-start(f32[8,144]{1,0:T(8,128)S(1)} %get-tuple-element.33), channel_id=1, source_target_pairs={{1,0},{2,1},{3,2},{4,3},{5,4},{6,5},{7,6},{0,7},{9,8},{10,9},{11,1... | collective-permute-start | bytes 13832 | tf_op jit(solution)/shard_map/ppermute | solution.py:458
  16.0 3.1 %copy-start.2 = (bf16[96,512]{1,0:T(8,128)(2,1)S(1)}, bf16[96,512]{1,0:T(8,128)(2,1)}, u32[]{:S(2)}) copy-start(bf16[96,512]{1,0:T(8,128)(2,1)} %constant.13.clone.place_ref) | copy-start | bytes 294916
  16.0 3.1 %copy-start.4 = (s32[4,4]{1,0:T(4,128)S(1)}, s32[4,4]{1,0:T(4,128)}, u32[]{:S(2)}) copy-start(s32[4,4]{1,0:T(4,128)} %owner_vmem.1) | copy-start | bytes 196
  31.1 13.4 %all-to-all-start.1 = ((f32[8,2,128]{2,1,0:T(2,128)}), f32[8,2,128]{2,1,0:T(2,128)S(1)}, u32[]{:S(2)}, u32[]{:S(2)}) async-start(f32[8,2,128]{2,1,0:T(2,128)} %broadcast_in_dim.7), calls=%async_computation.1 | async-start | bytes 16384 | tf_op jit(solution)/shard_map/all_to_all | solution.py:484
